TPU v7x, 32 devices: a whole 2x2x4 slice. The times are simulated.
32 devices in a mesh: group: 2 (over core), wide: 16 (over z, y, x).
Axes of the slice: x: 2, y: 2, z: 4, core: 2. Of those that a mesh axis runs over, the one named last changes fastest.
Arguments:
- passage_ids: int32 [32, 512], P(('group', 'wide')), may hold values from 0 to 50431
- query_ids: int32 [128, 32], P(('group', 'wide')), may hold values from 0 to 50431
- passage_len: int32 [32], P(('group', 'wide')), may hold values from 128 to 512, as said below
- query_len: int32 [128], P(('group', 'wide')), may hold values from 8 to 32, as said below
- positive: int32 [128], P(('group', 'wide')), may hold values from 0 to 31
- negatives: int32 [128, 7], P(('group', 'wide')), may hold values from 0 to 31
- valid: int32 [128], P(('group', 'wide')), may hold values from 0 to 1, as said below
- step_count: int32 [1], replicated, may hold values from 1 to 20
- embedding: float32 [768, 50432], P('wide', 'group'), may hold values from -6 to 6
- embedding_m: float32 [768, 50432], P('wide', 'group'), may hold values from -1.7881393e-07 to 1.7881393e-07
- embedding_v: float32 [768, 50432], P('wide', 'group'), may hold values from 6.2269707e-17 to 2.4907883e-16
- attn_in: float32 [768, 2304], P(('group', 'wide')), may hold values from -0.21875 to 0.21875
- attn_in_m: float32 [768, 2304], P(('group', 'wide')), may hold values from -1.9073486e-06 to 1.9073486e-06
- attn_in_v: float32 [768, 2304], P(('group', 'wide')), may hold values from 8.618645e-15 to 3.447458e-14
- attn_out: float32 [768, 768], P(('group', 'wide')), may hold values from -0.875 to 0.875
- attn_out_m: float32 [768, 768], P(('group', 'wide')), may hold values from -1.9073486e-06 to 1.9073486e-06
- attn_out_v: float32 [768, 768], P(('group', 'wide')), may hold values from 8.618645e-15 to 3.447458e-14
- ffn_up: float32 [768, 3072], P(('group', 'wide')), may hold values from -0.21875 to 0.21875
- ffn_up_m: float32 [768, 3072], P(('group', 'wide')), may hold values from -1.9073486e-06 to 1.9073486e-06
- ffn_up_v: float32 [768, 3072], P(('group', 'wide')), may hold values from 8.618645e-15 to 3.447458e-14
- ffn_down: float32 [3072, 768], P(('group', 'wide')), may hold values from -0.109375 to 0.109375
- ffn_down_m: float32 [3072, 768], P(('group', 'wide')), may hold values from -1.9073486e-06 to 1.9073486e-06
- ffn_down_v: float32 [3072, 768], P(('group', 'wide')), may hold values from 8.618645e-15 to 3.447458e-14
- head: float32 [768, 768], P(('group', 'wide')), may hold values from -0.21875 to 0.21875
- head_m: float32 [768, 768], P(('group', 'wide')), may hold values from -1.9073486e-06 to 1.9073486e-06
- head_v: float32 [768, 768], P(('group', 'wide')), may hold values from 8.618645e-15 to 3.447458e-14
- vectors: float32 [11520], P(('group', 'wide')), may hold values from -0.5 to 1.5, as said below
- vectors_m: float32 [11520], P(('group', 'wide')), may hold values from -7.6293945e-06 to 7.6293945e-06
- vectors_v: float32 [11520], P(('group', 'wide')), may hold values from 1.3789832e-13 to 5.515933e-13
Outputs:
- loss: float32 [], replicated
- grad_norm: float32 [], replicated
- new_embedding: float32 [768, 50432], P('wide', 'group')
- new_embedding_m: float32 [768, 50432], P('wide', 'group')
- new_embedding_v: float32 [768, 50432], P('wide', 'group')
- new_attn_in: float32 [768, 2304], P(('group', 'wide'))
- new_attn_in_m: float32 [768, 2304], P(('group', 'wide'))
- new_attn_in_v: float32 [768, 2304], P(('group', 'wide'))
- new_attn_out: float32 [768, 768], P(('group', 'wide'))
- new_attn_out_m: float32 [768, 768], P(('group', 'wide'))
- new_attn_out_v: float32 [768, 768], P(('group', 'wide'))
- new_ffn_up: float32 [768, 3072], P(('group', 'wide'))
- new_ffn_up_m: float32 [768, 3072], P(('group', 'wide'))
- new_ffn_up_v: float32 [768, 3072], P(('group', 'wide'))
- new_ffn_down: float32 [3072, 768], P(('group', 'wide'))
- new_ffn_down_m: float32 [3072, 768], P(('group', 'wide'))
- new_ffn_down_v: float32 [3072, 768], P(('group', 'wide'))
- new_head: float32 [768, 768], P(('group', 'wide'))
- new_head_m: float32 [768, 768], P(('group', 'wide'))
- new_head_v: float32 [768, 768], P(('group', 'wide'))
- new_vectors: float32 [11520], P(('group', 'wide'))
- new_vectors_m: float32 [11520], P(('group', 'wide'))
- new_vectors_v: float32 [11520], P(('group', 'wide'))
Inputs may be any that keep to these rules, and one draw needn't show every extreme that they name: `passage_len`: the first passage has all 512 slots live. `query_len`: the first query has all 32 slots live. At least one query of every aligned block of 4 queries is valid. `vectors`: gains lie near one, biases near zero.
All inputs are finite; a program needn't handle non-finite values.
Results may differ from a plain program's by a relative error of at most 0.02.
Values may be sent and summed in bfloat16 or wider, within the bound.
No kernel may reach another device: no remote copies, remote signals or barrier semaphores. Data moves between devices by JAX's collectives and lax.ppermute only.
A program may use at most 256 MiB of HBM per device.

v0:
```python
from functools import partial

import jax
import jax.numpy as jnp
import numpy as np
from jax import lax
from jax.experimental import pallas as pl
from jax.experimental.pallas import tpu as pltpu
from jax.sharding import PartitionSpec as P

D = 768
HEADS = 12
HEAD_DIM = 64
FF = 3072
ROWS = 8
LANES = 128
SIDE = 64
Z_AT = 68
KEEP = 24
ALL = ("group", "wide")
clip_level = 0.02
f32 = jnp.float32
bf16 = jnp.bfloat16
RATES = (0.5, 0.5 * D**-0.5, 0.5 * (D // 16) ** -0.5, 0.5 * D**-0.5, 0.5 * FF**-0.5, 0.5 * D**-0.5, 0.2)


def dot(a, b, ca=1, cb=0):
    return lax.dot_general(a, b, (((ca,), (cb,)), ((), ())), preferred_element_type=f32)


def split(x):
    high = x.astype(bf16)
    return high, (x - high.astype(f32)).astype(bf16)


def dot_split(x, w, cb=0):
    high, rest = split(x)
    return dot(high, w, 1, cb) + dot(rest, w, 1, cb)


def iota(shape, dim):
    return lax.broadcasted_iota(jnp.int32, shape, dim)


def stack_rows(rows):
    index = iota((ROWS, rows[0].shape[1]), 0)
    total = jnp.zeros(index.shape, f32)
    for number, row in enumerate(rows):
        total = jnp.where(index == number, row, total)
    return total


def layer_norm(resid):
    centred = resid - jnp.mean(resid, -1, keepdims=True)
    inv_std = lax.rsqrt(jnp.mean(centred * centred, -1, keepdims=True) + 1e-05)
    return centred * inv_std, inv_std


def norm_back(grad_out, normed, inv_std, gain):
    scaled = grad_out * gain
    return inv_std * (
        scaled
        - jnp.mean(scaled, -1, keepdims=True)
        - normed * jnp.mean(scaled * normed, -1, keepdims=True)
    )


def flag(condition):
    return jnp.where(condition, 1.0, 0.0)


def sequence_of(a, rows):
    assert HEADS == 12
    return jnp.where((a >= 0) & (a < rows * HEADS), lax.shift_right_logical(a * 43, 9), 99)


def head_of(a, rows):
    return a - HEADS * sequence_of(a, rows)


def spread_table(rows):
    return flag(sequence_of(iota((SIDE, ROWS), 0), rows) == iota((SIDE, ROWS), 1)).astype(bf16)


def column_table(rows):
    return flag(head_of(iota((SIDE, D), 0), rows) == lax.shift_right_logical(iota((SIDE, D), 1), 6))


def heads_table(rows):
    return flag(head_of(iota((16, SIDE), 1), rows) == iota((16, SIDE), 0)).astype(bf16)


def place_table(rows, first, count=None):
    count = rows * HEADS if count is None else count
    size = SIDE if count > ROWS else ROWS
    a = iota((LANES, size), 1)
    return flag((iota((LANES, size), 0) == first + a) & (a < count)).astype(bf16)


def expand_table(rows, first, r):
    return flag(iota((LANES, D), 0) == first + r * HEADS + lax.shift_right_logical(iota((LANES, D), 1), 6)).astype(bf16)


def prepare(ids, lens, seq, pos, group_rows):
    count = ids.shape[1]
    live = flag(pos < lens)
    first = jnp.where(ids < group_rows, 1.0, 0.0)
    high = lax.shift_right_logical(ids, 8)
    index = iota((ROWS, count), 0)
    values = jnp.zeros((ROWS, count), f32)
    pieces = (high.astype(f32), (ids - high * 256).astype(f32), seq.astype(f32), jnp.where(pos == 0, 1.0, 0.0), live)
    for number, row in enumerate(pieces):
        values = jnp.where(index == number, row, values)
    left, right = iota((count, count), 0), iota((count, count), 1)
    ahead = jnp.where(right < left, 1.0, 0.0).astype(bf16)
    same = jnp.where(right == left, 1.0, 0.0).astype(bf16)
    marks = jnp.broadcast_to(first, (ROWS, count)).astype(bf16)
    before = dot(ahead, marks, 1, 1)[:, :1]
    mine = dot(same, marks, 1, 1)[:, :1]
    total = jnp.sum(first, 1, keepdims=True)
    target = jnp.where(mine > 0.5, before, total + iota((count, 1), 0).astype(f32) - before)
    moves = jnp.where(target.astype(jnp.int32) == right, 1.0, 0.0).astype(bf16)
    return dot(values.astype(bf16), moves), total


def attend(xt, w, vec, moved, rows):
    g1, bq, bv, bo, be1 = vec[0:1], vec[3:4], vec[4:5], vec[5:6], vec[6:7]
    seq_id, slot0, live = moved[2:3], moved[3:4], moved[4:5]
    spread, columns = spread_table(rows), column_table(rows)
    index = iota((ROWS, xt.shape[1]), 0).astype(f32)
    pick0 = flag((index == seq_id) & (slot0 > 0.5)).astype(bf16)
    x00 = dot(pick0, xt, 1, 1)
    q = (dot(x00.astype(bf16), w(0)) + bq).astype(bf16)
    q_wide = (dot(spread, q) * columns).astype(bf16)
    qk = dot(q_wide, w(1), 1, 1) * HEAD_DIM ** (-0.5)
    mask = (sequence_of(iota((SIDE, 1), 0), rows).astype(f32) == seq_id) & (live > 0.5)
    scores = jnp.where(mask, dot_split(qk, xt), -1e30)
    raw = jnp.where(mask, jnp.exp(scores - jnp.max(scores, 1, keepdims=True)), 0.0)
    total = jnp.sum(raw, 1, keepdims=True)
    probs = raw / jnp.where(total > 0.0, total, 1.0)
    probs_low = probs.astype(bf16)
    y = dot(probs_low, xt, 1, 1)
    psum = jnp.sum(probs_low.astype(f32), 1, keepdims=True)
    mixed = dot_split(y, w(2)) + psum * bv
    o = dot(spread, (mixed * columns).astype(bf16), 0, 0).astype(bf16)
    normed, inv = layer_norm(x00 + dot(o, w(3)) + bo)
    p_heads = dot(heads_table(rows), probs_low).astype(bf16)
    return normed * g1 + be1, x00.astype(bf16), q, o, probs, psum, normed, inv, qk, y, p_heads


def attend_back(dx1, normed, inv, probs, psum, xt, w, vec, rows):
    g1, bv = vec[0:1], vec[4:5]
    spread, columns = spread_table(rows), column_table(rows)
    d_res = norm_back(dx1, normed, inv, g1)
    d_a = d_res.astype(bf16)
    d_o = dot(d_a, w(3), 1, 1).astype(bf16)
    d_o_wide = dot(spread, d_o) * columns
    vd = dot(d_o_wide.astype(bf16), w(2), 1, 1)
    dp = dot_split(vd, xt) + jnp.sum(d_o_wide * bv, 1, keepdims=True)
    ds = (probs * (dp - jnp.sum(probs * dp, 1, keepdims=True))).astype(bf16)
    z = dot(ds, xt, 1, 1)
    zw = dot_split(z, w(1)) * (HEAD_DIM ** (-0.5)) * columns
    d_q = dot(spread, zw.astype(bf16), 0, 0).astype(bf16)
    extra = d_res + dot(d_q, w(0), 1, 1)
    sums = [
        jnp.sum(dx1 * normed, 0, keepdims=True),
        jnp.sum(dx1, 0, keepdims=True),
        jnp.sum(d_a.astype(f32), 0, keepdims=True),
        jnp.sum(d_q.astype(f32), 0, keepdims=True),
        jnp.sum(d_o_wide * psum, 0, keepdims=True),
    ]
    return d_a, d_o, d_q, sums, vd, z, extra, dot(heads_table(rows), ds).astype(bf16)


def late_parts(vd, z, extra, rows):
    by_table = dot(place_table(rows, 0), vd.astype(bf16)) + dot(place_table(rows, rows * HEADS, rows), extra.astype(bf16))
    return by_table.T, dot(place_table(rows, Z_AT), z.astype(bf16)).T


def early_parts(qk, y, rows):
    return dot(place_table(rows, 0), qk).T, dot(place_table(rows, SIDE), y).T


def block_of(parts, dest, wide):
    by_table, by_rows = parts
    block = D // (2 * wide)
    return by_table[2 * block * dest : 2 * block * (dest + 1)] + jnp.concatenate(
        [by_rows[block * dest : block * (dest + 1)], by_rows[block * (wide + dest) : block * (wide + dest + 1)]], 0
    )


def in_chunks(heads):
    return jnp.concatenate([heads[:, k : k + LANES] for k in range(0, heads.shape[1], LANES)], 0)


def to_tiles(value):
    return jnp.concatenate([value[:, k : k + LANES] for k in range(0, value.shape[1], LANES)], 0)


def from_tiles(got, first, lines=ROWS):
    pieces = [got[:, first + k * lines : first + (k + 1) * lines, :] for k in range(D // LANES)]
    return jnp.concatenate([p.reshape(-1, LANES) for p in pieces], 1)


def ffn(x1, w_up, w_down, bias):
    u = dot(x1.astype(bf16), w_up) + bias
    h = (0.5 * u * (1.0 + lax.erf(u * 0.5**0.5))).astype(bf16)
    return u, h, dot(h, w_down)


def middle(x1, f, u, w_up, w_down, w, vec, picks, valid):
    g2, gc, b2, be2, bc, bec = vec[1:2], vec[2:3], vec[7:8], vec[8:9], vec[9:10], vec[10:11]
    count = x1.shape[0]
    normed2, inv2 = layer_norm(x1 + (f + b2))
    pooled = (normed2 * g2 + be2).astype(bf16)
    normed_c, inv_c = layer_norm(dot(pooled, w(4)) + bc)
    e = (normed_c * gc + bec).astype(bf16)
    scores = dot(e, e, 1, 1) * D ** (-0.5)
    col = iota((count, count), 1)
    is_pos = jnp.where(col == picks[:, 0:1], 1.0, 0.0)
    negs = jnp.zeros_like(is_pos)
    for number in range(1, picks.shape[1]):
        negs = negs + jnp.where(col == picks[:, number : number + 1], 1.0, 0.0)
    taken = (is_pos + negs) > 0.0
    top = jnp.max(jnp.where(taken, scores, -1e30), 1, keepdims=True)
    raw = jnp.where(taken, jnp.exp(scores - top), 0.0)
    total = jnp.sum(raw * (is_pos + negs), 1, keepdims=True)
    total = jnp.where(total > 0.0, total, 1.0)
    share = raw / total
    valid_count = jnp.sum(valid, 0, keepdims=True)
    per_query = top + jnp.log(total) - jnp.sum(is_pos * scores, 1, keepdims=True)
    loss = jnp.sum(jnp.where(valid > 0.0, valid * per_query, 0.0), 0, keepdims=True) / valid_count
    weight = valid / valid_count
    d_pos = (weight * (share - 1.0)).astype(bf16).astype(f32)
    d_neg = (weight * share).astype(bf16).astype(f32)
    d_scores = d_pos * is_pos + d_neg * negs
    high, rest = split(d_scores)
    d_e = (dot(high, e) + dot(rest, e) + dot(high, e, 0, 0) + dot(rest, e, 0, 0)) * D ** (-0.5)
    d_c = norm_back(d_e, normed_c, inv_c, gc).astype(bf16)
    d_x2 = dot(d_c, w(4), 1, 1)
    d_res2 = norm_back(d_x2, normed2, inv2, g2)
    d_f = d_res2.astype(bf16)
    d_h = dot(d_f, w_down, 1, 1)
    slope = 0.5 * (1.0 + lax.erf(u * 0.5**0.5)) + u * jnp.exp(-0.5 * u * u) * (2.0 * np.pi) ** (-0.5)
    d_u = (d_h * slope).astype(bf16)
    d_x1 = dot(d_u, w_up, 1, 1)
    sums = [
        jnp.sum(d_x2 * normed2, 0, keepdims=True),
        jnp.sum(d_e * normed_c, 0, keepdims=True),
        jnp.sum(d_f.astype(f32), 0, keepdims=True),
        jnp.sum(d_x2, 0, keepdims=True),
        jnp.sum(d_c.astype(f32), 0, keepdims=True),
        jnp.sum(d_e, 0, keepdims=True),
    ]
    return loss, pooled, d_c, d_res2, d_f, d_u, d_x1, sums


def update(weight, first, second, gradient, rate, scale_one, scale_two):
    first_new = 0.9 * first + 0.1 * gradient
    second_new = 0.999 * second + 0.001 * gradient * gradient
    first_hat = first_new * scale_one
    second_hat = second_new * scale_two
    return weight - rate * (first_hat / (jnp.sqrt(second_hat) + 1e-08) + 0.01 * weight), first_new, second_new


def shape(dims, kind=f32):
    return jax.ShapeDtypeStruct(dims, kind)


MIB = 1 << 20


def full_block(dims):
    return pl.BlockSpec(dims, lambda i: (0,) * len(dims), pipeline_mode=pl.Buffered(1))


def pinned(x):
    return pltpu.with_memory_space_constraint(x, pltpu.HBM)


def call(kernel, outs, *args, scalars=(), far=(), far_outs=(), after=(), near=(), near_outs=(), scratch=(), vmem=24, name=None, flops=0):
    anywhere = pl.BlockSpec(memory_space=pl.ANY)
    in_specs = [pl.BlockSpec(memory_space=pltpu.SMEM)] * len(scalars) + [anywhere] * len(far)
    in_specs += [full_block(a.shape) for a in args] + [anywhere] * len(after)
    moved = sum(int(np.prod(a.shape)) * a.dtype.itemsize for a in list(args) + list(far) + list(outs) + list(far_outs))
    used = len(scalars) + len(far) + len(args)

    def run(*refs):
        kernel(*refs[:used], *refs[used + len(after) :])

    shapes = [o if k in near_outs else pltpu.HBM(o.shape, o.dtype) for k, o in enumerate(outs)]
    shapes += [pltpu.HBM(o.shape, o.dtype) for o in far_outs]
    args = [a if k in near else pinned(a) for k, a in enumerate(args)]
    return pl.pallas_call(
        run,
        grid=(1,),
        out_shape=shapes,
        in_specs=in_specs,
        out_specs=[full_block(o.shape) for o in outs] + [anywhere] * len(far_outs),
        scratch_shapes=list(scratch),
        compiler_params=pltpu.CompilerParams(vmem_limit_bytes=vmem * MIB),
        cost_estimate=pl.CostEstimate(flops=int(flops), bytes_accessed=moved, transcendentals=0),
        name=name,
    )(*scalars, *(pinned(a) for a in far), *args, *after)


def square_weights(mats, first, buffers, signals, order):
    copies = {
        k: pltpu.make_async_copy(mats.at[:, pl.ds(k * D, D)], buffers.at[k - first], signals.at[k - first]) for k in order
    }
    for k in order:
        copies[k].start()
    ready = {}

    def get(k):
        if k not in ready:
            copies[k].wait()
            ready[k] = buffers[k - first]
        return ready[k]

    return get


def weight_scratch(count):
    return [pltpu.VMEM((count, D, D), bf16), pltpu.SemaphoreType.DMA((count,))]


def prepare_kernel(group_rows, count, base, seq, pos, packet, moved):
    chunks = count // LANES
    line = lambda first: jnp.concatenate([base[first + k : first + k + 1, :] for k in range(chunks)], 1).astype(jnp.int32)
    got, total = prepare(line(0), line(chunks), seq[...], pos[...], group_rows)
    moved[...] = got
    sent, code = got[0:1] * 256.0 + got[1:2], got[2:3] + 8.0 * got[3:4]
    lines = [sent[:, k * LANES : (k + 1) * LANES] for k in range(chunks)]
    lines += [code[:, k * LANES : (k + 1) * LANES] for k in range(chunks)]
    whole = base[...]
    index = iota(whole.shape, 0)
    for number, value in enumerate(lines):
        whole = jnp.where(index == number, value, whole)
    whole = jnp.where((index == 2 * chunks) & (iota(whole.shape, 1) == 0), total, whole)
    whole = jnp.where(index > 2 * chunks, whole.astype(bf16).astype(f32), whole)
    for dest in range(packet.shape[0]):
        packet[dest] = whole


def cast_kernel(attn_in, attn_out, head, out):
    out[:, : 3 * D] = attn_in[...].astype(bf16)
    out[:, 3 * D : 4 * D] = attn_out[...].astype(bf16)
    out[:, 4 * D :] = head[...].astype(bf16)


def build_kernel(emb, table):
    feats, vocab = emb.shape
    half = table.shape[0]
    blocks, second = half // LANES, (vocab - half) // LANES
    gap = jnp.zeros((SIDE - feats, LANES), f32)

    def build(b, both):
        start = pl.multiple_of(b * LANES, LANES)
        low = emb[:, pl.ds(start, LANES)]
        high = jnp.zeros_like(low)
        if both:
            high = emb[:, pl.ds(pl.multiple_of(half + start, LANES), LANES)]
        table[pl.ds(start, LANES), :] = jnp.concatenate([low, gap, high, gap], 0).astype(bf16).T.astype(f32)

    unroll = 7

    def step(i, carry):
        for k in range(unroll):
            build(i * unroll + k, True)
        return carry

    lax.fori_loop(0, second // unroll, step, 0)
    for b in range(second // unroll * unroll, blocks):
        build(jnp.int32(b), b < second)


def side_of(ids, group, half_rows, half):
    local = ids - (group * half_rows).astype(f32)
    inside = (local >= 0.0) & (local < float(half_rows))
    return jnp.where(inside, jnp.where(local >= float(half), 2.0, 1.0), 0.0)


def own_span(first, group, count):
    return jnp.where(group == 0, 0, first), jnp.where(group == 0, first, count)


def lookup_kernel(half_rows, per, unroll, add, where, numbers, firsts, packet, table, *refs):
    out, buf = refs[-2:]
    feats, count = out.shape[1:]
    group = where[0]
    chunks = count // LANES
    half = table.shape[0]
    eye = jnp.where(iota((LANES, LANES), 0) == iota((LANES, LANES), 1), 1.0, 0.0).astype(bf16)
    at = pl.program_id(0) * per
    for s in range(per):
        low, high = own_span(firsts[at + s], group, count)
        base = (at + s) * count

        def step(i, carry):
            for k in range(unroll):
                t = i * unroll + k
                buf[pl.ds(s * count + t, 1), :] = table[pl.ds(numbers[base + t], 1), :]
            return carry

        lax.fori_loop(low // unroll, (high + unroll - 1) // unroll, step, 0)
    for s in range(per):
        side = side_of(lanes_of(packet, s, 0, chunks), group, half_rows, half)
        turned = dot(eye, buf[s * count : (s + 1) * count, :].astype(bf16), 1, 1)
        pick = jnp.where(side > 1.5, turned[SIDE : SIDE + feats], turned[:feats])
        value = jnp.where(side > 0.5, pick, 0.0)
        if add:
            value = value + refs[0][s].astype(f32)
        out[s] = value.astype(bf16)


def lanes_of(packet, s, first, chunks):
    return jnp.concatenate([packet[s, first + c : first + c + 1, :] for c in range(chunks)], 1)


def lookup(where, numbers, firsts, packets, table, half_rows, feats, count, add=None, per=4, unroll=32):
    sources = packets.shape[0]
    some = lambda dims: pl.BlockSpec((per,) + dims, lambda i, *s: (i, 0, 0))
    extra = [] if add is None else [add]
    return pl.pallas_call(
        partial(lookup_kernel, half_rows, per, unroll, add is not None),
        out_shape=shape((sources, feats, count), bf16),
        grid_spec=pltpu.PrefetchScalarGridSpec(
            num_scalar_prefetch=3,
            grid=(sources // per,),
            in_specs=[some(packets.shape[1:]), pl.BlockSpec(table.shape, lambda i, *s: (0, 0), pipeline_mode=pl.Buffered(1))] + [some((feats, count)) for _ in extra],
            out_specs=some((feats, count)),
            scratch_shapes=[pltpu.VMEM((per * count, LANES), f32)],
        ),
        compiler_params=pltpu.CompilerParams(vmem_limit_bytes=16 * MIB),
        cost_estimate=pl.CostEstimate(flops=10**9, bytes_accessed=10**7, transcendentals=0),
        name="lookup" if add is None else "lookup_add",
    )(where, numbers, firsts, packets, pinned(table), *extra)


def spread_kernel(rows, half_rows, feats, per, unroll, copies, at_early, at_heads, where, numbers, firsts, packet, early_own, early_other, late_own, late_other, p_own, p_other, out, square, *scratch):
    parts, buf = scratch[:copies], scratch[copies]
    group = where[0]
    chunks = buf.shape[0] // (per * LANES)
    count = chunks * LANES
    half = parts[0].shape[0]
    vocab = out.shape[1]
    blocks = half // LANES
    step_at = pl.program_id(0)

    @pl.when(step_at == 0)
    def _():
        def clear(i, carry):
            for part in parts:
                part[pl.ds(pl.multiple_of(i * LANES, LANES), LANES), :] = jnp.zeros((LANES, LANES), f32)
            return carry

        lax.fori_loop(0, blocks, clear, 0)

    eye = jnp.where(iota((LANES, LANES), 0) == iota((LANES, LANES), 1), 1.0, 0.0).astype(bf16)
    gap = jnp.zeros((SIDE - feats, count), f32)
    lane = iota((LANES, 16), 0)
    low_heads = flag(head_of(lane, rows) == iota((LANES, 16), 1)).astype(bf16)
    lane = iota((LANES, 1), 0)
    seq_low = sequence_of(lane, rows).astype(f32)
    seq_extra = jnp.where((lane >= rows * HEADS) & (lane < rows * HEADS + rows), lane - rows * HEADS, 99).astype(f32)

    is_own = step_at < pl.num_programs(0) // 2

    def early(s, first, lines):
        return jnp.where(is_own, early_own[s, first : first + lines, :], early_other[s, first : first + lines, :])

    def late(s, first, lines):
        return jnp.where(is_own, late_own[s, first : first + lines, :], late_other[s, first : first + lines, :])

    def heads(s, first, lines):
        return jnp.where(is_own, p_own[s, first : first + lines, :], p_other[s, first : first + lines, :])

    def side_by_side(lines):
        return jnp.concatenate([lines[16 * c : 16 * (c + 1)] for c in range(chunks)], 1)

    for s in range(per):
        code = lanes_of(packet, s, chunks, chunks)
        slot0 = code >= 8.0
        seq = jnp.where(slot0, code - 8.0, code)
        here = seq_low == seq
        score_part = jnp.where(here, dot(low_heads, side_by_side(late(s, feats, 16 * chunks))), 0.0)
        value_part = jnp.where(here, dot(low_heads, side_by_side(heads(s, at_heads, 16 * chunks))), 0.0)
        value_part = jnp.where((seq_extra == seq) & slot0, 1.0, value_part)
        basis = jnp.concatenate([early(s, at_early, feats), late(s, 0, feats)], 1)
        x = dot(basis, jnp.concatenate([score_part, value_part], 0).astype(bf16))
        side = side_of(lanes_of(packet, s, 0, chunks), group, half_rows, half)
        tall = jnp.concatenate([jnp.where(side == 1.0, x, 0.0), gap, jnp.where(side == 2.0, x, 0.0), gap], 0).astype(bf16)
        for c in range(chunks):
            start = s * count + c * LANES
            buf[start : start + LANES, :] = dot(eye, tall[:, c * LANES : (c + 1) * LANES], 1, 1)
    for s in range(per):
        low, high = own_span(firsts[step_at * per + s], group, count)
        base = (step_at * per + s) * count

        def step(i, carry):
            for k in range(unroll):
                t = i * unroll + k
                part = parts[k % copies]
                row = numbers[base + t]
                part[pl.ds(row, 1), :] = part[pl.ds(row, 1), :] + buf[pl.ds(s * count + t, 1), :]
            return carry

        lax.fori_loop(low // unroll, (high + unroll - 1) // unroll, step, 0)

    @pl.when(step_at == pl.num_programs(0) - 1)
    def _():
        def emit(b, total, both):
            start = pl.multiple_of(b * LANES, LANES)
            lines = parts[0][pl.ds(start, LANES), :]
            for part in parts[1:]:
                lines = lines + part[pl.ds(start, LANES), :]
            turned = lines.T
            out[:, pl.ds(start, LANES)] = turned[:feats]
            if both:
                out[:, pl.ds(pl.multiple_of(half + start, LANES), LANES)] = turned[SIDE : SIDE + feats]
            return total + lines * lines

        second = (vocab - half) // LANES
        total = lax.fori_loop(0, second, lambda b, t: emit(b, t, True), jnp.zeros((LANES, LANES), f32))
        for b in range(second, blocks):
            total = emit(jnp.int32(b), total, False)
        square[...] = jnp.sum(total.reshape(LANES // ROWS, ROWS, LANES), 0)


def spread_tokens(where, numbers, firsts, packets, early, late, p_heads, at_early, rows, half_rows, feats, count, per=8, unroll=32, copies=4):
    devices = packets.shape[0]
    block = packets.shape[1:]
    half = -(-half_rows // (2 * LANES)) * LANES
    some = lambda dims: pl.BlockSpec((per,) + dims, lambda i, *s: (i, 0, 0))
    steps = devices // per
    mine = lambda pair: pl.BlockSpec((per,) + pair[0].shape[1:], lambda i, *s: (jnp.minimum(i, steps // 2 - 1), 0, 0))
    theirs = lambda pair: pl.BlockSpec((per,) + pair[0].shape[1:], lambda i, *s: (jnp.maximum(i - steps // 2, 0), 0, 0))
    return pl.pallas_call(
        partial(spread_kernel, rows, half_rows, feats, per, unroll, copies, at_early, at_early),
        out_shape=[pltpu.HBM((feats, half_rows), f32), pltpu.HBM((ROWS, LANES), f32)],
        grid_spec=pltpu.PrefetchScalarGridSpec(
            num_scalar_prefetch=3,
            grid=(steps,),
            in_specs=[some(block), mine(early), theirs(early), mine(late), theirs(late), mine(p_heads), theirs(p_heads)],
            out_specs=[pl.BlockSpec((feats, half_rows), lambda i, *s: (0, 0), pipeline_mode=pl.Buffered(1)), pl.BlockSpec((ROWS, LANES), lambda i, *s: (0, 0))],
            scratch_shapes=[pltpu.VMEM((half, LANES), f32)] * copies + [pltpu.VMEM((per * count, LANES), f32)],
        ),
        compiler_params=pltpu.CompilerParams(vmem_limit_bytes=44 * MIB),
        cost_estimate=pl.CostEstimate(flops=10**9, bytes_accessed=3 * 10**7, transcendentals=0),
        name="spread_tokens",
    )(where, numbers, firsts, packets, *early, *late, *p_heads)


def attend_kernel(rows, mats, xt, vec, moved, sent, heads_out, facts, probs_out, psum_out, normed_out, inv_out, *scratch):
    w = square_weights(mats, 0, *scratch, (0, 1, 2, 3))
    x1, x00, q, o, probs, psum, normed, inv, qk, y, p_heads = attend(xt[...], w, vec[...], moved[...], rows)
    tiles = to_tiles(x1)
    parts = early_parts(qk.astype(bf16), y.astype(bf16), rows)
    for dest in range(sent.shape[0]):
        sent[dest] = jnp.concatenate([tiles, block_of(parts, dest, sent.shape[0])], 0).astype(bf16)
    heads_out[...] = in_chunks(p_heads)
    facts[...] = jnp.concatenate([to_tiles(value.astype(f32)) for value in (x00, q, o)], 0).astype(bf16)
    probs_out[...], psum_out[...], normed_out[...], inv_out[...] = probs, psum, normed, inv


def attend_back_kernel(rows, place, mats, got, d_res2, sums_up, normed, inv, probs, psum, xt, vec, late_out, last, *scratch):
    w = square_weights(mats, 0, *scratch, (3, 2, 1, 0))
    wide = late_out.shape[0]
    dx1 = d_res2[pl.ds(pl.multiple_of(place[0] * ROWS, ROWS), ROWS), :]
    for k in range(wide):
        dx1 = dx1 + got[k].astype(f32)
    d_a, d_o, d_q, sums, vd, z, extra, ds_heads = attend_back(
        dx1, normed[...], inv[...], probs[...], psum[...], xt[...], w, vec[...], rows
    )
    parts = late_parts(vd, z, extra, rows)
    chunks = in_chunks(ds_heads)
    tail = stack_rows(sums + [sums_up[...]])
    for dest in range(wide):
        late_out[dest] = jnp.concatenate([block_of(parts, dest, wide).astype(bf16), chunks], 0)
    last[...] = jnp.concatenate([to_tiles(value.astype(f32)) for value in (d_q, d_o, d_a, tail)], 0).astype(bf16)


def pack_kernel(facts, last, d_up, out):
    wide = out.shape[0]
    block = d_up.shape[0] // (2 * wide)
    values = jnp.concatenate([facts[...], last[...]], 0)
    gap = jnp.zeros((block, LANES - d_up.shape[1]), f32)
    for dest in range(wide):
        pieces = [d_up[block * n : block * (n + 1), :].astype(f32) for n in (dest, wide + dest)]
        pieces = [jnp.concatenate([piece, gap], 1) for piece in pieces]
        out[dest] = jnp.concatenate([values, jnp.concatenate(pieces, 0).astype(bf16)], 0)


def rows_of(own, other):
    return jnp.concatenate([from_tiles(own[...], 0), from_tiles(other[...], 0)], 0)


def ffn_kernel(x_own, x_other, w_up, w_down, bias, u_out, h_out, own, other):
    u, h, f = ffn(rows_of(x_own, x_other), w_up[...], w_down[...], bias[...])
    half = own.shape[0]
    u_out[...], h_out[...] = u, h
    own[...] = f[:half]
    other[...] = f[half:].astype(bf16)


def total_kernel(got, heads, out):
    total = got[0].astype(f32)
    for k in range(1, got.shape[0]):
        total = total + got[k].astype(f32)
    lines = jnp.concatenate([to_tiles(total).astype(bf16), heads[...]], 0)
    for k in range(out.shape[0]):
        out[k] = lines


def middle_kernel(mats, x_own, x_other, f_own, f_other, u, w_up, w_down, vec, picks, valid, loss, pooled, d_c, d_res2, d_f, d_u, own, other, sums, sums_up, *scratch):
    w = square_weights(mats, 4, *scratch, (4,))
    x1 = rows_of(x_own, x_other).astype(f32)
    f = rows_of(f_own, f_other).astype(f32)
    got = middle(x1, f, u[...], w_up[...], w_down[...], w, vec[...], picks[...], valid[...])
    half = own.shape[0]
    loss[...], pooled[...], d_c[...], d_res2[...], d_f[...], d_u[...] = got[:6]
    own[...] = got[6][:half]
    other[...] = got[6][half:].astype(bf16)
    sums[...] = stack_rows(got[7])
    su = jnp.sum(got[5].astype(f32), 0, keepdims=True)
    sums_up[...] = jnp.concatenate([su, jnp.zeros((1, D - su.shape[1]), f32)], 1)


def own_cols(device, block):
    index = iota((D, LANES), 1)
    return jnp.where((iota((D, LANES), 0) == device * block + index) & (index < block), 1.0, 0.0).astype(bf16)


def own_rows(left, right, mine, block):
    return dot(dot(left, mine).astype(bf16), right, 0, 0)[:block]


def up_grad_kernel(x_own, x_other, d_u, d_up):
    x1 = rows_of(x_own, x_other)
    d_up[...] = dot(x1, d_u[...], 0, 0).astype(bf16)


def ffn_grads_kernel(where, h, d_f, pooled, d_c, d_down, d_head):
    d_down[...] = dot(h[...], d_f[...], 0, 0)
    block = d_head.shape[0]
    d_head[...] = own_rows(pooled[...], d_c[...], own_cols(where[1], block), block)


def grads_kernel(rows, at_early, where, early_own, early_other, late_own, late_other, facts_own, facts_other, d_wh, d_down, sums, square, in_out, out_out, up_out, vec_out, square_out, x00, q_all, o_all, d_q, d_o, d_a, y, z, wide_z):
    group, device = where[0], where[1]
    wide = facts_own.shape[0]
    devices = 2 * wide
    block = in_out.shape[0]
    first = group == 0
    for n in range(devices):
        at = slice(n * block, (n + 1) * block)
        early = (early_own, early_other)[n // wide]
        mine = [early[n % wide, at_early + k * block : at_early + (k + 1) * block, :].astype(f32) for k in range(2)]
        y[at, :] = jnp.where(first, *mine)
        late = (late_own, late_other)[n // wide]
        mine = [late[n % wide, k * block : (k + 1) * block, :].astype(f32) for k in range(2)]
        z[at, :] = jnp.where(first, *mine)
    for base, facts in ((0, facts_own), (1, facts_other)):
        at = slice(base * wide * ROWS, (base + 1) * wide * ROWS)
        lines = ROWS * (D // LANES)
        for k, out in enumerate((x00, q_all, o_all, d_q, d_o, d_a)):
            out[at, :] = from_tiles(facts, k * lines).astype(f32)
        hidden = FF // devices
        lines = 7 * lines
        for n in range(wide):
            piece = jnp.where(first, facts[n, lines : lines + block, :].astype(f32), facts[n, lines + block : lines + 2 * block, :].astype(f32))
            here, there = n * hidden, (wide + n) * hidden

            @pl.when(group == base)
            def _():
                up_out[:, here : here + hidden] = piece[:, :hidden]

            @pl.when(group != base)
            def _():
                up_out[:, there : there + hidden] = piece[:, :hidden]

    def by_heads(source, first, values):
        total = jnp.zeros((block, D), f32)
        low = source[...].astype(bf16)
        for r in range(rows):
            wide_z[...] = dot(low, expand_table(rows, first, r))
            for n in range(devices):
                total = total + wide_z[n * block : (n + 1) * block, :] * values[n * ROWS + r : n * ROWS + r + 1, :]
        return total

    d_wk = by_heads(z, Z_AT, q_all) * HEAD_DIM ** (-0.5)
    d_wv = by_heads(y, SIDE, d_o)
    mine = own_cols(device, block)
    d_wq = own_rows(x00[...].astype(bf16), d_q[...].astype(bf16), mine, block)
    d_wo = own_rows(o_all[...].astype(bf16), d_a[...].astype(bf16), mine, block)
    square_now = square[...]

    def fold(square_now, value):
        tiles = value * value
        total = jnp.sum(tiles.reshape(tiles.shape[0] // ROWS, ROWS, tiles.shape[1]), 0)
        for k in range(total.shape[1] // LANES):
            square_now = square_now + total[:, k * LANES : (k + 1) * LANES]
        return square_now

    in_out[:, :D], in_out[:, D : 2 * D], in_out[:, 2 * D :] = d_wq, d_wk, d_wv
    out_out[...] = d_wo
    for value in (d_wq, d_wk, d_wv, d_wo, d_wh[...], up_out[...], d_down[...]):
        square_now = fold(square_now, value)
    tails = jnp.concatenate([from_tiles(facts, 6 * ROWS * (D // LANES)) for facts in (facts_own, facts_other)], 0).astype(f32)
    tail = jnp.sum(tails.reshape(devices, ROWS, D), 0)
    mids = sums[...]
    pieces = [tail[0:1], mids[0:1], mids[1:2], tail[3:4], tail[4:5], tail[2:3], tail[1:2]] + [mids[k : k + 1] for k in range(2, 6)]
    index = iota((16, D), 0)
    total = jnp.zeros((16, D), f32)
    for number, row in enumerate(pieces):
        total = jnp.where(index == number, row, total)
    each = D // hidden
    for base in range(2):
        for k in range(wide):
            line = (base * wide + k) * ROWS + 5
            row = tails[line : line + 1]
            shift = hidden * (k % each)
            row = pltpu.roll(row, shift, 1) if shift else row
            number = 11 + (k // each) + jnp.where(group == base, 0, wide // each)
            total = total + jnp.where(index == number, row, 0.0)
    vec_out[...] = total
    square_now = square_now + fold(jnp.zeros((ROWS, LANES), f32), total) / devices
    for k in range(wide):
        square_out[k] = square_now


def adam_kernel(count, scales, weight, first, second, d_table, own, other, *refs):
    grads, state = refs[:count], refs[count : 4 * count]
    norm_out, factor_out = refs[4 * count : 4 * count + 2]
    outs = refs[4 * count + 2 : 7 * count + 2]
    far = refs[7 * count + 2 : 7 * count + 5]
    loads, stores, got, sent = refs[7 * count + 5 :]
    slots, lines = loads.shape[0], loads.shape[2]
    jobs = weight.shape[0] // lines
    sources = (weight, first, second, d_table)

    def load(j):
        return [pltpu.make_async_copy(ref.at[pl.ds(j * lines, lines), :], loads.at[j % slots, k], got.at[j % slots, k]) for k, ref in enumerate(sources)]

    def store(j):
        return [pltpu.make_async_copy(stores.at[j % slots, k], ref.at[pl.ds(j * lines, lines), :], sent.at[j % slots, k]) for k, ref in enumerate(far)]

    for j in range(min(slots, jobs)):
        for copy in load(j):
            copy.start()
    total = own[0] + other[0]
    for k in range(1, own.shape[0]):
        total = total + own[k] + other[k]
    total = jnp.sum(jnp.sum(total, 0, keepdims=True), 1, keepdims=True)
    norm = jnp.sqrt(total)
    factor = jnp.minimum(1.0, clip_level / (norm + 1e-06))
    norm_out[...], factor_out[...] = norm, factor
    one, two = scales[0], scales[1]
    for j in range(jobs):
        for copy in load(j):
            copy.wait()
        if j >= slots:
            for copy in store(j - slots):
                copy.wait()
        old = [loads[j % slots, k] for k in range(3)]
        new = update(*old, loads[j % slots, 3] * factor, RATES[0], one, two)
        for k in range(3):
            stores[j % slots, k] = new[k]
        for copy in store(j):
            copy.start()
        if j + slots < jobs:
            for copy in load(j + slots):
                copy.start()
    for number in range(count):
        old = [state[3 * number + k][...] for k in range(3)]
        new = update(*old, grads[number][...] * factor, RATES[number + 1], one, two)
        for k in range(3):
            outs[3 * number + k][...] = new[k]
    for j in range(max(0, jobs - slots), jobs):
        for copy in store(j):
            copy.wait()


def swap(x):
    return lax.ppermute(x, "group", [(0, 1), (1, 0)])


def exchange(x):
    return lax.all_to_all(x, "wide", split_axis=0, concat_axis=0, tiled=True)


def tie(*values):
    return lax.optimization_barrier(values)


def pair(x):
    own = exchange(x)
    return own, swap(own)


def in_order(own, other, group):
    return jnp.where(group == 0, jnp.concatenate([own, other], 0), jnp.concatenate([other, own], 0))


def plain_body(wide, passage_ids, query_ids, passage_len, query_len, positive, negatives, valid, step_count, *state):
    params, firsts, seconds = state[0::3], state[1::3], state[2::3]
    embedding, attn_in, attn_out, w_ffn_up, w_ffn_down, head, vectors = params
    group, place = lax.axis_index("group"), lax.axis_index("wide")
    device, devices = group * wide + place, 2 * wide
    feats, half_rows = embedding.shape
    block, hidden = D // devices, FF // devices
    pas_count, pas_len = passage_ids.shape
    qry_count, qry_len = query_ids.shape
    rows = pas_count + qry_count
    tokens = pas_count * pas_len + qry_count * qry_len
    live = rows * HEADS
    both = lambda x: jnp.concatenate(pair(x), 0)
    gather = lambda x: both(jnp.broadcast_to(x[None], (wide,) + x.shape))
    ids = jnp.concatenate([passage_ids.reshape(-1), query_ids.reshape(-1)])
    seq_np = np.concatenate([np.repeat(np.arange(pas_count), pas_len), pas_count + np.repeat(np.arange(qry_count), qry_len)])
    pos_np = np.concatenate([np.tile(np.arange(pas_len), pas_count), np.tile(np.arange(qry_len), qry_count)])
    lens = jnp.concatenate([jnp.repeat(passage_len, pas_len), jnp.repeat(query_len, qry_len)])
    moved = jnp.zeros((ROWS, tokens), f32).at[2].set(jnp.asarray(seq_np, f32)).at[3].set(jnp.asarray(pos_np == 0, f32))
    moved = moved.at[4].set(flag(jnp.asarray(pos_np) < lens))
    note = jnp.concatenate([ids, valid, positive, negatives.reshape(-1)])
    notes = gather(jnp.pad(note, (0, -note.shape[0] % LANES)).reshape(-1, LANES)).reshape(devices, -1)
    low_vectors = gather(jnp.pad(vectors.astype(bf16), (0, -vectors.shape[0] % LANES)).reshape(-1, LANES))
    vec = in_order(low_vectors[:wide], low_vectors[wide:], group).reshape(devices, -1)[:, : vectors.shape[0]].astype(f32).reshape(-1, D)
    all_ids = notes[:, :tokens]
    valid_rows = jnp.pad(notes[:, tokens : tokens + qry_count].astype(f32), ((0, 0), (pas_count, ROWS - rows))).reshape(-1, 1)
    at = tokens + qry_count
    picked = jnp.concatenate(
        [notes[:, at : at + qry_count, None], notes[:, at + qry_count : at + qry_count + negatives.size].reshape(devices, qry_count, -1)], 2
    )
    pick_dev = picked // pas_count
    pick_row = (((pick_dev // wide) ^ group) * wide + pick_dev % wide) * ROWS + picked % pas_count
    pick_rows = jnp.pad(pick_row, ((0, 0), (pas_count, ROWS - rows), (0, 0)), constant_values=-1).reshape(devices * ROWS, -1)
    mats = lax.all_gather(jnp.concatenate([attn_in, attn_out, head], 1).astype(bf16), ALL, axis=0, tiled=True)
    w = lambda k: mats[:, k * D : (k + 1) * D]
    w_up = lax.all_to_all(
        w_ffn_up.astype(bf16).reshape(block, devices, hidden).transpose(1, 0, 2), ALL, split_axis=0, concat_axis=0, tiled=True
    ).reshape(D, hidden)
    w_down = w_ffn_down.astype(bf16)
    bias_up = lax.dynamic_slice(vec.reshape(-1), (11 * D + device * hidden,), (hidden,))[None]
    local = all_ids - group * half_rows
    inside = ((local >= 0) & (local < half_rows)).reshape(1, -1)
    local = jnp.clip(local, 0, half_rows - 1).reshape(-1)
    looked = jnp.where(inside, jnp.take(embedding.astype(bf16), local, axis=1), jnp.zeros((), bf16))
    looked = looked.reshape(feats, devices, tokens).transpose(1, 0, 2)
    xt = exchange(looked[:wide] + swap(looked[wide:])).reshape(D, tokens)
    x1, x00, q, o, probs, psum, normed1, inv1, qk, y, p_heads = attend(xt, w, vec, moved, rows)
    x1_all = gather(x1.astype(bf16)).reshape(devices * ROWS, D)

    def to_owner(parts):
        mine = parts[: wide * ROWS] + swap(parts[wide * ROWS :])
        return jnp.sum(exchange(mine.astype(bf16).reshape(wide, ROWS, D)).astype(f32), 0)

    u, h, f_part = ffn(x1_all, w_up, w_down, bias_up)
    f_all = gather(to_owner(f_part).astype(bf16)).reshape(devices * ROWS, D).astype(f32)
    loss, pooled, d_c, d_res2, d_f, d_u, d_x1, sums = middle(x1_all.astype(f32), f_all, u, w_up, w_down, w, vec, pick_rows, valid_rows)
    d_x1 = lax.dynamic_slice(d_res2, (place * ROWS, 0), (ROWS, D)) + to_owner(d_x1)
    d_a, d_o, d_q, sums_back, vd, z, extra, ds_heads = attend_back(d_x1, normed1, inv1, probs, psum, xt, w, vec, rows)

    to_features = lambda t: both(t.T.astype(bf16).reshape(wide, feats, -1))

    def to_blocks(t):
        parts = t.T.astype(bf16).reshape(2, wide, block, -1).transpose(1, 0, 2, 3).reshape(wide, 2 * block, -1)
        got = both(parts).reshape(devices, 2, block, -1)
        return lax.dynamic_index_in_dim(got, group, 1, keepdims=False)[:, :, :live].reshape(devices, block, rows, HEADS)

    facts = gather(jnp.concatenate([x00, q, o, d_q, d_o, d_a], 0)).reshape(devices, 6, ROWS, D)
    flat_fact = lambda k: facts[:, k].reshape(devices * ROWS, D)
    by_head = lambda k: facts[:, k].reshape(devices, ROWS, HEADS, HEAD_DIM)[:, :rows]
    cut = lambda m: lax.dynamic_slice(m, (0, device * block), (devices * ROWS, block))
    d_wq = dot(cut(flat_fact(0)), flat_fact(3), 0, 0)
    d_wk = jnp.einsum("nfrh,nrhd->fhd", to_blocks(z), by_head(1), preferred_element_type=f32).reshape(block, D) * HEAD_DIM ** (-0.5)
    d_wv = jnp.einsum("nfrh,nrhd->fhd", to_blocks(y), by_head(4), preferred_element_type=f32).reshape(block, D)
    d_wo = dot(cut(flat_fact(2)), flat_fact(5), 0, 0)
    d_wup = dot(x1_all, d_u, 0, 0).astype(bf16).reshape(devices, block, hidden)
    d_wup = lax.all_to_all(d_wup, ALL, split_axis=0, concat_axis=0, tiled=True).astype(f32).transpose(1, 0, 2).reshape(block, FF)
    sums_up = jnp.pad(jnp.sum(d_u.astype(f32), 0, keepdims=True), ((0, 0), (0, D - hidden)))
    tails = gather(stack_rows(sums_back + [sums_up]))
    tail = jnp.sum(tails, 0)
    ups = in_order(tails[:wide], tails[wide:], group)[:, 5, :hidden].reshape(-1)
    mids = [row[0] for row in sums]
    d_vec = jnp.concatenate([tail[0], mids[0], mids[1], tail[3], tail[4], tail[2], tail[1]] + mids[2:] + [ups])
    d_vec = lax.dynamic_slice(d_vec, (device * vectors.shape[0],), vectors.shape)
    basis = jnp.concatenate([to_features(qk), to_features(vd), to_features(extra)], 2)
    lanes = gather(jnp.concatenate([ds_heads, p_heads], 0))
    seq = jnp.asarray(seq_np, jnp.int32)[None]
    here = sequence_of(iota((SIDE, 1), 0), rows) == seq
    widen = lambda t: jnp.where(here[None], jnp.einsum("ha,nht->nat", heads_table(rows), t, preferred_element_type=f32), 0.0).astype(bf16)
    first = ((iota((ROWS, 1), 0) == seq) & jnp.asarray(pos_np == 0)[None]).astype(bf16)
    coef = jnp.concatenate([widen(lanes[:, :16]), widen(lanes[:, 16:]), jnp.broadcast_to(first[None], (devices,) + first.shape)], 1)
    d_tok = jnp.einsum("nfa,nat->fnt", basis, coef, preferred_element_type=f32).reshape(feats, -1)
    d_table = jnp.zeros((feats, half_rows), f32).at[:, local].add(jnp.where(inside, d_tok, 0.0))
    d_head = dot(cut(pooled), d_c, 0, 0)
    grads = (d_table, jnp.concatenate([d_wq, d_wk, d_wv], 1), d_wo, d_wup, dot(h, d_f, 0, 0), d_head, d_vec)
    squares = sum(jnp.sum(g * g) for g in grads)
    grad_norm = jnp.sqrt(jnp.sum(gather(jnp.full((ROWS, LANES), squares))[:, 0, 0]))
    factor = jnp.minimum(1.0, clip_level / (grad_norm + 1e-06))
    step_float = step_count[0].astype(f32)
    one, two = 1.0 / (1.0 - jnp.power(0.9, step_float)), 1.0 / (1.0 - jnp.power(0.999, step_float))
    new = [update(params[k], firsts[k], seconds[k], grads[k] * factor, RATES[k], one, two) for k in range(7)]
    return (loss[0, 0], grad_norm) + tuple(t for group_of in new for t in group_of)


def body(wide, passage_ids, query_ids, passage_len, query_len, positive, negatives, valid, step_count, *state):
    embedding, attn_in, attn_out, w_ffn_up, w_ffn_down, head, vectors = state[0::3]
    group = lax.axis_index("group")
    place = lax.axis_index("wide")
    device = group * wide + place
    devices = 2 * wide
    feats, half_rows = embedding.shape
    block = D // devices
    hidden = FF // devices
    pas_count, pas_len = passage_ids.shape
    qry_count, qry_len = query_ids.shape
    rows = pas_count + qry_count
    tokens = pas_count * pas_len + qry_count * qry_len
    chunks = tokens // LANES
    half = -(-half_rows // (2 * LANES)) * LANES
    where = jnp.stack([group, device]).astype(jnp.int32)
    place_at = place.astype(jnp.int32)[None]
    lines = wide * ROWS

    seq_np = np.concatenate([np.repeat(np.arange(pas_count), pas_len), pas_count + np.repeat(np.arange(qry_count), qry_len)])
    pos_np = np.concatenate([np.tile(np.arange(pas_len), pas_count), np.tile(np.arange(qry_len), qry_count)])
    vec_lines = -(-vectors.shape[0] // LANES)
    packet_lines = -(-(2 * chunks + 1 + vec_lines) // ROWS) * ROWS
    note = [valid.astype(f32), positive.astype(f32), negatives.astype(f32).reshape(-1)]
    note_size = sum(t.shape[0] for t in note)
    assert 1 + note_size <= LANES
    pieces = [passage_ids.astype(f32).reshape(-1), query_ids.astype(f32).reshape(-1)]
    pieces += [jnp.repeat(passage_len.astype(f32), pas_len), jnp.repeat(query_len.astype(f32), qry_len)]
    pieces += [jnp.zeros((1,), f32)] + note + [jnp.zeros((LANES - 1 - note_size,), f32), vectors]
    pieces.append(jnp.zeros((packet_lines * LANES - sum(t.shape[0] for t in pieces),), f32))
    packet, moved = call(
        partial(prepare_kernel, half_rows, tokens),
        [shape((wide, packet_lines, LANES)), shape((ROWS, tokens))],
        jnp.concatenate(pieces).reshape(packet_lines, LANES), jnp.asarray(seq_np, jnp.int32)[None], jnp.asarray(pos_np, jnp.int32)[None],
        near_outs=(0,), name="prepare",
    )
    packet_own = exchange(packet)
    (table,) = call(build_kernel, [shape((half, LANES))], embedding, name="build", flops=10**8)
    packet_own, table = tie(packet_own, table)
    packet_other = swap(packet_own)
    (low_mats,) = call(cast_kernel, [shape((block, 5 * D), bf16)], attn_in, attn_out, head, near_outs=(0,), name="cast")
    mats = lax.all_gather(low_mats, ALL, axis=0, tiled=True)
    w_ffn_up, w_ffn_down, _ = tie(w_ffn_up, w_ffn_down, packet)
    w_up = lax.all_to_all(
        w_ffn_up.astype(bf16).reshape(block, devices, hidden).transpose(1, 0, 2), ALL, split_axis=0, concat_axis=0, tiled=True
    ).reshape(D, hidden)
    w_down = w_ffn_down.astype(bf16)

    def numbers_of(packets):
        local = packets[:, :chunks] - (group * half_rows).astype(f32)
        row_at = jnp.clip(jnp.where(local >= half, local - half, local), 0, half - 1)
        return row_at.astype(jnp.int32).reshape(-1), packets[:, 2 * chunks, 0].astype(jnp.int32)

    look = partial(lookup, half_rows=half_rows, feats=feats, count=tokens)
    num_own, num_other = numbers_of(packet_own), numbers_of(packet_other)
    theirs = look(where, *num_other, packet_other, table)
    xt = exchange(look(where, *num_own, packet_own, table, add=swap(theirs))).reshape(D, tokens)
    numbers = jnp.concatenate([num_own[0], num_other[0]])
    firsts = jnp.concatenate([num_own[1], num_other[1]])
    packets = jnp.concatenate([packet_own, packet_other], 0)

    vec = in_order(packet_own, packet_other, group)[:, 2 * chunks + 1 : 2 * chunks + 1 + vec_lines].reshape(devices, -1)
    vec = vec[:, : vectors.shape[0]].reshape(-1, D)
    bias_up = lax.dynamic_slice(vec.reshape(-1), (11 * D + device * hidden,), (hidden,))[None]
    notes = packets[:, 2 * chunks]
    valid_rows = jnp.pad(notes[:, 1 : 1 + qry_count], ((0, 0), (pas_count, ROWS - rows))).reshape(-1, 1)
    at = 1 + qry_count
    picked = jnp.concatenate(
        [notes[:, at : at + qry_count, None], notes[:, at + qry_count : at + qry_count + negatives.size].reshape(devices, qry_count, -1)], 2
    ).astype(jnp.int32)
    pick_dev = picked // pas_count
    pick_row = (((pick_dev // wide) ^ group) * wide + pick_dev % wide) * ROWS + picked % pas_count
    pick_rows = jnp.pad(pick_row, ((0, 0), (pas_count, ROWS - rows), (0, 0)), constant_values=-1).reshape(devices * ROWS, -1)

    xt, vec, bias_up, valid_rows, pick_rows, w_up, w_down, packets, numbers, firsts = tie(
        xt, vec, bias_up, valid_rows, pick_rows, w_up, w_down, packets, numbers, firsts
    )
    tile_lines = ROWS * (D // LANES)
    sent, p_heads, facts, probs, psum, normed1, inv1 = call(
        partial(attend_kernel, rows),
        [
            shape((wide, tile_lines + 2 * block, LANES), bf16), shape((16 * chunks, LANES), bf16),
            shape((3 * tile_lines, LANES), bf16),
            shape((SIDE, tokens)), shape((SIDE, 1)), shape((ROWS, D)), shape((ROWS, 1)),
        ],
        xt, vec, moved,
        far=(mats,), near=(0,), near_outs=(0,), scratch=weight_scratch(4), name="attend", flops=10**9,
    )
    x_own, x_other = pair(sent)
    u, h, f_mine, f_theirs = call(
        ffn_kernel,
        [shape((devices * ROWS, hidden)), shape((devices * ROWS, hidden), bf16), shape((lines, D)), shape((lines, D), bf16)],
        x_own, x_other, w_up, w_down, bias_up,
        near=(0, 1), near_outs=(2, 3), name="ffn", flops=10**8, vmem=16,
    )
    f_parts = exchange((f_mine + swap(f_theirs)).astype(bf16).reshape(wide, ROWS, D))
    (f_sum,) = call(
        total_kernel, [shape((wide, tile_lines + 16 * chunks, LANES), bf16)], f_parts, p_heads, near=(0,), near_outs=(0,), name="total"
    )
    f_own, f_other = pair(f_sum)
    loss, pooled, d_c, d_res2, d_f, d_u, d_mine, d_theirs, sums, sums_up = call(
        middle_kernel,
        [
            shape((1, 1)), shape((devices * ROWS, D), bf16), shape((devices * ROWS, D), bf16), shape((devices * ROWS, D)),
            shape((devices * ROWS, D), bf16), shape((devices * ROWS, hidden), bf16), shape((lines, D)), shape((lines, D), bf16),
            shape((ROWS, D)), shape((1, D)),
        ],
        x_own, x_other, f_own, f_other, u, w_up, w_down, vec, pick_rows, valid_rows,
        far=(mats,), scratch=weight_scratch(1), near=(0, 1, 2, 3), near_outs=(6, 7), name="middle", flops=10**9, vmem=32,
    )
    d_sum = (d_mine + swap(d_theirs)).astype(bf16).reshape(wide, ROWS, D)
    got = exchange(d_sum)
    (d_up,) = call(up_grad_kernel, [shape((D, hidden), bf16)], x_own, x_other, d_u, after=(d_sum,), near=(0, 1), name="up_grad", flops=10**8)
    late, last = call(
        partial(attend_back_kernel, rows),
        [shape((wide, 2 * block + 16 * chunks, LANES), bf16), shape((4 * tile_lines, LANES), bf16)],
        got, d_res2, sums_up, normed1, inv1, probs, psum, xt, vec,
        scalars=(place_at,), far=(mats,), near=(0,), near_outs=(0,), scratch=weight_scratch(4), name="attend_back", flops=10**9,
    )
    late_own, late_other = pair(late)
    d_down, d_whead = call(
        ffn_grads_kernel, [shape((hidden, D)), shape((block, D))], h, d_f, pooled, d_c,
        scalars=(where,), after=(late,), name="ffn_grads", flops=10**8,
    )
    (packed,) = call(
        pack_kernel, [shape((wide, 7 * tile_lines + 2 * block, LANES), bf16)], facts, last, d_up, after=(late_own,), near_outs=(0,), name="pack",
    )
    last_own = exchange(packed)
    d_table, square = spread_tokens(
        where, numbers, firsts, packets, (x_own, x_other), (late_own, late_other), (f_own, f_other), tile_lines, rows, half_rows, feats, tokens
    )
    last_own = last_own + (square[0, 0] * 0.0).astype(bf16)
    last_other = swap(last_own)
    d_attn_in, d_wo, d_wup, d_vec, squares = call(
        partial(grads_kernel, rows, tile_lines),
        [shape((block, 3 * D)), shape((block, D)), shape((block, FF)), shape((16, D)), shape((wide, ROWS, LANES))],
        x_own, x_other, late_own, late_other, last_own, last_other, d_whead, d_down, sums, square,
        scalars=(where,),
        scratch=[pltpu.VMEM((devices * ROWS, D), f32)] * 6 + [pltpu.VMEM((D, LANES), f32)] * 2 + [pltpu.VMEM((D, D), f32)],
        near=(4, 5), near_outs=(4,), name="grads", flops=10**9, vmem=32,
    )
    squares_own, squares_other = pair(squares)
    d_vectors = lax.dynamic_slice(d_vec.reshape(-1), (device * vectors.shape[0],), vectors.shape)
    step_float = step_count[0].astype(f32)
    scales = jnp.stack([1.0 / (1.0 - jnp.power(0.9, step_float)), 1.0 / (1.0 - jnp.power(0.999, step_float))])
    grads = (d_attn_in, d_wo, d_wup, d_down, d_whead)
    middle_state = state[3:18]
    slots, step_rows = 3, ROWS
    norm, factor, *new = call(
        partial(adam_kernel, len(grads)),
        [shape((1, 1)), shape((1, 1))] + [shape(t.shape) for t in middle_state],
        squares_own, squares_other, *grads, *middle_state,
        scalars=(scales,), far=(*state[:3], d_table), far_outs=[shape(embedding.shape)] * 3,
        scratch=[
            pltpu.VMEM((slots, 4, step_rows, half_rows), f32), pltpu.VMEM((slots, 3, step_rows, half_rows), f32),
            pltpu.SemaphoreType.DMA((slots, 4)), pltpu.SemaphoreType.DMA((slots, 3)),
        ],
        near=(0, 1), name="adam", vmem=40,
    )
    new_vectors = update(*state[18:], d_vectors * factor[0, 0], RATES[6], scales[0], scales[1])
    return (loss[0, 0], norm[0, 0]) + tuple(new[15:]) + tuple(new[:15]) + new_vectors


def solution(mesh):
    split_rows = P(ALL, None)
    flat = P(ALL)
    table = P("wide", "group")
    mats = (table,) * 3 + (split_rows,) * 15 + (flat,) * 3
    in_specs = (split_rows, split_rows, flat, flat, flat, split_rows, flat, P()) + mats
    wide = mesh.shape["wide"]
    thick = D % (2 * wide * ROWS) == 0 and wide * ROWS <= LANES
    return jax.shard_map(
        partial(body if thick else plain_body, wide), mesh=mesh, in_specs=in_specs, out_specs=(P(), P()) + mats, check_vma=False
    )
```

profile of v0, /device:TPU:0, one launch (start us, length us, event | category | flops | bytes accessed | tf_op | source)
XLA Modules:
  0.0 322.8 jit_solution(8692461051372403626)
XLA Ops:
  7.2 1.7 cast.1
  9.6 0.7 convert_element_type.86
  10.3 0.7 convert_element_type.88
  10.9 0.7 convert_element_type.87
  11.8 0.7 convert_element_type.82
  12.4 0.7 convert_element_type.83
  13.2 0.7 convert_element_type.89
  14.0 1.4 concatenate.19
  15.3 2.2 prepare.1
  17.6 8.3 %all-to-all-start = ((f32[16,16,128]{2,1,0:T(8,128)}), f32[16,16,128]{2,1,0:T(8,128)S(1)}, u32[]{:S(2)}, u32[]{:S(2)}) async-start(f32[16,16,128]{2,1,0:T(8,128)} %get-tuple-element.91), calls=%async_computation | async-start | bytes 262144 | tf_op jit(solution)/shard_map/all_to_all | solution.py:790
  25.9 7.0 %build.1.table = f32[12672,128]{1,0:T(8,128)} custom-call(f32[48,25216]{1,0:T(8,128)} %refs_1_.3), custom_call_target="tpu_custom_call" | custom-call | flops 100000000 | bytes 11329536 | tf_op jit(solution)/shard_map/build/pallas_call | solution.py:294
  32.9 1.9 all-to-all-done.packet
  34.8 1.3 collective-permute-done.packet
  36.1 0.4 fusion.14.firsts
  36.5 11.8 %lookup.1 = bf16[16,48,640]{2,1,0:T(8,128)(2,1)S(1)} custom-call(s32[2]{0:T(128)S(1)} %pad_add_fusion.1.where.refs_0_, s32[10240]{0:T(1024)S(1)} %reshape.131.numbers, s32[16]{0:T(128)S(1)} %fusion.14.firsts, f32[16,16,128]{2,1,0:T(8,128)S(1)} %collective-permute-done.packet, f32[12672,128]{1,0:T(8,128)} %build.1.table), custom_call_target="tpu_custom_call" | custom-call | flops 1000000000 | bytes 10000000 | tf_op jit(solution)/shard_map/lookup/pallas_call | solution.py:425
  48.3 0.9 collective-permute-start.1
  49.2 0.2 reshape.138
  49.4 0.8 copy.70
  50.2 4.0 %all-to-all-start.2 = ((bf16[32,24,96]{2,1,0:T(8,128)(2,1)}), bf16[32,24,96]{2,1,0:T(8,128)(2,1)S(1)}, u32[]{:S(2)}, u32[]{:S(2)}) async-start(bf16[32,24,96]{2,1,0:T(8,128)(2,1)} %bitcast.32), calls=%async_computation.2 | async-start | bytes 393216 | tf_op jit(solution)/shard_map/all_to_all | solution.py:952
  54.3 0.4 convert_reduce_fusion.firsts
  54.7 12.7 %lookup_add.1 = bf16[16,48,640]{2,1,0:T(8,128)(2,1)} custom-call(s32[2]{0:T(128)S(1)} %pad_add_fusion.1.where.refs_0_, s32[10240]{0:T(1024)S(1)} %reshape.130.numbers, s32[16]{0:T(128)S(1)} %convert_reduce_fusion.firsts, f32[16,16,128]{2,1,0:T(8,128)S(1)} %all-to-all-done.packet, f32[12672,128]{1,0:T(8,128)} %build.1.table, ...), custom_call_target="tpu_custom_call" | custom-call | flops 1000000000 | bytes 10000000 | tf_op jit(solution)/shard_map/lookup_add/pallas_call | solution.py:425
  67.4 6.8 %all-to-all-start.1 = ((bf16[16,48,640]{2,1,0:T(8,128)(2,1)}), bf16[16,48,640]{2,1,0:T(8,128)(2,1)S(1)}, u32[]{:S(2)}, u32[]{:S(2)}) async-start(bf16[16,48,640]{2,1,0:T(8,128)(2,1)} %lookup_add.1), calls=%async_computation.1 | async-start | bytes 1966080 | tf_op jit(solution)/shard_map/all_to_all | solution.py:790
  74.3 0.7 convert_element_type.99.refs_3_.refs_7_
  75.0 0.1 reshape_reshape.3
  75.2 0.7 reshape.134.refs_2_.refs_8_.refs_10_
  76.3 0.1 reshape.135
  76.6 0.6 dynamic-slice_bitcast_fusion.refs_4_
  77.2 0.7 pad_bitcast_fusion.refs_9_
  77.9 22.1 %all-to-all-done.1 = bf16[16,48,640]{2,1,0:T(8,128)(2,1)S(1)} async-done(((bf16[16,48,640]{2,1,0:T(8,128)(2,1)}), bf16[16,48,640]{2,1,0:T(8,128)(2,1)S(1)}, u32[]{:S(2)}, u32[]{:S(2)}) %all-to-all-start.1) | async-done | bytes 983072 | tf_op jit(solution)/shard_map/all_to_all | solution.py:790
  100.0 6.3 %attend.1 = (bf16[16,96,128]{2,1,0:T(8,128)(2,1)S(1)}, bf16[80,128]{1,0:T(8,128)(2,1)}, bf16[144,128]{1,0:T(8,128)(2,1)}, f32[64,640]{1,0:T(8,128)}, f32[64,1]{1...) custom-call(bf16[768,3840]{1,0:T(8,128)(2,1)} %all-gather.2.cloned.1.call-done.refs_0_.refs_1_, ...), custom_call_target="tpu_custom_call" | custom-call | flops 1000000000 | bytes 7587104 | tf_op jit(solution)/shard_map/attend/pallas_call | solution.py:294
  106.3 20.5 %all_to_all.50.refs_0_.refs_1_.early_own = bf16[16,96,128]{2,1,0:T(8,128)(2,1)S(1)} all-to-all(bf16[16,96,128]{2,1,0:T(8,128)(2,1)S(1)} %get-tuple-element.99), channel_id=1, replica_groups=mesh['group'=2,'wide'=16] {'wide'}, dimensions={0} | all-to-all | bytes 786432 | tf_op jit(solution)/shard_map/all_to_all | solution.py:790
  126.8 1.7 collective-permute-done.2.refs_1_.refs_2_.early_other
  128.5 2.1 ffn.1
  130.6 0.1 collective-permute-start.3
  130.8 1.3 collective-permute-done.3
  132.1 12.4 %all_to_all.51.refs_0_ = bf16[16,8,768]{2,1,0:T(8,128)(2,1)S(1)} all-to-all(bf16[16,8,768]{2,1,0:T(8,128)(2,1)S(1)} %fusion), channel_id=1, replica_groups=mesh['group'=2,'wide'=16] {'wide'}, dimensions={0} | all-to-all | bytes 393216 | tf_op jit(solution)/shard_map/all_to_all | solution.py:790
  144.5 0.8 total.1
  145.3 17.9 %all_to_all.52.refs_3_.p_own = bf16[16,128,128]{2,1,0:T(8,128)(2,1)S(1)} all-to-all(bf16[16,128,128]{2,1,0:T(8,128)(2,1)S(1)} %total.1), channel_id=1, replica_groups=mesh['group'=2,'wide'=16] {'wide'}, dimensions={0} | all-to-all | bytes 1048576 | tf_op jit(solution)/shard_map/all_to_all | solution.py:790
  163.2 0.8 copy.63.refs_10_
  164.0 1.1 collective-permute-done.4.refs_4_.p_other
  165.1 7.2 %middle.1 = (f32[1,1]{1,0:T(1,128)}, bf16[256,768]{1,0:T(8,128)(2,1)}, bf16[256,768]{1,0:T(8,128)(2,1)}, f32[256,768]{1,0:T(8,128)}, bf16[256,768]{1,0:T(8,128)(...) custom-call(bf16[768,3840]{1,0:T(8,128)(2,1)} %all-gather.2.cloned.1, ...), custom_call_target="tpu_custom_call" | custom-call | flops 1000000000 | bytes 10814468 | tf_op jit(solution)/shard_map/middle/pallas_call | solution.py:294
  172.3 0.2 collective-permute-start.5
  172.5 1.3 collective-permute-done.5
  173.9 12.8 %all_to_all.53.refs_2_ = bf16[16,8,768]{2,1,0:T(8,128)(2,1)S(1)} all-to-all(bf16[16,8,768]{2,1,0:T(8,128)(2,1)S(1)} %fusion.1.refs_3_), channel_id=1, replica_groups=mesh['group'=2,'wide'=16] {'wide'}, dimensions={0} | all-to-all | bytes 393216 | tf_op jit(solution)/shard_map/all_to_all | solution.py:790
  186.7 7.2 %attend_back.1 = (bf16[16,128,128]{2,1,0:T(8,128)(2,1)}, bf16[192,128]{1,0:T(8,128)(2,1)}) custom-call(s32[1]{0:T(128)} %bitcast.14.refs_0_, bf16[768,3840]{1,0:T(8,128)(2,1)} %all-gather.2.cloned.1.call-done.refs_0_.refs_1_, bf16[16,8,768]{2,1,0:T(8,128)(2,1)S(1)} %all_to_all.53.refs_2_, f32[256,768]{1,0:T(8,128)} %get-tuple-element.115.refs_3_, ...), custom_call_target="tpu_custom_call" | custom-call | flops 1000000000 | bytes 8675616 | tf_op jit(solution)/shard_map/attend_back/pallas_call | solution.py:294
  193.9 3.7 %all-to-all-start.7 = ((bf16[16,128,128]{2,1,0:T(8,128)(2,1)}), bf16[16,128,128]{2,1,0:T(8,128)(2,1)S(1)}, u32[]{:S(2)}, u32[]{:S(2)}) async-start(bf16[16,128,128]{2,1,0:T(8,128)(2,1)} %get-tuple-element.121.refs_5_), calls=%async_computation.7 | async-start | bytes 1048576 | tf_op jit(solution)/shard_map/all_to_all | solution.py:790
  197.6 1.8 up_grad.1.refs_2_
  199.4 12.7 %all-to-all-done.7.late_own.refs_3_ = bf16[16,128,128]{2,1,0:T(8,128)(2,1)S(1)} async-done(((bf16[16,128,128]{2,1,0:T(8,128)(2,1)}), bf16[16,128,128]{2,1,0:T(8,128)(2,1)S(1)}, u32[]{:S(2)}, u32[]{:S(2)}) %all-to-all-start.7) | async-done | bytes 524320 | tf_op jit(solution)/shard_map/all_to_all | solution.py:790
  212.2 2.6 pack.1
  214.8 4.4 %all-to-all-start.8 = ((bf16[16,384,128]{2,1,0:T(8,128)(2,1)}), bf16[16,384,128]{2,1,0:T(8,128)(2,1)}, u32[]{:S(2)}, u32[]{:S(2)}) async-start(bf16[16,384,128]{2,1,0:T(8,128)(2,1)} %pack.1), calls=%async_computation.8 | async-start | bytes 3145728 | tf_op jit(solution)/shard_map/all_to_all | solution.py:790
  219.2 1.9 collective-permute-done.6.late_other.refs_4_
  221.2 45.7 %spread_tokens.1 = (f32[48,25216]{1,0:T(8,128)}, f32[8,128]{1,0:T(8,128)}) custom-call(s32[2]{0:T(128)S(1)} %pad_add_fusion.1.where.refs_0_, s32[20480]{0:T(1024)S(1)} %pad_add_fusion.numbers, s32[32]{0:T(128)S(1)} %pad_add_fusion.2.firsts, f32[32,16,128]{2,1,0:T(8,128)S(1)} %copy-done.6, bf16[16,96,128]{2,1,0:T(8,128)(2,1)S(1)} %all_to_all.50.refs_0_.refs_1_.early_own, ...), custom_call_target="tpu_custom_call" | custom-call | flops 1000000000 | bytes 30000000 | tf_op jit(solution)/shard_map/spread_tokens/pallas_call | solution.py:539
  266.8 1.2 slice.43
  268.7 1.5 broadcast_add_fusion.refs_5_
  270.2 1.9 collective-permute-start.7
  272.1 2.5 ffn_grads.1
  274.6 0.6 collective-permute-done.7.refs_6_
  275.1 8.5 %grads.1 = (f32[24,2304]{1,0:T(8,128)}, f32[24,768]{1,0:T(8,128)}, f32[24,3072]{1,0:T(8,128)}, f32[16,768]{1,0:T(8,128)}, f32[16,8,128]{2,1,0:T(8,128)}) custom-call(s32[2]{0:T(128)S(1)} %pad_add_fusion.1.where.refs_0_, bf16[16,96,128]{2,1,0:T(8,128)(2,1)} %copy-done, bf16[16,96,128]{2,1,0:T(8,128)(2,1)} %copy-done.2, bf16[16,128,128]{2,1,0:T(8,128)(2,1)} %copy-done.3, ...), custom_call_target="tpu_custom_call" | custom-call | flops 1000000000 | bytes 6082560 | tf_op jit(solution)/shard_map/grads/pallas_call | solution.py:294
  283.7 6.8 %all-to-all-start.9 = ((f32[16,8,128]{2,1,0:T(8,128)}), f32[16,8,128]{2,1,0:T(8,128)S(1)}, u32[]{:S(2)}, u32[]{:S(2)}) async-start(f32[16,8,128]{2,1,0:T(8,128)} %get-tuple-element.134), calls=%async_computation.9 | async-start | bytes 131072 | tf_op jit(solution)/shard_map/all_to_all | solution.py:790
  291.3 6.7 %all-to-all-done.9.refs_5_ = f32[16,8,128]{2,1,0:T(8,128)S(1)} async-done(((f32[16,8,128]{2,1,0:T(8,128)}), f32[16,8,128]{2,1,0:T(8,128)S(1)}, u32[]{:S(2)}, u32[]{:S(2)}) %all-to-all-start.9) | async-done | bytes 65568 | tf_op jit(solution)/shard_map/all_to_all | solution.py:790
  298.1 0.8 reshape.142
  298.9 0.4 collective-permute-done.8.refs_6_
  299.3 15.4 %adam.1 = (f32[1,1]{1,0:T(1,128)}, f32[1,1]{1,0:T(1,128)}, f32[24,2304]{1,0:T(8,128)}, f32[24,2304]{1,0:T(8,128)}, f32[24,2304]{1,0:T(8,128)}, /*index=5*/f32[24...) custom-call(f32[2]{0:T(128)S(1)} %pad_maximum_fusion.1.refs_0_, ...), custom_call_target="tpu_custom_call" | custom-call | bytes 40730632 | tf_op jit(solution)/shard_map/adam/pallas_call | solution.py:294
  314.7 1.3 multiply_subtract_fusion
  (68 shorter events, 1.5 us)
Async XLA Ops:
  7.2 92.8 %all-gather.2.cloned.1.call-start = ((), (), s32[]{:S(2)}) async-start(), calls=%async_computation.10 | async-start | bytes 6082560 | tf_op jit(solution)/shard_map/all_gather | solution.py:950
  17.6 17.2 %all-to-all-start = ((f32[16,16,128]{2,1,0:T(8,128)}), f32[16,16,128]{2,1,0:T(8,128)S(1)}, u32[]{:S(2)}, u32[]{:S(2)}) async-start(f32[16,16,128]{2,1,0:T(8,128)} %get-tuple-element.91), calls=%async_computation | async-start | bytes 262144 | tf_op jit(solution)/shard_map/all_to_all | solution.py:790
  32.9 16.4 %copy-start.8 = (f32[24,3072]{1,0:T(8,128)S(1)}, f32[24,3072]{1,0:T(8,128)}, u32[]{:S(2)}) copy-start(f32[24,3072]{1,0:T(8,128)} %refs_18_.1) | copy-start | bytes 884740
  34.7 1.3 collective-permute-start
  48.3 6.3 %collective-permute-start.1 = (bf16[16,48,640]{2,1,0:T(8,128)(2,1)S(1)}, bf16[16,48,640]{2,1,0:T(8,128)(2,1)S(1)}, u32[]{:S(2)}, u32[]{:S(2)}) collective-permute-start(bf16[16,48,640]{2,1,0:T(8,128)(2,1)S(1)} %lookup.1), channel_id=1, source_target_pairs={{0,16},{16,0},{1,17},{17,1},{2,18},{18,2},{3,19},{19,3},{4,20},{20... | collective-permute-start | bytes 2949128 | tf_op jit(solution)/shard_map/ppermute | solution.py:786
  50.2 17.2 %all-to-all-start.2 = ((bf16[32,24,96]{2,1,0:T(8,128)(2,1)}), bf16[32,24,96]{2,1,0:T(8,128)(2,1)S(1)}, u32[]{:S(2)}, u32[]{:S(2)}) async-start(bf16[32,24,96]{2,1,0:T(8,128)(2,1)} %bitcast.32), calls=%async_computation.2 | async-start | bytes 393216 | tf_op jit(solution)/shard_map/all_to_all | solution.py:952
  54.7 19.6 %copy-start.9 = (f32[96,768]{1,0:T(8,128)S(1)}, f32[96,768]{1,0:T(8,128)}, u32[]{:S(2)}) copy-start(f32[96,768]{1,0:T(8,128)} %refs_21_.1) | copy-start | bytes 884740
  67.4 38.9 %copy-start.7 = (bf16[32,24,96]{2,1,0:T(8,128)(2,1)}, bf16[32,24,96]{2,1,0:T(8,128)(2,1)S(1)}, u32[]{:S(2)}) copy-start(bf16[32,24,96]{2,1,0:T(8,128)(2,1)S(1)} %all-to-all-done.2) | copy-start | bytes 442372
  67.4 32.6 %all-to-all-start.1 = ((bf16[16,48,640]{2,1,0:T(8,128)(2,1)}), bf16[16,48,640]{2,1,0:T(8,128)(2,1)S(1)}, u32[]{:S(2)}, u32[]{:S(2)}) async-start(bf16[16,48,640]{2,1,0:T(8,128)(2,1)} %lookup_add.1), calls=%async_computation.1 | async-start | bytes 1966080 | tf_op jit(solution)/shard_map/all_to_all | solution.py:790
  75.0 31.3 %copy-start.5 = (f32[32,16,128]{2,1,0:T(8,128)}, f32[32,16,128]{2,1,0:T(8,128)S(1)}, u32[]{:S(2)}) copy-start(f32[32,16,128]{2,1,0:T(8,128)S(1)} %constant_dynamic-update-slice_fusion.packet) | copy-start | bytes 786436
  99.9 44.6 %copy-start.1 = (bf16[16,48,640]{2,1,0:T(8,128)(2,1)}, bf16[16,48,640]{2,1,0:T(8,128)(2,1)S(1)}, u32[]{:S(2)}) copy-start(bf16[16,48,640]{2,1,0:T(8,128)(2,1)S(1)} %all-to-all-done.1) | copy-start | bytes 2949124
  126.8 94.3 %copy-start = (bf16[16,96,128]{2,1,0:T(8,128)(2,1)}, bf16[16,96,128]{2,1,0:T(8,128)(2,1)S(1)}, u32[]{:S(2)}) copy-start(bf16[16,96,128]{2,1,0:T(8,128)(2,1)S(1)} %all_to_all.50.refs_0_.refs_1_.early_own) | copy-start | bytes 1179652
  126.8 1.7 collective-permute-start.2
  128.5 92.6 %copy-start.2 = (bf16[16,96,128]{2,1,0:T(8,128)(2,1)}, bf16[16,96,128]{2,1,0:T(8,128)(2,1)S(1)}, u32[]{:S(2)}) copy-start(bf16[16,96,128]{2,1,0:T(8,128)(2,1)S(1)} %collective-permute-done.2.refs_1_.refs_2_.early_other) | copy-start | bytes 1179652
  130.6 1.4 collective-permute-start.3
  163.2 1.9 collective-permute-start.4
  172.3 1.5 collective-permute-start.5
  193.9 27.3 %copy-start.6 = (f32[32,16,128]{2,1,0:T(8,128)S(1)}, f32[32,16,128]{2,1,0:T(8,128)}, u32[]{:S(2)}) copy-start(f32[32,16,128]{2,1,0:T(8,128)} %copy-done.5) | copy-start | bytes 786436
  193.9 18.3 %all-to-all-start.7 = ((bf16[16,128,128]{2,1,0:T(8,128)(2,1)}), bf16[16,128,128]{2,1,0:T(8,128)(2,1)S(1)}, u32[]{:S(2)}, u32[]{:S(2)}) async-start(bf16[16,128,128]{2,1,0:T(8,128)(2,1)} %get-tuple-element.121.refs_5_), calls=%async_computation.7 | async-start | bytes 1048576 | tf_op jit(solution)/shard_map/all_to_all | solution.py:790
  212.2 58.0 %copy-start.3 = (bf16[16,128,128]{2,1,0:T(8,128)(2,1)}, bf16[16,128,128]{2,1,0:T(8,128)(2,1)S(1)}, u32[]{:S(2)}) copy-start(bf16[16,128,128]{2,1,0:T(8,128)(2,1)S(1)} %all-to-all-done.7.late_own.refs_3_) | copy-start | bytes 1572868
  214.8 53.9 %all-to-all-start.8 = ((bf16[16,384,128]{2,1,0:T(8,128)(2,1)}), bf16[16,384,128]{2,1,0:T(8,128)(2,1)}, u32[]{:S(2)}, u32[]{:S(2)}) async-start(bf16[16,384,128]{2,1,0:T(8,128)(2,1)} %pack.1), calls=%async_computation.8 | async-start | bytes 3145728 | tf_op jit(solution)/shard_map/all_to_all | solution.py:790
  219.2 2.0 collective-permute-start.6
  221.1 54.0 %copy-start.4 = (bf16[16,128,128]{2,1,0:T(8,128)(2,1)}, bf16[16,128,128]{2,1,0:T(8,128)(2,1)S(1)}, u32[]{:S(2)}) copy-start(bf16[16,128,128]{2,1,0:T(8,128)(2,1)S(1)} %collective-permute-done.6.late_other.refs_4_) | copy-start | bytes 1572868
  270.2 4.9 %collective-permute-start.7 = (bf16[16,384,128]{2,1,0:T(8,128)(2,1)S(1)}, bf16[16,384,128]{2,1,0:T(8,128)(2,1)S(1)}, u32[]{:S(2)}, u32[]{:S(2)}) collective-permute-start(bf16[16,384,128]{2,1,0:T(8,128)(2,1)S(1)} %broadcast_add_fusion.refs_5_), channel_id=1, source_target_pairs={{0,16},{16,0},{1,17},{17,1},{2,18},{18,2},{3,19},{19,3},{4,20},{20... | collective-permute-start | bytes 4718600 | tf_op jit(solution)/shard_map/ppermute | solution.py:786
  283.7 14.3 %all-to-all-start.9 = ((f32[16,8,128]{2,1,0:T(8,128)}), f32[16,8,128]{2,1,0:T(8,128)S(1)}, u32[]{:S(2)}, u32[]{:S(2)}) async-start(f32[16,8,128]{2,1,0:T(8,128)} %get-tuple-element.134), calls=%async_computation.9 | async-start | bytes 131072 | tf_op jit(solution)/shard_map/all_to_all | solution.py:790
  298.0 1.3 collective-permute-start.8
  299.2 15.4 %copy-start.10 = (f32[360]{0:T(512)S(1)}, f32[360]{0:T(512)}, u32[]{:S(2)}) copy-start(f32[360]{0:T(512)} %param.57) | copy-start | bytes 4324
  299.2 15.4 %copy-start.11 = (f32[360]{0:T(512)S(1)}, f32[360]{0:T(512)}, u32[]{:S(2)}) copy-start(f32[360]{0:T(512)} %param.58) | copy-start | bytes 4324
  299.2 15.4 %copy-start.12 = (f32[360]{0:T(512)S(1)}, f32[360]{0:T(512)}, u32[]{:S(2)}) copy-start(f32[360]{0:T(512)} %param.59) | copy-start | bytes 4324
Sparse Core Ops, SparseCore 0:
  11.5 79.5 all-gather.1
where the time goes:
time: 325 us; the launch traced here: 323 us
  Pallas kernels  135 us (42%)
  blocking collectives  63.6 us (20%)
  waiting for transfers between devices  53 us (16%)
  starting transfers between devices  37.3 us (11%)
  between operations  16.5 us (5%)
  other arithmetic  8.66 us (3%)
  local copies, waits for them, and re-layouts  8.21 us (3%)
    pallas_call x13, Pallas kernels, call(): pl.pallas_call(run, grid=(1,), out_shape=shapes, in_specs=in_specs, out_s...  65.3 us
    all_to_all x4, blocking collectives, exchange(): return lax.all_to_all(x, 'wide', split_axis=0, concat_axis=0, tiled=True)  63.6 us
    pallas_call x1, Pallas kernels, spread_tokens(): pl.pallas_call(partial(spread_kernel, rows, half_rows, feats, per, unroll...  45.7 us
    all_to_all x5, waiting for transfers between devices, exchange(): return lax.all_to_all(x, 'wide', split_axis=0, concat_axis=0, tiled=True)  43.4 us
    all_to_all x5, starting transfers between devices, exchange(): return lax.all_to_all(x, 'wide', split_axis=0, concat_axis=0, tiled=True)  30.1 us
    pallas_call x2, Pallas kernels, lookup(): pl.pallas_call(partial(lookup_kernel, half_rows, per, unroll, add is not...  24.5 us
    ppermute x9, waiting for transfers between devices, swap(): return lax.ppermute(x, 'group', [(0, 1), (1, 0)])  9.55 us
  transfers between devices with their start and end apart: 16, of which 12 were waited for; matrix products, arithmetic and copies ran while one was open for 4% of the time, Pallas kernels for 26%

commit v1 on v0

--- a/solution.py
+++ b/solution.py
@@ -15,8 +15,7 @@
 ROWS = 8
 LANES = 128
 SIDE = 64
-Z_AT = 68
-KEEP = 24
+STEP = 16
 ALL = ("group", "wide")
 clip_level = 0.02
 f32 = jnp.float32
@@ -90,20 +89,17 @@
     return flag(head_of(iota((16, SIDE), 1), rows) == iota((16, SIDE), 0)).astype(bf16)
 
 
-def place_table(rows, first, count=None):
-    count = rows * HEADS if count is None else count
-    size = SIDE if count > ROWS else ROWS
-    a = iota((LANES, size), 1)
-    return flag((iota((LANES, size), 0) == first + a) & (a < count)).astype(bf16)
+def place_table(rows, first):
+    a = iota((LANES, SIDE), 1)
+    return flag((iota((LANES, SIDE), 0) == first + a) & (a < rows * HEADS)).astype(bf16)
 
 
 def expand_table(rows, first, r):
     return flag(iota((LANES, D), 0) == first + r * HEADS + lax.shift_right_logical(iota((LANES, D), 1), 6)).astype(bf16)
 
 
-def prepare(ids, lens, seq, pos, group_rows):
+def prepare(ids, live, seq, pos, group_rows):
     count = ids.shape[1]
-    live = flag(pos < lens)
     first = jnp.where(ids < group_rows, 1.0, 0.0)
     high = lax.shift_right_logical(ids, 8)
     index = iota((ROWS, count), 0)
@@ -144,8 +140,7 @@
     mixed = dot_split(y, w(2)) + psum * bv
     o = dot(spread, (mixed * columns).astype(bf16), 0, 0).astype(bf16)
     normed, inv = layer_norm(x00 + dot(o, w(3)) + bo)
-    p_heads = dot(heads_table(rows), probs_low).astype(bf16)
-    return normed * g1 + be1, x00.astype(bf16), q, o, probs, psum, normed, inv, qk, y, p_heads
+    return normed * g1 + be1, x00.astype(bf16), q, o, probs, psum, normed, inv, qk, y
 
 
 def attend_back(dx1, normed, inv, probs, psum, xt, w, vec, rows):
@@ -169,28 +164,51 @@
         jnp.sum(d_q.astype(f32), 0, keepdims=True),
         jnp.sum(d_o_wide * psum, 0, keepdims=True),
     ]
-    return d_a, d_o, d_q, sums, vd, z, extra, dot(heads_table(rows), ds).astype(bf16)
-
-
-def late_parts(vd, z, extra, rows):
-    by_table = dot(place_table(rows, 0), vd.astype(bf16)) + dot(place_table(rows, rows * HEADS, rows), extra.astype(bf16))
-    return by_table.T, dot(place_table(rows, Z_AT), z.astype(bf16)).T
-
-
-def early_parts(qk, y, rows):
-    return dot(place_table(rows, 0), qk).T, dot(place_table(rows, SIDE), y).T
-
-
-def block_of(parts, dest, wide):
-    by_table, by_rows = parts
-    block = D // (2 * wide)
-    return by_table[2 * block * dest : 2 * block * (dest + 1)] + jnp.concatenate(
-        [by_rows[block * dest : block * (dest + 1)], by_rows[block * (wide + dest) : block * (wide + dest + 1)]], 0
-    )
-
-
-def in_chunks(heads):
-    return jnp.concatenate([heads[:, k : k + LANES] for k in range(0, heads.shape[1], LANES)], 0)
+    return d_a, d_o, d_q, sums, vd, z, extra, ds
+
+
+def both_halves(value, rows):
+    low = value.astype(bf16)
+    return dot(place_table(rows, 0), low).T, dot(place_table(rows, SIDE), low).T
+
+
+def table_block(halves, dest, block):
+    first = 2 * block * dest
+    return halves[0][first : first + block] + halves[1][first + block : first + 2 * block]
+
+
+def weight_block(halves, dest, block, wide):
+    return halves[0][block * dest : block * (dest + 1)] + halves[1][block * (wide + dest) : block * (wide + dest + 1)]
+
+
+HEAD_LINES = 8
+
+
+def pack_heads(value, rows):
+    row, head = iota((HEAD_LINES, SIDE), 0), head_of(iota((HEAD_LINES, SIDE), 1), rows)
+    most = dot(flag(row == head).astype(bf16), value)
+    rest = [dot(flag((row - 4 * k + 8 == head) & (head >= 8) & (head < HEADS)).astype(bf16), value) for k in range(2)]
+    cut = lambda t, k: t[:, k * LANES : (k + 1) * LANES]
+    chunks = value.shape[1] // LANES
+    tiles = [cut(most, k) for k in range(chunks)]
+    for k in range(0, chunks, 2):
+        tiles.append(cut(rest[0], k) + cut(rest[1], k + 1) if k + 1 < chunks else cut(rest[0], k))
+    return jnp.concatenate(tiles, 0).astype(bf16)
+
+
+def unpack_heads(lines, chunks):
+    tile = lambda k: lines[k * HEAD_LINES : (k + 1) * HEAD_LINES].astype(f32)
+    most = jnp.concatenate([tile(k) for k in range(chunks)], 1)
+    rest = []
+    for k in range(chunks):
+        value = tile(chunks + k // 2)
+        rest.append(pltpu.roll(value, 4, 0) if k % 2 else value)
+    rest = jnp.concatenate(rest, 1)
+    return jnp.concatenate([most, jnp.where(iota(rest.shape, 0) < HEADS - 8, rest, 0.0)], 0)
+
+
+def head_lines(chunks):
+    return HEAD_LINES * (chunks + (chunks + 1) // 2)
 
 
 def to_tiles(value):
@@ -208,9 +226,10 @@
     return u, h, dot(h, w_down)
 
 
-def middle(x1, f, u, w_up, w_down, w, vec, picks, valid):
+def middle(x1, f, u, w_up, w_down, w, vec, picks):
     g2, gc, b2, be2, bc, bec = vec[1:2], vec[2:3], vec[7:8], vec[8:9], vec[9:10], vec[10:11]
     count = x1.shape[0]
+    valid, picks = picks[:, :1].astype(f32), picks[:, 1:]
     normed2, inv2 = layer_norm(x1 + (f + b2))
     pooled = (normed2 * g2 + be2).astype(bf16)
     normed_c, inv_c = layer_norm(dot(pooled, w(4)) + bc)
@@ -240,7 +259,8 @@
     d_x2 = dot(d_c, w(4), 1, 1)
     d_res2 = norm_back(d_x2, normed2, inv2, g2)
     d_f = d_res2.astype(bf16)
-    d_h = dot(d_f, w_down, 1, 1)
+    lines = u.shape[0]
+    d_h = dot(d_f[:lines], w_down, 1, 1)
     slope = 0.5 * (1.0 + lax.erf(u * 0.5**0.5)) + u * jnp.exp(-0.5 * u * u) * (2.0 * np.pi) ** (-0.5)
     d_u = (d_h * slope).astype(bf16)
     d_x1 = dot(d_u, w_up, 1, 1)
@@ -325,28 +345,39 @@
     return [pltpu.VMEM((count, D, D), bf16), pltpu.SemaphoreType.DMA((count,))]
 
 
-def prepare_kernel(group_rows, count, base, seq, pos, packet, moved):
+def prepare_kernel(group_rows, count, rows, base, vectors, seq, pos, up, packet, moved):
     chunks = count // LANES
-    line = lambda first: jnp.concatenate([base[first + k : first + k + 1, :] for k in range(chunks)], 1).astype(jnp.int32)
-    got, total = prepare(line(0), line(chunks), seq[...], pos[...], group_rows)
+    ids = jnp.concatenate([base[k : k + 1, :] for k in range(chunks)], 1)
+    entries = base[chunks : chunks + 1, :]
+    live = jnp.zeros((1, count), f32)
+    for number in range(rows):
+        live = jnp.where((seq[...] == number) & (pos[...] < entries[:, number : number + 1]), 1.0, live)
+    got, total = prepare(ids, live, seq[...], pos[...], group_rows)
     moved[...] = got
-    sent, code = got[0:1] * 256.0 + got[1:2], got[2:3] + 8.0 * got[3:4]
-    lines = [sent[:, k * LANES : (k + 1) * LANES] for k in range(chunks)]
-    lines += [code[:, k * LANES : (k + 1) * LANES] for k in range(chunks)]
-    whole = base[...]
-    index = iota(whole.shape, 0)
-    for number, value in enumerate(lines):
-        whole = jnp.where(index == number, value, whole)
-    whole = jnp.where((index == 2 * chunks) & (iota(whole.shape, 1) == 0), total, whole)
-    whole = jnp.where(index > 2 * chunks, whole.astype(bf16).astype(f32), whole)
-    for dest in range(packet.shape[0]):
-        packet[dest] = whole
-
-
-def cast_kernel(attn_in, attn_out, head, out):
+    code = got[2:3] + 8.0 * got[3:4]
+    lane = iota((1, LANES), 1)
+    note = pltpu.roll(entries.astype(f32), LANES - rows + 1, 1)
+    high = lax.shift_right_logical(total.astype(jnp.int32), 8)
+    note = jnp.where(lane == 0, total - 256.0 * high.astype(f32), jnp.where(lane == LANES - 1, high.astype(f32), note))
+    lines = [line[:, k * LANES : (k + 1) * LANES] for line in (got[0:1], got[1:2], code) for k in range(chunks)]
+    lines += [note] + [vectors[k : k + 1, :] for k in range(vectors.shape[0])]
+    wide, block = packet.shape[0], up.shape[0]
+    hidden = up.shape[1] // (2 * wide)
+    first = packet.shape[1] - 2 * block
+    index = iota((first, LANES), 0)
+    whole = jnp.zeros((first, LANES), f32)
+    for number, line in enumerate(lines):
+        whole = jnp.where(index == number, line, whole)
+    gap = jnp.zeros((block, LANES - hidden), f32)
+    for dest in range(wide):
+        pieces = [jnp.concatenate([up[:, n * hidden : (n + 1) * hidden], gap], 1) for n in (dest, wide + dest)]
+        packet[dest] = jnp.concatenate([whole] + pieces, 0).astype(bf16)
+
+
+def cast_kernel(attn_in, attn_out, head, out, head_out):
     out[:, : 3 * D] = attn_in[...].astype(bf16)
     out[:, 3 * D : 4 * D] = attn_out[...].astype(bf16)
-    out[:, 4 * D :] = head[...].astype(bf16)
+    head_out[...] = head[...].astype(bf16)
 
 
 def build_kernel(emb, table):
@@ -375,7 +406,8 @@
         build(jnp.int32(b), b < second)
 
 
-def side_of(ids, group, half_rows, half):
+def side_of(packet, s, chunks, group, half_rows, half):
+    ids = lanes_of(packet, s, 0, chunks) * 256.0 + lanes_of(packet, s, chunks, chunks)
     local = ids - (group * half_rows).astype(f32)
     inside = (local >= 0.0) & (local < float(half_rows))
     return jnp.where(inside, jnp.where(local >= float(half), 2.0, 1.0), 0.0)
@@ -385,7 +417,11 @@
     return jnp.where(group == 0, 0, first), jnp.where(group == 0, first, count)
 
 
-def lookup_kernel(half_rows, per, unroll, add, where, numbers, firsts, packet, table, *refs):
+def number_block(per, count):
+    return pl.BlockSpec((1, 1, per * count), lambda i, *s: (i, 0, 0), memory_space=pltpu.SMEM)
+
+
+def lookup_kernel(half_rows, per, unroll, add, where, firsts, numbers, packet, table, *refs):
     out, buf = refs[-2:]
     feats, count = out.shape[1:]
     group = where[0]
@@ -395,17 +431,16 @@
     at = pl.program_id(0) * per
     for s in range(per):
         low, high = own_span(firsts[at + s], group, count)
-        base = (at + s) * count
 
         def step(i, carry):
             for k in range(unroll):
                 t = i * unroll + k
-                buf[pl.ds(s * count + t, 1), :] = table[pl.ds(numbers[base + t], 1), :]
+                buf[pl.ds(s * count + t, 1), :] = table[pl.ds(numbers[0, 0, s * count + t], 1), :]
             return carry
 
         lax.fori_loop(low // unroll, (high + unroll - 1) // unroll, step, 0)
     for s in range(per):
-        side = side_of(lanes_of(packet, s, 0, chunks), group, half_rows, half)
+        side = side_of(packet, s, chunks, group, half_rows, half)
         turned = dot(eye, buf[s * count : (s + 1) * count, :].astype(bf16), 1, 1)
         pick = jnp.where(side > 1.5, turned[SIDE : SIDE + feats], turned[:feats])
         value = jnp.where(side > 0.5, pick, 0.0)
@@ -415,7 +450,7 @@
 
 
 def lanes_of(packet, s, first, chunks):
-    return jnp.concatenate([packet[s, first + c : first + c + 1, :] for c in range(chunks)], 1)
+    return jnp.concatenate([packet[s, first + c : first + c + 1, :].astype(f32) for c in range(chunks)], 1)
 
 
 def lookup(where, numbers, firsts, packets, table, half_rows, feats, count, add=None, per=4, unroll=32):
@@ -426,19 +461,19 @@
         partial(lookup_kernel, half_rows, per, unroll, add is not None),
         out_shape=shape((sources, feats, count), bf16),
         grid_spec=pltpu.PrefetchScalarGridSpec(
-            num_scalar_prefetch=3,
+            num_scalar_prefetch=2,
             grid=(sources // per,),
-            in_specs=[some(packets.shape[1:]), pl.BlockSpec(table.shape, lambda i, *s: (0, 0), pipeline_mode=pl.Buffered(1))] + [some((feats, count)) for _ in extra],
+            in_specs=[number_block(per, count), some(packets.shape[1:]), pl.BlockSpec(table.shape, lambda i, *s: (0, 0), pipeline_mode=pl.Buffered(1))] + [some((feats, count)) for _ in extra],
             out_specs=some((feats, count)),
             scratch_shapes=[pltpu.VMEM((per * count, LANES), f32)],
         ),
         compiler_params=pltpu.CompilerParams(vmem_limit_bytes=16 * MIB),
         cost_estimate=pl.CostEstimate(flops=10**9, bytes_accessed=10**7, transcendentals=0),
         name="lookup" if add is None else "lookup_add",
-    )(where, numbers, firsts, packets, pinned(table), *extra)
-
-
-def spread_kernel(rows, half_rows, feats, per, unroll, copies, at_early, at_heads, where, numbers, firsts, packet, early_own, early_other, late_own, late_other, p_own, p_other, out, square, *scratch):
+    )(where, firsts, numbers.reshape(-1, 1, per * count), packets, pinned(table), *extra)
+
+
+def spread_kernel(rows, half_rows, feats, per, unroll, copies, at_early, at_heads, where, firsts, numbers, packet, early_own, early_other, late_own, late_other, p_own, p_other, out, square, *scratch):
     parts, buf = scratch[:copies], scratch[copies]
     group = where[0]
     chunks = buf.shape[0] // (per * LANES)
@@ -457,52 +492,47 @@
 
         lax.fori_loop(0, blocks, clear, 0)
 
-    eye = jnp.where(iota((LANES, LANES), 0) == iota((LANES, LANES), 1), 1.0, 0.0).astype(bf16)
+    eye = flag(iota((LANES, LANES), 0) == iota((LANES, LANES), 1)).astype(bf16)
     gap = jnp.zeros((SIDE - feats, count), f32)
-    lane = iota((LANES, 16), 0)
-    low_heads = flag(head_of(lane, rows) == iota((LANES, 16), 1)).astype(bf16)
-    lane = iota((LANES, 1), 0)
-    seq_low = sequence_of(lane, rows).astype(f32)
-    seq_extra = jnp.where((lane >= rows * HEADS) & (lane < rows * HEADS + rows), lane - rows * HEADS, 99).astype(f32)
-
+    block = feats // 2
+    lane, slot = iota((LANES, 2 * LANES), 0), iota((LANES, 2 * LANES), 1)
+    half_of = lax.shift_right_logical(slot, 7)
+    slot = slot - half_of * LANES
+    seq_of, head = lax.shift_right_logical(slot, 4), slot - lax.shift_right_logical(slot, 4) * STEP
+    relane = flag((lane == half_of * SIDE + seq_of * HEADS + head) & (head < HEADS) & (seq_of < rows)).astype(bf16)
+    empty = jnp.zeros((LANES - rows * STEP, count), f32)
     is_own = step_at < pl.num_programs(0) // 2
 
-    def early(s, first, lines):
-        return jnp.where(is_own, early_own[s, first : first + lines, :], early_other[s, first : first + lines, :])
-
-    def late(s, first, lines):
-        return jnp.where(is_own, late_own[s, first : first + lines, :], late_other[s, first : first + lines, :])
-
-    def heads(s, first, lines):
-        return jnp.where(is_own, p_own[s, first : first + lines, :], p_other[s, first : first + lines, :])
-
-    def side_by_side(lines):
-        return jnp.concatenate([lines[16 * c : 16 * (c + 1)] for c in range(chunks)], 1)
+    def pick(own, other, s, first, lines):
+        return jnp.where(is_own, own[s, first : first + lines, :], other[s, first : first + lines, :])
 
     for s in range(per):
-        code = lanes_of(packet, s, chunks, chunks)
+        code = lanes_of(packet, s, 2 * chunks, chunks)
         slot0 = code >= 8.0
         seq = jnp.where(slot0, code - 8.0, code)
-        here = seq_low == seq
-        score_part = jnp.where(here, dot(low_heads, side_by_side(late(s, feats, 16 * chunks))), 0.0)
-        value_part = jnp.where(here, dot(low_heads, side_by_side(heads(s, at_heads, 16 * chunks))), 0.0)
-        value_part = jnp.where((seq_extra == seq) & slot0, 1.0, value_part)
-        basis = jnp.concatenate([early(s, at_early, feats), late(s, 0, feats)], 1)
-        x = dot(basis, jnp.concatenate([score_part, value_part], 0).astype(bf16))
-        side = side_of(lanes_of(packet, s, 0, chunks), group, half_rows, half)
+        scores = unpack_heads(pick(late_own, late_other, s, block + ROWS, head_lines(chunks)), chunks)
+        values = unpack_heads(pick(p_own, p_other, s, at_heads, head_lines(chunks)), chunks)
+        parts_of = [jnp.where(seq == float(r), scores, 0.0) for r in range(rows)] + [empty]
+        parts_of += [jnp.where(seq == float(r), values, 0.0) for r in range(rows)] + [empty]
+        both = jnp.concatenate([pick(early_own, early_other, s, at_early, block), pick(late_own, late_other, s, 0, block)], 0)
+        wide_rows = dot(both, relane).astype(bf16)
+        basis = [jnp.concatenate([wide_rows[k : k + block, :LANES], wide_rows[k : k + block, LANES:]], 0) for k in (0, block)]
+        x = dot(jnp.concatenate(basis, 1), jnp.concatenate(parts_of, 0).astype(bf16))
+        first = flag((iota((ROWS, count), 0).astype(f32) == seq) & slot0).astype(bf16)
+        x = x + dot(pick(late_own, late_other, s, block, ROWS), first, 0, 0)[:feats]
+        side = side_of(packet, s, chunks, group, half_rows, half)
         tall = jnp.concatenate([jnp.where(side == 1.0, x, 0.0), gap, jnp.where(side == 2.0, x, 0.0), gap], 0).astype(bf16)
         for c in range(chunks):
             start = s * count + c * LANES
             buf[start : start + LANES, :] = dot(eye, tall[:, c * LANES : (c + 1) * LANES], 1, 1)
     for s in range(per):
         low, high = own_span(firsts[step_at * per + s], group, count)
-        base = (step_at * per + s) * count
 
         def step(i, carry):
             for k in range(unroll):
                 t = i * unroll + k
                 part = parts[k % copies]
-                row = numbers[base + t]
+                row = numbers[0, 0, s * count + t]
                 part[pl.ds(row, 1), :] = part[pl.ds(row, 1), :] + buf[pl.ds(s * count + t, 1), :]
             return carry
 
@@ -522,13 +552,20 @@
             return total + lines * lines
 
         second = (vocab - half) // LANES
-        total = lax.fori_loop(0, second, lambda b, t: emit(b, t, True), jnp.zeros((LANES, LANES), f32))
-        for b in range(second, blocks):
-            total = emit(jnp.int32(b), total, False)
+        group_of = 7
+
+        def several(i, total):
+            for k in range(group_of):
+                total = emit(i * group_of + k, total, True)
+            return total
+
+        total = lax.fori_loop(0, second // group_of, several, jnp.zeros((LANES, LANES), f32))
+        for b in range(second // group_of * group_of, blocks):
+            total = emit(jnp.int32(b), total, b < second)
         square[...] = jnp.sum(total.reshape(LANES // ROWS, ROWS, LANES), 0)
 
 
-def spread_tokens(where, numbers, firsts, packets, early, late, p_heads, at_early, rows, half_rows, feats, count, per=8, unroll=32, copies=4):
+def spread_tokens(where, numbers, firsts, packets, early, late, p_heads, at_early, rows, half_rows, feats, count, per=8, unroll=40, copies=5):
     devices = packets.shape[0]
     block = packets.shape[1:]
     half = -(-half_rows // (2 * LANES)) * LANES
@@ -540,55 +577,72 @@
         partial(spread_kernel, rows, half_rows, feats, per, unroll, copies, at_early, at_early),
         out_shape=[pltpu.HBM((feats, half_rows), f32), pltpu.HBM((ROWS, LANES), f32)],
         grid_spec=pltpu.PrefetchScalarGridSpec(
-            num_scalar_prefetch=3,
+            num_scalar_prefetch=2,
             grid=(steps,),
-            in_specs=[some(block), mine(early), theirs(early), mine(late), theirs(late), mine(p_heads), theirs(p_heads)],
+            in_specs=[number_block(per, count), some(block), mine(early), theirs(early), mine(late), theirs(late), mine(p_heads), theirs(p_heads)],
             out_specs=[pl.BlockSpec((feats, half_rows), lambda i, *s: (0, 0), pipeline_mode=pl.Buffered(1)), pl.BlockSpec((ROWS, LANES), lambda i, *s: (0, 0))],
             scratch_shapes=[pltpu.VMEM((half, LANES), f32)] * copies + [pltpu.VMEM((per * count, LANES), f32)],
         ),
-        compiler_params=pltpu.CompilerParams(vmem_limit_bytes=44 * MIB),
+        compiler_params=pltpu.CompilerParams(vmem_limit_bytes=52 * MIB),
         cost_estimate=pl.CostEstimate(flops=10**9, bytes_accessed=3 * 10**7, transcendentals=0),
         name="spread_tokens",
-    )(where, numbers, firsts, packets, *early, *late, *p_heads)
-
-
-def attend_kernel(rows, mats, xt, vec, moved, sent, heads_out, facts, probs_out, psum_out, normed_out, inv_out, *scratch):
+    )(where, firsts, numbers.reshape(-1, 1, per * count), packets, *early, *late, *p_heads)
+
+
+def attend_kernel(rows, mats, xt, vec, moved, sent, heads_out, facts, y_out, probs_out, psum_out, normed_out, inv_out, *scratch):
     w = square_weights(mats, 0, *scratch, (0, 1, 2, 3))
-    x1, x00, q, o, probs, psum, normed, inv, qk, y, p_heads = attend(xt[...], w, vec[...], moved[...], rows)
+    x1, x00, q, o, probs, psum, normed, inv, qk, y = attend(xt[...], w, vec[...], moved[...], rows)
     tiles = to_tiles(x1)
-    parts = early_parts(qk.astype(bf16), y.astype(bf16), rows)
-    for dest in range(sent.shape[0]):
-        sent[dest] = jnp.concatenate([tiles, block_of(parts, dest, sent.shape[0])], 0).astype(bf16)
-    heads_out[...] = in_chunks(p_heads)
+    halves = both_halves(qk, rows)
+    wide = sent.shape[0]
+    block = D // (2 * wide)
+    for dest in range(wide):
+        sent[dest] = jnp.concatenate([tiles, table_block(halves, dest, block)], 0).astype(bf16)
+    heads_out[...] = pack_heads(probs.astype(bf16), rows)
     facts[...] = jnp.concatenate([to_tiles(value.astype(f32)) for value in (x00, q, o)], 0).astype(bf16)
+    y_out[...] = y.astype(bf16)
     probs_out[...], psum_out[...], normed_out[...], inv_out[...] = probs, psum, normed, inv
 
 
-def attend_back_kernel(rows, place, mats, got, d_res2, sums_up, normed, inv, probs, psum, xt, vec, late_out, last, *scratch):
+def attend_back_kernel(rows, place, mats, got, d_res2, sums_up, normed, inv, probs, psum, xt, vec, late_out, last, z_out, *scratch):
     w = square_weights(mats, 0, *scratch, (3, 2, 1, 0))
     wide = late_out.shape[0]
+    block = D // (2 * wide)
+    feats = 2 * block
     dx1 = d_res2[pl.ds(pl.multiple_of(place[0] * ROWS, ROWS), ROWS), :]
     for k in range(wide):
         dx1 = dx1 + got[k].astype(f32)
-    d_a, d_o, d_q, sums, vd, z, extra, ds_heads = attend_back(
+    d_a, d_o, d_q, sums, vd, z, extra, ds = attend_back(
         dx1, normed[...], inv[...], probs[...], psum[...], xt[...], w, vec[...], rows
     )
-    parts = late_parts(vd, z, extra, rows)
-    chunks = in_chunks(ds_heads)
-    tail = stack_rows(sums + [sums_up[...]])
+    halves = both_halves(vd, rows)
+    heads = pack_heads(ds, rows)
+    gap = jnp.zeros((ROWS, LANES - feats), f32)
     for dest in range(wide):
-        late_out[dest] = jnp.concatenate([block_of(parts, dest, wide).astype(bf16), chunks], 0)
-    last[...] = jnp.concatenate([to_tiles(value.astype(f32)) for value in (d_q, d_o, d_a, tail)], 0).astype(bf16)
-
-
-def pack_kernel(facts, last, d_up, out):
+        row_part = jnp.concatenate([extra[:, feats * dest : feats * (dest + 1)], gap], 1)
+        late_out[dest] = jnp.concatenate([jnp.concatenate([table_block(halves, dest, block), row_part], 0).astype(bf16), heads], 0)
+    z_out[...] = z.astype(bf16)
+    sums = sums + [sums_up[...]]
+    index = iota((ROWS, D), 0)
+    spare = ROWS - rows
+    values = [d_q.astype(f32), d_o.astype(f32), d_a.astype(f32)]
+    for number, row in enumerate(sums):
+        values[number // spare] = jnp.where(index == rows + number % spare, row, values[number // spare])
+    last[...] = jnp.concatenate([to_tiles(value) for value in values], 0).astype(bf16)
+
+
+def pack_kernel(rows, facts, last, y, z, d_up, d_up_other, out):
     wide = out.shape[0]
-    block = d_up.shape[0] // (2 * wide)
+    block = d_up.shape[0] // wide
+    hidden = d_up.shape[1] // 2
     values = jnp.concatenate([facts[...], last[...]], 0)
-    gap = jnp.zeros((block, LANES - d_up.shape[1]), f32)
+    halves_y, halves_z = both_halves(y[...], rows), both_halves(z[...], rows)
+    up = d_up[...] + d_up_other[...].astype(f32)
+    gap = jnp.zeros((block, LANES - hidden), f32)
     for dest in range(wide):
-        pieces = [d_up[block * n : block * (n + 1), :].astype(f32) for n in (dest, wide + dest)]
-        pieces = [jnp.concatenate([piece, gap], 1) for piece in pieces]
+        mine = up[block * dest : block * (dest + 1), :]
+        pieces = [jnp.concatenate([mine[:, k * hidden : (k + 1) * hidden], gap], 1) for k in range(2)]
+        pieces += [weight_block(halves_y, dest, block, wide), weight_block(halves_z, dest, block, wide)]
         out[dest] = jnp.concatenate([values, jnp.concatenate(pieces, 0).astype(bf16)], 0)
 
 
@@ -596,12 +650,10 @@
     return jnp.concatenate([from_tiles(own[...], 0), from_tiles(other[...], 0)], 0)
 
 
-def ffn_kernel(x_own, x_other, w_up, w_down, bias, u_out, h_out, own, other):
-    u, h, f = ffn(rows_of(x_own, x_other), w_up[...], w_down[...], bias[...])
-    half = own.shape[0]
+def ffn_kernel(x_own, w_up, w_down, bias, u_out, h_out, out):
+    u, h, f = ffn(from_tiles(x_own[...], 0), w_up[...], w_down[...], bias[...])
     u_out[...], h_out[...] = u, h
-    own[...] = f[:half]
-    other[...] = f[half:].astype(bf16)
+    out[...] = f.astype(bf16)
 
 
 def total_kernel(got, heads, out):
@@ -613,15 +665,16 @@
         out[k] = lines
 
 
-def middle_kernel(mats, x_own, x_other, f_own, f_other, u, w_up, w_down, vec, picks, valid, loss, pooled, d_c, d_res2, d_f, d_u, own, other, sums, sums_up, *scratch):
-    w = square_weights(mats, 4, *scratch, (4,))
+def middle_kernel(mats, x_own, x_other, f_own, f_other, u, w_up, w_down, vec, picks, loss, pooled, d_c, d_res2, d_f, d_u, out, sums, sums_up, *scratch):
+    get = square_weights(mats, 0, *scratch, (0,))
+    w = lambda k: get(0)
     x1 = rows_of(x_own, x_other).astype(f32)
     f = rows_of(f_own, f_other).astype(f32)
-    got = middle(x1, f, u[...], w_up[...], w_down[...], w, vec[...], picks[...], valid[...])
-    half = own.shape[0]
-    loss[...], pooled[...], d_c[...], d_res2[...], d_f[...], d_u[...] = got[:6]
-    own[...] = got[6][:half]
-    other[...] = got[6][half:].astype(bf16)
+    got = middle(x1, f, u[...], w_up[...], w_down[...], w, vec[...], picks[...])
+    lines = u.shape[0]
+    loss[...], pooled[...], d_c[...], d_res2[...] = got[:4]
+    d_f[...], d_u[...] = got[4][:lines], got[5]
+    out[...] = got[6].astype(bf16)
     sums[...] = stack_rows(got[7])
     su = jnp.sum(got[5].astype(f32), 0, keepdims=True)
     sums_up[...] = jnp.concatenate([su, jnp.zeros((1, D - su.shape[1]), f32)], 1)
@@ -629,68 +682,62 @@
 
 def own_cols(device, block):
     index = iota((D, LANES), 1)
-    return jnp.where((iota((D, LANES), 0) == device * block + index) & (index < block), 1.0, 0.0).astype(bf16)
+    return flag((iota((D, LANES), 0) == device * block + index) & (index < block)).astype(bf16)
 
 
 def own_rows(left, right, mine, block):
     return dot(dot(left, mine).astype(bf16), right, 0, 0)[:block]
 
 
-def up_grad_kernel(x_own, x_other, d_u, d_up):
-    x1 = rows_of(x_own, x_other)
-    d_up[...] = dot(x1, d_u[...], 0, 0).astype(bf16)
-
-
-def ffn_grads_kernel(where, h, d_f, pooled, d_c, d_down, d_head):
-    d_down[...] = dot(h[...], d_f[...], 0, 0)
+def ffn_grads_kernel(where, x_own, h, d_f, d_u, pooled, d_c, down_mine, down_theirs, d_head, up_mine, up_theirs):
+    first = where[0] == 0
+    hidden = down_mine.shape[0]
+    half = up_mine.shape[0]
+    d_up = dot(from_tiles(x_own[...], 0), d_u[...], 0, 0)
+    up_mine[...] = jnp.where(first, d_up[:half], d_up[half:])
+    up_theirs[...] = jnp.where(first, d_up[half:], d_up[:half]).astype(bf16)
+    d_down = dot(h[...], d_f[...], 0, 0)
+    down_mine[...] = jnp.where(first, d_down[:hidden], d_down[hidden:])
+    down_theirs[...] = jnp.where(first, d_down[hidden:], d_down[:hidden]).astype(bf16)
     block = d_head.shape[0]
     d_head[...] = own_rows(pooled[...], d_c[...], own_cols(where[1], block), block)
 
 
-def grads_kernel(rows, at_early, where, early_own, early_other, late_own, late_other, facts_own, facts_other, d_wh, d_down, sums, square, in_out, out_out, up_out, vec_out, square_out, x00, q_all, o_all, d_q, d_o, d_a, y, z, wide_z):
+def grads_kernel(rows, where, facts_own, facts_other, d_wh, down_mine, down_other, sums, square, in_out, out_out, up_out, down_out, vec_out, square_out, x00, q_all, o_all, d_q, d_o, d_a, y, z, wide_z):
     group, device = where[0], where[1]
     wide = facts_own.shape[0]
     devices = 2 * wide
     block = in_out.shape[0]
+    hidden = FF // devices
     first = group == 0
-    for n in range(devices):
-        at = slice(n * block, (n + 1) * block)
-        early = (early_own, early_other)[n // wide]
-        mine = [early[n % wide, at_early + k * block : at_early + (k + 1) * block, :].astype(f32) for k in range(2)]
-        y[at, :] = jnp.where(first, *mine)
-        late = (late_own, late_other)[n // wide]
-        mine = [late[n % wide, k * block : (k + 1) * block, :].astype(f32) for k in range(2)]
-        z[at, :] = jnp.where(first, *mine)
+    lines = ROWS * (D // LANES)
+    at_up = 6 * lines
     for base, facts in ((0, facts_own), (1, facts_other)):
         at = slice(base * wide * ROWS, (base + 1) * wide * ROWS)
-        lines = ROWS * (D // LANES)
         for k, out in enumerate((x00, q_all, o_all, d_q, d_o, d_a)):
             out[at, :] = from_tiles(facts, k * lines).astype(f32)
-        hidden = FF // devices
-        lines = 7 * lines
         for n in range(wide):
-            piece = jnp.where(first, facts[n, lines : lines + block, :].astype(f32), facts[n, lines + block : lines + 2 * block, :].astype(f32))
-            here, there = n * hidden, (wide + n) * hidden
-
-            @pl.when(group == base)
-            def _():
-                up_out[:, here : here + hidden] = piece[:, :hidden]
-
-            @pl.when(group != base)
-            def _():
-                up_out[:, there : there + hidden] = piece[:, :hidden]
-
-    def by_heads(source, first, values):
+            at = slice((base * wide + n) * block, (base * wide + n + 1) * block)
+            y[at, :] = facts[n, at_up + 2 * block : at_up + 3 * block, :].astype(f32)
+            z[at, :] = facts[n, at_up + 3 * block : at_up + 4 * block, :].astype(f32)
+    for n in range(wide):
+        for k in range(2):
+            piece = facts_own[n, at_up + k * block : at_up + (k + 1) * block, :].astype(f32)
+            at = (k * wide + n) * hidden
+            up_out[:, at : at + hidden] = piece[:, :hidden]
+    down_out[...] = down_mine[...] + down_other[...].astype(f32)
+
+    def by_heads(source, values):
         total = jnp.zeros((block, D), f32)
         low = source[...].astype(bf16)
         for r in range(rows):
-            wide_z[...] = dot(low, expand_table(rows, first, r))
+            wide_z[...] = dot(low, expand_table(rows, jnp.where(group == 0, 0, SIDE), r))
             for n in range(devices):
                 total = total + wide_z[n * block : (n + 1) * block, :] * values[n * ROWS + r : n * ROWS + r + 1, :]
         return total
 
-    d_wk = by_heads(z, Z_AT, q_all) * HEAD_DIM ** (-0.5)
-    d_wv = by_heads(y, SIDE, d_o)
+    d_wk = by_heads(z, q_all) * HEAD_DIM ** (-0.5)
+    d_wv = by_heads(y, d_o)
     mine = own_cols(device, block)
     d_wq = own_rows(x00[...].astype(bf16), d_q[...].astype(bf16), mine, block)
     d_wo = own_rows(o_all[...].astype(bf16), d_a[...].astype(bf16), mine, block)
@@ -705,43 +752,46 @@
 
     in_out[:, :D], in_out[:, D : 2 * D], in_out[:, 2 * D :] = d_wq, d_wk, d_wv
     out_out[...] = d_wo
-    for value in (d_wq, d_wk, d_wv, d_wo, d_wh[...], up_out[...], d_down[...]):
+    for value in (d_wq, d_wk, d_wv, d_wo, d_wh[...], up_out[...], down_out[...]):
         square_now = fold(square_now, value)
-    tails = jnp.concatenate([from_tiles(facts, 6 * ROWS * (D // LANES)) for facts in (facts_own, facts_other)], 0).astype(f32)
-    tail = jnp.sum(tails.reshape(devices, ROWS, D), 0)
+    spare = ROWS - rows
+    grouped = [jnp.sum(t[...].reshape(devices, ROWS, D), 0) for t in (d_q, d_o)]
+    tail = [grouped[k // spare][rows + k % spare : rows + k % spare + 1] for k in range(5)]
     mids = sums[...]
-    pieces = [tail[0:1], mids[0:1], mids[1:2], tail[3:4], tail[4:5], tail[2:3], tail[1:2]] + [mids[k : k + 1] for k in range(2, 6)]
+    pieces = [tail[0], mids[0:1], mids[1:2], tail[3], tail[4], tail[2], tail[1]] + [mids[k : k + 1] for k in range(2, 6)]
     index = iota((16, D), 0)
     total = jnp.zeros((16, D), f32)
     for number, row in enumerate(pieces):
         total = jnp.where(index == number, row, total)
     each = D // hidden
-    for base in range(2):
-        for k in range(wide):
-            line = (base * wide + k) * ROWS + 5
-            row = tails[line : line + 1]
-            shift = hidden * (k % each)
-            row = pltpu.roll(row, shift, 1) if shift else row
-            number = 11 + (k // each) + jnp.where(group == base, 0, wide // each)
-            total = total + jnp.where(index == number, row, 0.0)
+    for k in range(wide):
+        lines_of = [(base * wide + k) * ROWS + rows + 5 % spare for base in range(2)]
+        source = (d_q, d_o)[5 // spare]
+        row = source[lines_of[0] : lines_of[0] + 1, :] + source[lines_of[1] : lines_of[1] + 1, :]
+        for core in range(2):
+            shift = (hidden * (k % each) - hidden * core) % D
+            turned = pltpu.roll(row, shift, 1) if shift else row
+            col = iota((1, D), 1)
+            turned = jnp.where((col >= hidden * (k % each)) & (col < hidden * (k % each + 1)), turned, 0.0)
+            total = total + jnp.where(index == 11 + (core * wide + k) // each, turned, 0.0)
     vec_out[...] = total
     square_now = square_now + fold(jnp.zeros((ROWS, LANES), f32), total) / devices
-    for k in range(wide):
+    for k in range(devices):
         square_out[k] = square_now
 
 
-def adam_kernel(count, scales, weight, first, second, d_table, own, other, *refs):
+def adam_kernel(count, scales, weight, first, second, d_table, got, *refs):
     grads, state = refs[:count], refs[count : 4 * count]
     norm_out, factor_out = refs[4 * count : 4 * count + 2]
     outs = refs[4 * count + 2 : 7 * count + 2]
     far = refs[7 * count + 2 : 7 * count + 5]
-    loads, stores, got, sent = refs[7 * count + 5 :]
+    loads, stores, got_in, sent = refs[7 * count + 5 :]
     slots, lines = loads.shape[0], loads.shape[2]
     jobs = weight.shape[0] // lines
     sources = (weight, first, second, d_table)
 
     def load(j):
-        return [pltpu.make_async_copy(ref.at[pl.ds(j * lines, lines), :], loads.at[j % slots, k], got.at[j % slots, k]) for k, ref in enumerate(sources)]
+        return [pltpu.make_async_copy(ref.at[pl.ds(j * lines, lines), :], loads.at[j % slots, k], got_in.at[j % slots, k]) for k, ref in enumerate(sources)]
 
     def store(j):
         return [pltpu.make_async_copy(stores.at[j % slots, k], ref.at[pl.ds(j * lines, lines), :], sent.at[j % slots, k]) for k, ref in enumerate(far)]
@@ -749,9 +799,9 @@
     for j in range(min(slots, jobs)):
         for copy in load(j):
             copy.start()
-    total = own[0] + other[0]
-    for k in range(1, own.shape[0]):
-        total = total + own[k] + other[k]
+    total = got[0]
+    for k in range(1, got.shape[0]):
+        total = total + got[k]
     total = jnp.sum(jnp.sum(total, 0, keepdims=True), 1, keepdims=True)
     norm = jnp.sqrt(total)
     factor = jnp.minimum(1.0, clip_level / (norm + 1e-06))
@@ -849,7 +899,8 @@
     looked = jnp.where(inside, jnp.take(embedding.astype(bf16), local, axis=1), jnp.zeros((), bf16))
     looked = looked.reshape(feats, devices, tokens).transpose(1, 0, 2)
     xt = exchange(looked[:wide] + swap(looked[wide:])).reshape(D, tokens)
-    x1, x00, q, o, probs, psum, normed1, inv1, qk, y, p_heads = attend(xt, w, vec, moved, rows)
+    x1, x00, q, o, probs, psum, normed1, inv1, qk, y = attend(xt, w, vec, moved, rows)
+    p_heads = dot(heads_table(rows), probs.astype(bf16)).astype(bf16)
     x1_all = gather(x1.astype(bf16)).reshape(devices * ROWS, D)
 
     def to_owner(parts):
@@ -858,9 +909,9 @@
 
     u, h, f_part = ffn(x1_all, w_up, w_down, bias_up)
     f_all = gather(to_owner(f_part).astype(bf16)).reshape(devices * ROWS, D).astype(f32)
-    loss, pooled, d_c, d_res2, d_f, d_u, d_x1, sums = middle(x1_all.astype(f32), f_all, u, w_up, w_down, w, vec, pick_rows, valid_rows)
+    loss, pooled, d_c, d_res2, d_f, d_u, d_x1, sums = middle(x1_all.astype(f32), f_all, u, w_up, w_down, w, vec, jnp.concatenate([valid_rows.astype(jnp.int32), pick_rows], 1))
     d_x1 = lax.dynamic_slice(d_res2, (place * ROWS, 0), (ROWS, D)) + to_owner(d_x1)
-    d_a, d_o, d_q, sums_back, vd, z, extra, ds_heads = attend_back(d_x1, normed1, inv1, probs, psum, xt, w, vec, rows)
+    d_a, d_o, d_q, sums_back, vd, z, extra, ds = attend_back(d_x1, normed1, inv1, probs, psum, xt, w, vec, rows)
 
     to_features = lambda t: both(t.T.astype(bf16).reshape(wide, feats, -1))
 
@@ -887,7 +938,7 @@
     d_vec = jnp.concatenate([tail[0], mids[0], mids[1], tail[3], tail[4], tail[2], tail[1]] + mids[2:] + [ups])
     d_vec = lax.dynamic_slice(d_vec, (device * vectors.shape[0],), vectors.shape)
     basis = jnp.concatenate([to_features(qk), to_features(vd), to_features(extra)], 2)
-    lanes = gather(jnp.concatenate([ds_heads, p_heads], 0))
+    lanes = gather(jnp.concatenate([dot(heads_table(rows), ds).astype(bf16), p_heads], 0))
     seq = jnp.asarray(seq_np, jnp.int32)[None]
     here = sequence_of(iota((SIDE, 1), 0), rows) == seq
     widen = lambda t: jnp.where(here[None], jnp.einsum("ha,nht->nat", heads_table(rows), t, preferred_element_type=f32), 0.0).astype(bf16)
@@ -928,36 +979,35 @@
     seq_np = np.concatenate([np.repeat(np.arange(pas_count), pas_len), pas_count + np.repeat(np.arange(qry_count), qry_len)])
     pos_np = np.concatenate([np.tile(np.arange(pas_len), pas_count), np.tile(np.arange(qry_len), qry_count)])
     vec_lines = -(-vectors.shape[0] // LANES)
-    packet_lines = -(-(2 * chunks + 1 + vec_lines) // ROWS) * ROWS
-    note = [valid.astype(f32), positive.astype(f32), negatives.astype(f32).reshape(-1)]
-    note_size = sum(t.shape[0] for t in note)
-    assert 1 + note_size <= LANES
-    pieces = [passage_ids.astype(f32).reshape(-1), query_ids.astype(f32).reshape(-1)]
-    pieces += [jnp.repeat(passage_len.astype(f32), pas_len), jnp.repeat(query_len.astype(f32), qry_len)]
-    pieces += [jnp.zeros((1,), f32)] + note + [jnp.zeros((LANES - 1 - note_size,), f32), vectors]
-    pieces.append(jnp.zeros((packet_lines * LANES - sum(t.shape[0] for t in pieces),), f32))
+    packet_lines = -(-(3 * chunks + 1 + vec_lines) // ROWS) * ROWS + 2 * block
+    at_note = 3 * chunks
+    pieces = [passage_ids.reshape(-1), query_ids.reshape(-1), passage_len, query_len, valid, positive, negatives.reshape(-1)]
+    size = sum(t.shape[0] for t in pieces)
+    assert size < tokens + LANES
+    base = jnp.concatenate(pieces + [jnp.zeros((-size % (ROWS * LANES),), jnp.int32)]).reshape(-1, LANES)
+    vec_pad = jnp.concatenate([vectors, jnp.zeros((-vectors.shape[0] % LANES,), f32)]).reshape(-1, LANES)
     packet, moved = call(
-        partial(prepare_kernel, half_rows, tokens),
-        [shape((wide, packet_lines, LANES)), shape((ROWS, tokens))],
-        jnp.concatenate(pieces).reshape(packet_lines, LANES), jnp.asarray(seq_np, jnp.int32)[None], jnp.asarray(pos_np, jnp.int32)[None],
+        partial(prepare_kernel, half_rows, tokens, rows),
+        [shape((wide, packet_lines, LANES), bf16), shape((ROWS, tokens))],
+        base, vec_pad, jnp.asarray(seq_np, jnp.int32)[None], jnp.asarray(pos_np, jnp.int32)[None], w_ffn_up,
         near_outs=(0,), name="prepare",
     )
     packet_own = exchange(packet)
     (table,) = call(build_kernel, [shape((half, LANES))], embedding, name="build", flops=10**8)
     packet_own, table = tie(packet_own, table)
     packet_other = swap(packet_own)
-    (low_mats,) = call(cast_kernel, [shape((block, 5 * D), bf16)], attn_in, attn_out, head, near_outs=(0,), name="cast")
+    low_mats, low_head = call(cast_kernel, [shape((block, 4 * D), bf16), shape((block, D), bf16)], attn_in, attn_out, head, near_outs=(0, 1), name="cast")
     mats = lax.all_gather(low_mats, ALL, axis=0, tiled=True)
-    w_ffn_up, w_ffn_down, _ = tie(w_ffn_up, w_ffn_down, packet)
-    w_up = lax.all_to_all(
-        w_ffn_up.astype(bf16).reshape(block, devices, hidden).transpose(1, 0, 2), ALL, split_axis=0, concat_axis=0, tiled=True
-    ).reshape(D, hidden)
-    w_down = w_ffn_down.astype(bf16)
+    w_head = lax.all_gather(low_head, ALL, axis=0, tiled=True)
+    down_low = w_ffn_down.astype(bf16)
+    w_down = in_order(down_low, swap(down_low), group)
 
     def numbers_of(packets):
-        local = packets[:, :chunks] - (group * half_rows).astype(f32)
+        ids = packets[:, :chunks].astype(f32) * 256.0 + packets[:, chunks : 2 * chunks].astype(f32)
+        local = ids - (group * half_rows).astype(f32)
         row_at = jnp.clip(jnp.where(local >= half, local - half, local), 0, half - 1)
-        return row_at.astype(jnp.int32).reshape(-1), packets[:, 2 * chunks, 0].astype(jnp.int32)
+        first = packets[:, at_note, 0].astype(f32) + 256.0 * packets[:, at_note, LANES - 1].astype(f32)
+        return row_at.astype(jnp.int32).reshape(-1), first.astype(jnp.int32)
 
     look = partial(lookup, half_rows=half_rows, feats=feats, count=tokens)
     num_own, num_other = numbers_of(packet_own), numbers_of(packet_other)
@@ -966,88 +1016,88 @@
     numbers = jnp.concatenate([num_own[0], num_other[0]])
     firsts = jnp.concatenate([num_own[1], num_other[1]])
     packets = jnp.concatenate([packet_own, packet_other], 0)
-
-    vec = in_order(packet_own, packet_other, group)[:, 2 * chunks + 1 : 2 * chunks + 1 + vec_lines].reshape(devices, -1)
+    ordered = in_order(packet_own, packet_other, group)
+    w_up = ordered[:, packet_lines - 2 * block :, :hidden].reshape(devices, 2, block, hidden).transpose(0, 2, 1, 3).reshape(D, 2 * hidden)
+    vec = ordered[:, at_note + 1 : at_note + 1 + vec_lines].astype(f32).reshape(devices, -1)
     vec = vec[:, : vectors.shape[0]].reshape(-1, D)
-    bias_up = lax.dynamic_slice(vec.reshape(-1), (11 * D + device * hidden,), (hidden,))[None]
-    notes = packets[:, 2 * chunks]
-    valid_rows = jnp.pad(notes[:, 1 : 1 + qry_count], ((0, 0), (pas_count, ROWS - rows))).reshape(-1, 1)
+    bias_all = vec[11:].reshape(2, wide, hidden)
+    bias_up = lax.dynamic_slice(bias_all, (0, place, 0), (2, 1, hidden)).reshape(1, 2 * hidden)
+    notes = packets[:, at_note].astype(f32)
     at = 1 + qry_count
     picked = jnp.concatenate(
         [notes[:, at : at + qry_count, None], notes[:, at + qry_count : at + qry_count + negatives.size].reshape(devices, qry_count, -1)], 2
     ).astype(jnp.int32)
     pick_dev = picked // pas_count
     pick_row = (((pick_dev // wide) ^ group) * wide + pick_dev % wide) * ROWS + picked % pas_count
-    pick_rows = jnp.pad(pick_row, ((0, 0), (pas_count, ROWS - rows), (0, 0)), constant_values=-1).reshape(devices * ROWS, -1)
-
-    xt, vec, bias_up, valid_rows, pick_rows, w_up, w_down, packets, numbers, firsts = tie(
-        xt, vec, bias_up, valid_rows, pick_rows, w_up, w_down, packets, numbers, firsts
+    pick_row = jnp.concatenate([notes[:, 1 : 1 + qry_count, None].astype(jnp.int32), pick_row], 2)
+    pick_rows = jnp.pad(pick_row, ((0, 0), (pas_count, ROWS - rows), (0, 0))).reshape(devices * ROWS, -1)
+
+    xt, vec, bias_up, pick_rows, w_up, w_down, packets, numbers, firsts = tie(
+        xt, vec, bias_up, pick_rows, w_up, w_down, packets, numbers, firsts
     )
     tile_lines = ROWS * (D // LANES)
-    sent, p_heads, facts, probs, psum, normed1, inv1 = call(
+    heads_at, units = head_lines(chunks), 2 * hidden
+    sent, p_heads, facts, y, probs, psum, normed1, inv1 = call(
         partial(attend_kernel, rows),
         [
-            shape((wide, tile_lines + 2 * block, LANES), bf16), shape((16 * chunks, LANES), bf16),
-            shape((3 * tile_lines, LANES), bf16),
-            shape((SIDE, tokens)), shape((SIDE, 1)), shape((ROWS, D)), shape((ROWS, 1)),
+            shape((wide, tile_lines + block, LANES), bf16), shape((heads_at, LANES), bf16), shape((3 * tile_lines, LANES), bf16),
+            shape((SIDE, D), bf16), shape((SIDE, tokens)), shape((SIDE, 1)), shape((ROWS, D)), shape((ROWS, 1)),
         ],
         xt, vec, moved,
         far=(mats,), near=(0,), near_outs=(0,), scratch=weight_scratch(4), name="attend", flops=10**9,
     )
     x_own, x_other = pair(sent)
-    u, h, f_mine, f_theirs = call(
-        ffn_kernel,
-        [shape((devices * ROWS, hidden)), shape((devices * ROWS, hidden), bf16), shape((lines, D)), shape((lines, D), bf16)],
-        x_own, x_other, w_up, w_down, bias_up,
-        near=(0, 1), near_outs=(2, 3), name="ffn", flops=10**8, vmem=16,
-    )
-    f_parts = exchange((f_mine + swap(f_theirs)).astype(bf16).reshape(wide, ROWS, D))
-    (f_sum,) = call(
-        total_kernel, [shape((wide, tile_lines + 16 * chunks, LANES), bf16)], f_parts, p_heads, near=(0,), near_outs=(0,), name="total"
-    )
+    u, h, f_mine = call(
+        ffn_kernel, [shape((lines, units)), shape((lines, units), bf16), shape((lines, D), bf16)], x_own, w_up, w_down, bias_up,
+        near=(0,), near_outs=(2,), name="ffn", flops=10**8, vmem=16,
+    )
+    f_parts = exchange(f_mine.reshape(wide, ROWS, D))
+    (f_sum,) = call(total_kernel, [shape((wide, tile_lines + heads_at, LANES), bf16)], f_parts, p_heads, near=(0,), near_outs=(0,), name="total")
     f_own, f_other = pair(f_sum)
-    loss, pooled, d_c, d_res2, d_f, d_u, d_mine, d_theirs, sums, sums_up = call(
+    loss, pooled, d_c, d_res2, d_f, d_u, d_sum, sums, sums_up = call(
         middle_kernel,
         [
             shape((1, 1)), shape((devices * ROWS, D), bf16), shape((devices * ROWS, D), bf16), shape((devices * ROWS, D)),
-            shape((devices * ROWS, D), bf16), shape((devices * ROWS, hidden), bf16), shape((lines, D)), shape((lines, D), bf16),
-            shape((ROWS, D)), shape((1, D)),
+            shape((lines, D), bf16), shape((lines, units), bf16), shape((lines, D), bf16), shape((ROWS, D)), shape((1, D)),
         ],
-        x_own, x_other, f_own, f_other, u, w_up, w_down, vec, pick_rows, valid_rows,
-        far=(mats,), scratch=weight_scratch(1), near=(0, 1, 2, 3), near_outs=(6, 7), name="middle", flops=10**9, vmem=32,
-    )
-    d_sum = (d_mine + swap(d_theirs)).astype(bf16).reshape(wide, ROWS, D)
-    got = exchange(d_sum)
-    (d_up,) = call(up_grad_kernel, [shape((D, hidden), bf16)], x_own, x_other, d_u, after=(d_sum,), near=(0, 1), name="up_grad", flops=10**8)
-    late, last = call(
+        x_own, x_other, f_own, f_other, u, w_up, w_down, vec, pick_rows,
+        far=(w_head,), scratch=weight_scratch(1), near=(0, 1, 2, 3), near_outs=(6,), name="middle", flops=10**9, vmem=32,
+    )
+    got = exchange(d_sum.reshape(wide, ROWS, D))
+    down_mine, down_theirs, d_whead, up_mine, up_theirs = call(
+        ffn_grads_kernel,
+        [shape((hidden, D)), shape((hidden, D), bf16), shape((block, D)), shape((D // 2, units)), shape((D // 2, units), bf16)],
+        x_own, h, d_f, d_u, pooled, d_c,
+        scalars=(where,), after=(d_sum,), near=(0,), name="ffn_grads", flops=10**8,
+    )
+    late, last, z = call(
         partial(attend_back_kernel, rows),
-        [shape((wide, 2 * block + 16 * chunks, LANES), bf16), shape((4 * tile_lines, LANES), bf16)],
+        [shape((wide, block + ROWS + heads_at, LANES), bf16), shape((3 * tile_lines, LANES), bf16), shape((SIDE, D), bf16)],
         got, d_res2, sums_up, normed1, inv1, probs, psum, xt, vec,
-        scalars=(place_at,), far=(mats,), near=(0,), near_outs=(0,), scratch=weight_scratch(4), name="attend_back", flops=10**9,
+        scalars=(place_at,), far=(mats,), after=(up_mine,), near=(0,), near_outs=(0,), scratch=weight_scratch(4), name="attend_back", flops=10**9,
     )
     late_own, late_other = pair(late)
-    d_down, d_whead = call(
-        ffn_grads_kernel, [shape((hidden, D)), shape((block, D))], h, d_f, pooled, d_c,
-        scalars=(where,), after=(late,), name="ffn_grads", flops=10**8,
-    )
     (packed,) = call(
-        pack_kernel, [shape((wide, 7 * tile_lines + 2 * block, LANES), bf16)], facts, last, d_up, after=(late_own,), near_outs=(0,), name="pack",
-    )
-    last_own = exchange(packed)
+        partial(pack_kernel, rows), [shape((wide, 6 * tile_lines + 4 * block, LANES), bf16)], facts, last, y, z, up_mine, swap(up_theirs),
+        after=(late,), near_outs=(0,), name="pack",
+    )
+    piece = packed[:1, :ROWS] + late_own[:1, :ROWS] * jnp.zeros((), bf16)
+    last_own = exchange(lax.dynamic_update_slice(packed, piece, (0, 0, 0)))
     d_table, square = spread_tokens(
         where, numbers, firsts, packets, (x_own, x_other), (late_own, late_other), (f_own, f_other), tile_lines, rows, half_rows, feats, tokens
     )
-    last_own = last_own + (square[0, 0] * 0.0).astype(bf16)
+    piece = last_own[:1, :ROWS] + (square[None] * 0.0).astype(bf16)
+    last_own = lax.dynamic_update_slice(last_own, piece, (0, 0, 0))
     last_other = swap(last_own)
-    d_attn_in, d_wo, d_wup, d_vec, squares = call(
-        partial(grads_kernel, rows, tile_lines),
-        [shape((block, 3 * D)), shape((block, D)), shape((block, FF)), shape((16, D)), shape((wide, ROWS, LANES))],
-        x_own, x_other, late_own, late_other, last_own, last_other, d_whead, d_down, sums, square,
+    d_attn_in, d_wo, d_wup, d_down, d_vec, squares = call(
+        partial(grads_kernel, rows),
+        [shape((block, 3 * D)), shape((block, D)), shape((block, FF)), shape((hidden, D)), shape((16, D)), shape((devices, ROWS, LANES))],
+        last_own, last_other, d_whead, down_mine, swap(down_theirs), sums, square,
         scalars=(where,),
         scratch=[pltpu.VMEM((devices * ROWS, D), f32)] * 6 + [pltpu.VMEM((D, LANES), f32)] * 2 + [pltpu.VMEM((D, D), f32)],
-        near=(4, 5), near_outs=(4,), name="grads", flops=10**9, vmem=32,
-    )
-    squares_own, squares_other = pair(squares)
+        near=(0, 1), near_outs=(5,), name="grads", flops=10**9, vmem=32,
+    )
+    squares_got = lax.all_to_all(squares, ALL, split_axis=0, concat_axis=0, tiled=True)
     d_vectors = lax.dynamic_slice(d_vec.reshape(-1), (device * vectors.shape[0],), vectors.shape)
     step_float = step_count[0].astype(f32)
     scales = jnp.stack([1.0 / (1.0 - jnp.power(0.9, step_float)), 1.0 / (1.0 - jnp.power(0.999, step_float))])
@@ -1057,13 +1107,13 @@
     norm, factor, *new = call(
         partial(adam_kernel, len(grads)),
         [shape((1, 1)), shape((1, 1))] + [shape(t.shape) for t in middle_state],
-        squares_own, squares_other, *grads, *middle_state,
+        squares_got, *grads, *middle_state,
         scalars=(scales,), far=(*state[:3], d_table), far_outs=[shape(embedding.shape)] * 3,
         scratch=[
             pltpu.VMEM((slots, 4, step_rows, half_rows), f32), pltpu.VMEM((slots, 3, step_rows, half_rows), f32),
             pltpu.SemaphoreType.DMA((slots, 4)), pltpu.SemaphoreType.DMA((slots, 3)),
         ],
-        near=(0, 1), name="adam", vmem=40,
+        near=(0,), name="adam", vmem=40,
     )
     new_vectors = update(*state[18:], d_vectors * factor[0, 0], RATES[6], scales[0], scales[1])
     return (loss[0, 0], norm[0, 0]) + tuple(new[15:]) + tuple(new[:15]) + new_vectors

time: 325 us -> 290 us (0.89)
  blocking collectives: 63.6 us -> 44.7 us
  Pallas kernels: 135 us -> 119 us
  waiting for transfers between devices: 53 us -> 59.4 us
  starting transfers between devices: 37.3 us -> 31.2 us
    all_to_all x4 -> x3, blocking collectives: 63.6 us -> 44.7 us  [exchange(): return lax.all_to_all(x, 'wide', split_axis=0, concat_axis=0, tiled=True)]
    pallas_call x1, Pallas kernels: 45.7 us -> 34.8 us  [spread_tokens(): pl.pallas_call(partial(spread_kernel, rows, half_rows, feats, per, unroll...]
    all_to_all x5, starting transfers between devices: 30.1 us -> 23.3 us  [exchange(): return lax.all_to_all(x, 'wide', split_axis=0, concat_axis=0, tiled=True)]
    all_to_all x1, waiting for transfers between devices: 0.01 us -> 6 us  [body(): lax.all_to_all(squares, ALL, split_axis=0, concat_axis=0, tiled=True)]
    convert_element_type x12 -> x7, other arithmetic: 5.53 us -> 1.08 us  [the longest x4 0.97 us: numbers_of(): return (row_at.astype(jnp.int32).reshape(-1), first.astype(jnp.int32))]
    pallas_call x13 -> x12, Pallas kernels: 65.3 us -> 61.8 us  [call(): pl.pallas_call(run, grid=(1,), out_shape=shapes, in_specs=in_specs, out_s...]
    reshape x10, local copies, waits for them, and re-layouts: 1.99 us -> 5.46 us  [the longest x1 1.26 us: body(): jnp.concatenate([vectors, jnp.zeros((-vectors.shape[0] % LANES,), f32)])]
  transfers between devices with their start and end apart: 16 -> 17, of which waited for: 12 -> 11; matrix products, arithmetic and copies ran while one was open for 4% -> 4% of each run, Pallas kernels for 26% -> 28%
where the time goes in v1:
time: 290 us; the launch traced here: 286 us
  Pallas kernels  119 us (41%)
  waiting for transfers between devices  59.4 us (20%)
  blocking collectives  44.7 us (15%)
  starting transfers between devices  31.2 us (11%)
  between operations  15.9 us (5%)
  local copies, waits for them, and re-layouts  10.8 us (4%)
  other arithmetic  5.43 us (2%)
    pallas_call x12, Pallas kernels, call(): pl.pallas_call(run, grid=(1,), out_shape=shapes, in_specs=in_specs, out_s...  61.8 us
    all_to_all x3, blocking collectives, exchange(): return lax.all_to_all(x, 'wide', split_axis=0, concat_axis=0, tiled=True)  44.7 us
    all_to_all x5, waiting for transfers between devices, exchange(): return lax.all_to_all(x, 'wide', split_axis=0, concat_axis=0, tiled=True)  41.7 us
    pallas_call x1, Pallas kernels, spread_tokens(): pl.pallas_call(partial(spread_kernel, rows, half_rows, feats, per, unroll...  34.8 us
    all_to_all x5, starting transfers between devices, exchange(): return lax.all_to_all(x, 'wide', split_axis=0, concat_axis=0, tiled=True)  23.3 us
    pallas_call x2, Pallas kernels, lookup(): pl.pallas_call(partial(lookup_kernel, half_rows, per, unroll, add is not...  22.1 us
    ppermute x9, waiting for transfers between devices, swap(): return lax.ppermute(x, 'group', [(0, 1), (1, 0)])  11.6 us
    all_to_all x1, starting transfers between devices, body(): lax.all_to_all(squares, ALL, split_axis=0, concat_axis=0, tiled=True)  6.02 us
  transfers between devices with their start and end apart: 17, of which 11 were waited for; matrix products, arithmetic and copies ran while one was open for 4% of the time, Pallas kernels for 28%

profile of v1, /device:TPU:0, one launch (start us, length us, event | category | flops | bytes accessed | tf_op | source)
XLA Modules:
  0.0 286.0 jit_solution(12559544982186984868)
XLA Ops:
  7.2 1.7 cast.1
  9.6 0.8 reshape.143
  10.4 0.8 reshape.144
  11.2 1.4 concatenate.31
  12.5 1.3 pad_bitcast_fusion.1.refs_1_
  13.8 2.6 prepare.1
  16.4 8.3 %all-to-all-start = ((bf16[16,72,128]{2,1,0:T(8,128)(2,1)}), bf16[16,72,128]{2,1,0:T(8,128)(2,1)S(1)}, u32[]{:S(2)}, u32[]{:S(2)}) async-start(bf16[16,72,128]{2,1,0:T(8,128)(2,1)} %get-tuple-element.96), calls=%async_computation | async-start | bytes 589824 | tf_op jit(solution)/shard_map/all_to_all | solution.py:840
  24.7 7.0 %build.1.table = f32[12672,128]{1,0:T(8,128)} custom-call(f32[48,25216]{1,0:T(8,128)} %refs_1_.3), custom_call_target="tpu_custom_call" | custom-call | flops 100000000 | bytes 11329536 | tf_op jit(solution)/shard_map/build/pallas_call | solution.py:314
  31.7 6.1 %all-to-all-done.packet = bf16[16,72,128]{2,1,0:T(8,128)(2,1)S(1)} async-done(((bf16[16,72,128]{2,1,0:T(8,128)(2,1)}), bf16[16,72,128]{2,1,0:T(8,128)(2,1)S(1)}, u32[]{:S(2)}, u32[]{:S(2)}) %all-to-all-start) | async-done | bytes 294944 | tf_op jit(solution)/shard_map/all_to_all | solution.py:840
  37.9 1.5 collective-permute-done.packet
  39.5 0.5 convert_reduce_fusion.firsts
  40.0 10.6 %lookup.1 = bf16[16,48,640]{2,1,0:T(8,128)(2,1)S(1)} custom-call(s32[2]{0:T(128)S(1)} %pad_add_fusion.2.where.refs_0_, s32[16]{0:T(128)S(1)} %convert_reduce_fusion.firsts, s32[4,1,2560]{2,1,0:T(1,128)S(1)} %reshape_reshape.9.numbers, bf16[16,72,128]{2,1,0:T(8,128)(2,1)S(1)} %collective-permute-done.packet, f32[12672,128]{1,0:T(8,128)} %build.1.table), custom_call_target="tpu_custom_call" | custom-call | flops 1000000000 | bytes 10000000 | tf_op jit(solution)/shard_map/lookup/pallas_call | solution.py:460
  50.8 0.5 collective-permute-start.2
  51.3 2.1 collective-permute-done.2
  53.5 0.8 maximum_select_fusion.1.refs_2_.refs_7_
  54.4 0.5 convert_reduce_fusion.1.firsts
  54.8 11.4 %lookup_add.1 = bf16[16,48,640]{2,1,0:T(8,128)(2,1)} custom-call(s32[2]{0:T(128)S(1)} %pad_add_fusion.2.where.refs_0_, s32[16]{0:T(128)S(1)} %convert_reduce_fusion.1.firsts, s32[4,1,2560]{2,1,0:T(1,128)S(1)} %reshape_reshape.8.numbers, bf16[16,72,128]{2,1,0:T(8,128)(2,1)S(1)} %all-to-all-done.packet, f32[12672,128]{1,0:T(8,128)} %build.1.table, ...), custom_call_target="tpu_custom_call" | custom-call | flops 1000000000 | bytes 10000000 | tf_op jit(solution)/shard_map/lookup_add/pallas_call | solution.py:460
  66.2 3.6 %all-to-all-start.1 = ((bf16[16,48,640]{2,1,0:T(8,128)(2,1)}), bf16[16,48,640]{2,1,0:T(8,128)(2,1)S(1)}, u32[]{:S(2)}, u32[]{:S(2)}) async-start(bf16[16,48,640]{2,1,0:T(8,128)(2,1)} %lookup_add.1), calls=%async_computation.1 | async-start | bytes 1966080 | tf_op jit(solution)/shard_map/all_to_all | solution.py:840
  70.0 0.1 maximum_select_fusion
  70.2 0.1 copy.74
  70.4 0.1 copy.76
  70.5 0.1 copy.75
  70.6 0.1 copy.83
  70.7 0.3 copy.87
  71.1 1.0 reshape.156.refs_1_.refs_6_
  72.0 0.1 reshape.164.refs_2_.refs_8_.refs_10_
  72.2 0.1 reshape.151
  72.3 0.6 reshape.152.refs_3_
  73.0 0.7 pad_bitcast_fusion.refs_9_
  73.7 22.3 %all-to-all-done.1 = bf16[16,48,640]{2,1,0:T(8,128)(2,1)S(1)} async-done(((bf16[16,48,640]{2,1,0:T(8,128)(2,1)}), bf16[16,48,640]{2,1,0:T(8,128)(2,1)S(1)}, u32[]{:S(2)}, u32[]{:S(2)}) %all-to-all-start.1) | async-done | bytes 983072 | tf_op jit(solution)/shard_map/all_to_all | solution.py:840
  96.0 6.3 %attend.1 = (bf16[16,72,128]{2,1,0:T(8,128)(2,1)S(1)}, bf16[64,128]{1,0:T(8,128)(2,1)}, bf16[144,128]{1,0:T(8,128)(2,1)}, bf16[64,768]{1,0:T(8,128)(2,1)}, f32[6...) custom-call(bf16[768,3072]{1,0:T(8,128)(2,1)} %all-gather.5.cloned.1.call-done.refs_0_.refs_1_, ...), custom_call_target="tpu_custom_call" | custom-call | flops 1000000000 | bytes 6403360 | tf_op jit(solution)/shard_map/attend/pallas_call | solution.py:314
  102.3 17.4 %all_to_all.45.refs_0_.refs_1_.early_own = bf16[16,72,128]{2,1,0:T(8,128)(2,1)S(1)} all-to-all(bf16[16,72,128]{2,1,0:T(8,128)(2,1)S(1)} %get-tuple-element.102), channel_id=1, replica_groups=mesh['group'=2,'wide'=16] {'wide'}, dimensions={0} | all-to-all | bytes 589824 | tf_op jit(solution)/shard_map/all_to_all | solution.py:840
  119.7 2.0 ffn.1
  121.7 11.4 %all_to_all.46.refs_0_ = bf16[16,8,768]{2,1,0:T(8,128)(2,1)S(1)} all-to-all(bf16[16,8,768]{2,1,0:T(8,128)(2,1)S(1)} %bitcast.41), channel_id=1, replica_groups=mesh['group'=2,'wide'=16] {'wide'}, dimensions={0} | all-to-all | bytes 393216 | tf_op jit(solution)/shard_map/all_to_all | solution.py:840
  133.1 0.8 total.1
  133.9 15.9 %all_to_all.47.refs_3_.p_own = bf16[16,112,128]{2,1,0:T(8,128)(2,1)S(1)} all-to-all(bf16[16,112,128]{2,1,0:T(8,128)(2,1)S(1)} %total.1), channel_id=1, replica_groups=mesh['group'=2,'wide'=16] {'wide'}, dimensions={0} | all-to-all | bytes 917504 | tf_op jit(solution)/shard_map/all_to_all | solution.py:840
  149.8 0.5 collective-permute-start.3
  150.3 1.7 collective-permute-done.3.refs_2_.early_other
  152.0 7.4 %middle.1 = (f32[1,1]{1,0:T(1,128)}, bf16[256,768]{1,0:T(8,128)(2,1)}, bf16[256,768]{1,0:T(8,128)(2,1)}, f32[256,768]{1,0:T(8,128)}, bf16[128,768]{1,0:T(8,128)(...) custom-call(bf16[768,768]{1,0:T(8,128)(2,1)} %all-gather.3.cloned.1.call-done.r, ...), custom_call_target="tpu_custom_call" | custom-call | flops 1000000000 | bytes 5473284 | tf_op jit(solution)/shard_map/middle/pallas_call | solution.py:314
  159.5 4.0 %all-to-all-start.5 = ((bf16[16,8,768]{2,1,0:T(8,128)(2,1)}), bf16[16,8,768]{2,1,0:T(8,128)(2,1)S(1)}, u32[]{:S(2)}, u32[]{:S(2)}) async-start(bf16[16,8,768]{2,1,0:T(8,128)(2,1)} %bitcast.16), calls=%async_computation.5 | async-start | bytes 393216 | tf_op jit(solution)/shard_map/all_to_all | solution.py:840
  163.5 2.6 ffn_grads.1
  166.0 6.3 %all-to-all-done.5.refs_2_ = bf16[16,8,768]{2,1,0:T(8,128)(2,1)S(1)} async-done(((bf16[16,8,768]{2,1,0:T(8,128)(2,1)}), bf16[16,8,768]{2,1,0:T(8,128)(2,1)S(1)}, u32[]{:S(2)}, u32[]{:S(2)}) %all-to-all-start.5) | async-done | bytes 196640 | tf_op jit(solution)/shard_map/all_to_all | solution.py:840
  172.4 1.0 copy-done.1
  173.4 7.1 %attend_back.1 = (bf16[16,96,128]{2,1,0:T(8,128)(2,1)}, bf16[144,128]{1,0:T(8,128)(2,1)}, bf16[64,768]{1,0:T(8,128)(2,1)}) custom-call(s32[1]{0:T(128)} %bitcast.15.refs_0_, bf16[768,3072]{1,0:T(8,128)(2,1)} %all-gather.5.cloned.1.call-done.refs_0_.refs_1_, bf16[16,8,768]{2,1,0:T(8,128)(2,1)S(1)} %all-to-all-done.5.refs_2_, ...), custom_call_target="tpu_custom_call" | custom-call | flops 1000000000 | bytes 7450912 | tf_op jit(solution)/shard_map/attend_back/pallas_call | solution.py:314
  180.5 3.6 %all-to-all-start.6 = ((bf16[16,96,128]{2,1,0:T(8,128)(2,1)}), bf16[16,96,128]{2,1,0:T(8,128)(2,1)S(1)}, u32[]{:S(2)}, u32[]{:S(2)}) async-start(bf16[16,96,128]{2,1,0:T(8,128)(2,1)} %get-tuple-element.127.refs_6_), calls=%async_computation.6 | async-start | bytes 786432 | tf_op jit(solution)/shard_map/all_to_all | solution.py:840
  184.2 1.4 collective-permute-done.6.refs_5_
  185.6 0.7 copy-done.8
  186.3 2.9 %pack.1 = bf16[16,384,128]{2,1,0:T(8,128)(2,1)} custom-call(bf16[144,128]{1,0:T(8,128)(2,1)} %get-tuple-element.129.refs_0_, bf16[144,128]{1,0:T(8,128)(2,1)} %get-tuple-element.130.refs_1_, bf16[64,768]{1,0:T(8,128)(2,1)} %get-tuple-element.131.refs_2_, bf16[64,768]{1,0:T(8,128)(2,1)} %get-tuple-element.132.refs_3_, ...), custom_call_target="tpu_custom_call" | custom-call | bytes 2285568 | tf_op jit(solution)/shard_map/pack/pallas_call | solution.py:314
  189.2 6.9 %all-to-all-done.6.late_own = bf16[16,96,128]{2,1,0:T(8,128)(2,1)S(1)} async-done(((bf16[16,96,128]{2,1,0:T(8,128)(2,1)}), bf16[16,96,128]{2,1,0:T(8,128)(2,1)S(1)}, u32[]{:S(2)}, u32[]{:S(2)}) %all-to-all-start.6) | async-done | bytes 393248 | tf_op jit(solution)/shard_map/all_to_all | solution.py:840
  196.1 1.3 fusion.20
  197.4 3.8 %all-to-all-start.7 = ((bf16[16,384,128]{2,1,0:T(8,128)(2,1)}), bf16[16,384,128]{2,1,0:T(8,128)(2,1)S(1)}, u32[]{:S(2)}, u32[]{:S(2)}) async-start(bf16[16,384,128]{2,1,0:T(8,128)(2,1)} %fusion.20), calls=%async_computation.7 | async-start | bytes 3145728 | tf_op jit(solution)/shard_map/all_to_all | solution.py:840
  201.3 1.7 collective-permute-done.5.late_other
  203.0 34.8 %spread_tokens.1 = (f32[48,25216]{1,0:T(8,128)}, f32[8,128]{1,0:T(8,128)}) custom-call(s32[2]{0:T(128)S(1)} %pad_add_fusion.2.where.refs_0_, s32[32]{0:T(128)S(1)} %pad_add_fusion.3.firsts, s32[4,1,5120]{2,1,0:T(1,128)S(1)} %bitcast.42, bf16[32,72,128]{2,1,0:T(8,128)(2,1)} %copy-done.5, bf16[16,72,128]{2,1,0:T(8,128)(2,1)S(1)} %all_to_all.45.refs_0_.refs_1_.early_own, ...), custom_call_target="tpu_custom_call" | custom-call | flops 1000000000 | bytes 30000000 | tf_op jit(solution)/shard_map/spread_tokens/pallas_call | solution.py:576
  237.8 0.7 fusion.18.refs_1_
  238.5 0.5 collective-permute-start.8
  239.0 3.1 %collective-permute-done.8.refs_5_ = bf16[96,768]{1,0:T(8,128)(2,1)S(1)} collective-permute-done((bf16[96,768]{1,0:T(8,128)(2,1)S(1)}, bf16[96,768]{1,0:T(8,128)(2,1)S(1)}, u32[]{:S(2)}, u32[]{:S(2)}) %collective-permute-start.8) | collective-permute-done | bytes 147488 | tf_op jit(solution)/shard_map/ppermute | solution.py:836
  242.2 0.7 copy-done.14
  242.8 6.0 %grads.1 = (f32[24,2304]{1,0:T(8,128)}, f32[24,768]{1,0:T(8,128)}, f32[24,3072]{1,0:T(8,128)}, f32[96,768]{1,0:T(8,128)}, f32[16,768]{1,0:T(8,128)}, /*index=5*/f32[32,8,128]{2,1,0:T(8,128)}) custom-call(s32[2]{0:T(128)S(1)} %pad_add_fusion.2.where.refs_0_, bf16[16,384,128]{2,1,0:T(8,128)(2,1)S(1)} %fusion.18.refs_1_, ...), custom_call_target="tpu_custom_call" | custom-call | flops 1000000000 | bytes 4755456 | tf_op jit(solution)/shard_map/grads/pallas_call | solution.py:314
  248.8 6.0 %all-to-all-start.8 = ((f32[32,8,128]{2,1,0:T(8,128)}), f32[32,8,128]{2,1,0:T(8,128)S(1)}, u32[]{:S(2)}, u32[]{:S(2)}) async-start(f32[32,8,128]{2,1,0:T(8,128)} %get-tuple-element.139), calls=%async_computation.8 | async-start | bytes 262144 | tf_op jit(solution)/shard_map/all_to_all | solution.py:1100
  255.6 0.1 pad_maximum_fusion.refs_0_
  255.7 0.8 reshape.162
  256.5 6.0 %all-to-all-done.8.refs_5_ = f32[32,8,128]{2,1,0:T(8,128)S(1)} async-done(((f32[32,8,128]{2,1,0:T(8,128)}), f32[32,8,128]{2,1,0:T(8,128)S(1)}, u32[]{:S(2)}, u32[]{:S(2)}) %all-to-all-start.8) | async-done | bytes 131104 | tf_op jit(solution)/shard_map/all_to_all | solution.py:1100
  262.5 15.4 %adam.1 = (f32[1,1]{1,0:T(1,128)}, f32[1,1]{1,0:T(1,128)}, f32[24,2304]{1,0:T(8,128)}, f32[24,2304]{1,0:T(8,128)}, f32[24,2304]{1,0:T(8,128)}, /*index=5*/f32[24...) custom-call(f32[2]{0:T(128)S(1)} %pad_maximum_fusion.refs_0_, ...), custom_call_target="tpu_custom_call" | custom-call | bytes 40730632 | tf_op jit(solution)/shard_map/adam/pallas_call | solution.py:314
  278.0 1.2 multiply_subtract_fusion
  (68 shorter events, 1.1 us)
Async XLA Ops:
  7.2 88.8 %all-gather.5.cloned.1.call-start = ((), (), s32[]{:S(2)}) async-start(), calls=%async_computation.10 | async-start | bytes 4866048 | tf_op jit(solution)/shard_map/all_gather | solution.py:1000
  16.4 21.5 %all-to-all-start = ((bf16[16,72,128]{2,1,0:T(8,128)(2,1)}), bf16[16,72,128]{2,1,0:T(8,128)(2,1)S(1)}, u32[]{:S(2)}, u32[]{:S(2)}) async-start(bf16[16,72,128]{2,1,0:T(8,128)(2,1)} %get-tuple-element.96), calls=%async_computation | async-start | bytes 589824 | tf_op jit(solution)/shard_map/all_to_all | solution.py:840
  24.7 125.6 %all-gather.3.cloned.1.call-start = ((), (), s32[]{:S(2)}) async-start(), calls=%async_computation.9 | async-start | bytes 1216512 | tf_op jit(solution)/shard_map/all_gather | solution.py:1001
  37.9 1.6 collective-permute-start
  40.0 10.7 %copy-start.6 = (f32[96,768]{1,0:T(8,128)S(1)}, f32[96,768]{1,0:T(8,128)}, u32[]{:S(2)}) copy-start(f32[96,768]{1,0:T(8,128)} %refs_20_.1) | copy-start | bytes 884740
  50.6 4.2 %collective-permute-start.1 = (bf16[16,48,640]{2,1,0:T(8,128)(2,1)S(1)}, bf16[16,48,640]{2,1,0:T(8,128)(2,1)S(1)}, u32[]{:S(2)}, u32[]{:S(2)}) collective-permute-start(bf16[16,48,640]{2,1,0:T(8,128)(2,1)S(1)} %lookup.1), channel_id=1, source_target_pairs={{0,16},{16,0},{1,17},{17,1},{2,18},{18,2},{3,19},{19,3},{4,20},{20... | collective-permute-start | bytes 2949128 | tf_op jit(solution)/shard_map/ppermute | solution.py:836
  50.8 2.7 collective-permute-start.2
  66.2 29.7 %all-to-all-start.1 = ((bf16[16,48,640]{2,1,0:T(8,128)(2,1)}), bf16[16,48,640]{2,1,0:T(8,128)(2,1)S(1)}, u32[]{:S(2)}, u32[]{:S(2)}) async-start(bf16[16,48,640]{2,1,0:T(8,128)(2,1)} %lookup_add.1), calls=%async_computation.1 | async-start | bytes 1966080 | tf_op jit(solution)/shard_map/all_to_all | solution.py:840
  70.0 1.1 copy-start.5
  72.1 23.8 %copy-start.7 = (f32[15,768]{1,0:T(8,128)}, f32[15,768]{1,0:T(8,128)S(1)}, u32[]{:S(2)}) copy-start(f32[15,768]{1,0:T(8,128)S(1)} %reshape.164.refs_2_.refs_8_.refs_10_) | copy-start | bytes 138244
  96.0 6.3 %copy-start = (bf16[16,48,640]{2,1,0:T(8,128)(2,1)}, bf16[16,48,640]{2,1,0:T(8,128)(2,1)S(1)}, u32[]{:S(2)}) copy-start(bf16[16,48,640]{2,1,0:T(8,128)(2,1)S(1)} %all-to-all-done.1) | copy-start | bytes 2949124
  149.8 2.2 collective-permute-start.4
  149.8 2.2 collective-permute-start.3
  152.0 7.4 %copy-start.3 = (bf16[16,72,128]{2,1,0:T(8,128)(2,1)}, bf16[16,72,128]{2,1,0:T(8,128)(2,1)S(1)}, u32[]{:S(2)}) copy-start(bf16[16,72,128]{2,1,0:T(8,128)(2,1)S(1)} %collective-permute-done.3.refs_2_.early_other) | copy-start | bytes 884740
  152.0 7.4 %copy-start.2 = (bf16[16,112,128]{2,1,0:T(8,128)(2,1)}, bf16[16,112,128]{2,1,0:T(8,128)(2,1)S(1)}, u32[]{:S(2)}) copy-start(bf16[16,112,128]{2,1,0:T(8,128)(2,1)S(1)} %collective-permute-done.4.refs_4_.p_other) | copy-start | bytes 1376260
  159.5 12.9 %all-to-all-start.5 = ((bf16[16,8,768]{2,1,0:T(8,128)(2,1)}), bf16[16,8,768]{2,1,0:T(8,128)(2,1)S(1)}, u32[]{:S(2)}, u32[]{:S(2)}) async-start(bf16[16,8,768]{2,1,0:T(8,128)(2,1)} %bitcast.16), calls=%async_computation.5 | async-start | bytes 393216 | tf_op jit(solution)/shard_map/all_to_all | solution.py:840
  172.4 1.0 copy-start.1
  173.4 10.7 %copy-start.12 = (bf16[384,192]{1,0:T(8,128)(2,1)S(1)}, bf16[384,192]{1,0:T(8,128)(2,1)}, u32[]{:S(2)}) copy-start(bf16[384,192]{1,0:T(8,128)(2,1)} %get-tuple-element.133) | copy-start | bytes 442372
  180.5 15.6 %all-to-all-start.6 = ((bf16[16,96,128]{2,1,0:T(8,128)(2,1)}), bf16[16,96,128]{2,1,0:T(8,128)(2,1)S(1)}, u32[]{:S(2)}, u32[]{:S(2)}) async-start(bf16[16,96,128]{2,1,0:T(8,128)(2,1)} %get-tuple-element.127.refs_6_), calls=%async_computation.6 | async-start | bytes 786432 | tf_op jit(solution)/shard_map/all_to_all | solution.py:840
  184.1 1.5 collective-permute-start.6
  185.6 0.7 copy-start.8
  197.4 5.6 %copy-start.4 = (bf16[16,72,128]{2,1,0:T(8,128)(2,1)S(1)}, bf16[16,72,128]{2,1,0:T(8,128)(2,1)}, u32[]{:S(2)}) copy-start(bf16[16,72,128]{2,1,0:T(8,128)(2,1)} %copy-done.3) | copy-start | bytes 884740
  197.4 40.5 %all-to-all-start.7 = ((bf16[16,384,128]{2,1,0:T(8,128)(2,1)}), bf16[16,384,128]{2,1,0:T(8,128)(2,1)S(1)}, u32[]{:S(2)}, u32[]{:S(2)}) async-start(bf16[16,384,128]{2,1,0:T(8,128)(2,1)} %fusion.20), calls=%async_computation.7 | async-start | bytes 3145728 | tf_op jit(solution)/shard_map/all_to_all | solution.py:840
  201.2 1.8 collective-permute-start.5
  203.0 35.5 %copy-start.13 = (bf16[96,768]{1,0:T(8,128)(2,1)S(1)}, bf16[96,768]{1,0:T(8,128)(2,1)}, u32[]{:S(2)}) copy-start(bf16[96,768]{1,0:T(8,128)(2,1)} %get-tuple-element.137) | copy-start | bytes 442372
  238.5 3.6 %collective-permute-start.7 = (bf16[16,384,128]{2,1,0:T(8,128)(2,1)S(1)}, bf16[16,384,128]{2,1,0:T(8,128)(2,1)S(1)}, u32[]{:S(2)}, u32[]{:S(2)}) collective-permute-start(bf16[16,384,128]{2,1,0:T(8,128)(2,1)S(1)} %fusion.18.refs_1_), channel_id=1, source_target_pairs={{0,16},{16,0},{1,17},{17,1},{2,18},{18,2},{3,19},{19,3},{4,20},{20... | collective-permute-start | bytes 4718600 | tf_op jit(solution)/shard_map/ppermute | solution.py:836
  238.5 3.6 %collective-permute-start.8 = (bf16[96,768]{1,0:T(8,128)(2,1)S(1)}, bf16[96,768]{1,0:T(8,128)(2,1)S(1)}, u32[]{:S(2)}, u32[]{:S(2)}) collective-permute-start(bf16[96,768]{1,0:T(8,128)(2,1)S(1)} %copy-done.13), channel_id=1, source_target_pairs={{0,16},{16,0},{1,17},{17,1},{2,18},{18,2},{3,19},{19,3},{4,20},{20... | collective-permute-start | bytes 442376 | tf_op jit(solution)/shard_map/ppermute | solution.py:836
  242.2 0.7 copy-start.14
  248.8 13.7 %all-to-all-start.8 = ((f32[32,8,128]{2,1,0:T(8,128)}), f32[32,8,128]{2,1,0:T(8,128)S(1)}, u32[]{:S(2)}, u32[]{:S(2)}) async-start(f32[32,8,128]{2,1,0:T(8,128)} %get-tuple-element.139), calls=%async_computation.8 | async-start | bytes 262144 | tf_op jit(solution)/shard_map/all_to_all | solution.py:1100
  262.5 15.4 %copy-start.9 = (f32[360]{0:T(512)S(1)}, f32[360]{0:T(512)}, u32[]{:S(2)}) copy-start(f32[360]{0:T(512)} %param.57) | copy-start | bytes 4324
  262.5 15.4 %copy-start.10 = (f32[360]{0:T(512)S(1)}, f32[360]{0:T(512)}, u32[]{:S(2)}) copy-start(f32[360]{0:T(512)} %param.58) | copy-start | bytes 4324
  262.5 15.4 %copy-start.11 = (f32[360]{0:T(512)S(1)}, f32[360]{0:T(512)}, u32[]{:S(2)}) copy-start(f32[360]{0:T(512)} %param.59) | copy-start | bytes 4324
Sparse Core Ops, SparseCore 0:
  11.5 75.4 all-gather.4
  90.5 52.4 all-gather.2

commit v2 on v1

--- a/solution.py
+++ b/solution.py
@@ -324,6 +324,19 @@
     )(*scalars, *(pinned(a) for a in far), *args, *after)
 
 
+def once(x, other):
+    anywhere = pl.BlockSpec(memory_space=pl.ANY)
+    return pl.pallas_call(
+        lambda *refs: None,
+        out_shape=pltpu.HBM(x.shape, x.dtype),
+        in_specs=[anywhere, anywhere],
+        out_specs=anywhere,
+        input_output_aliases={0: 0},
+        compiler_params=pltpu.CompilerParams(vmem_limit_bytes=MIB),
+        name="once",
+    )(pinned(x), other)
+
+
 def square_weights(mats, first, buffers, signals, order):
     copies = {
         k: pltpu.make_async_copy(mats.at[:, pl.ds(k * D, D)], buffers.at[k - first], signals.at[k - first]) for k in order
@@ -345,10 +358,12 @@
     return [pltpu.VMEM((count, D, D), bf16), pltpu.SemaphoreType.DMA((count,))]
 
 
-def prepare_kernel(group_rows, count, rows, base, vectors, seq, pos, up, packet, moved):
+def prepare_kernel(group_rows, rows, passages, queries, negatives, small, vectors, seq, pos, up, packet, moved):
+    line_up = lambda ref: [ref[k : k + 1, :] for k in range(ref.shape[0])]
+    ids = jnp.concatenate(line_up(passages) + line_up(queries), 1)
+    count = ids.shape[1]
     chunks = count // LANES
-    ids = jnp.concatenate([base[k : k + 1, :] for k in range(chunks)], 1)
-    entries = base[chunks : chunks + 1, :]
+    entries = small[...]
     live = jnp.zeros((1, count), f32)
     for number in range(rows):
         live = jnp.where((seq[...] == number) & (pos[...] < entries[:, number : number + 1]), 1.0, live)
@@ -356,11 +371,17 @@
     moved[...] = got
     code = got[2:3] + 8.0 * got[3:4]
     lane = iota((1, LANES), 1)
+    at = 1 + 2 * queries.shape[0]
+    after = LANES - at - negatives.shape[0] * negatives.shape[1]
+    rest = [jnp.zeros((1, at), jnp.int32)] + line_up(negatives) + [jnp.zeros((1, after), jnp.int32)]
     note = pltpu.roll(entries.astype(f32), LANES - rows + 1, 1)
+    note = jnp.where((lane < at) | (lane == LANES - 1), note, jnp.concatenate(rest, 1).astype(f32))
     high = lax.shift_right_logical(total.astype(jnp.int32), 8)
     note = jnp.where(lane == 0, total - 256.0 * high.astype(f32), jnp.where(lane == LANES - 1, high.astype(f32), note))
     lines = [line[:, k * LANES : (k + 1) * LANES] for line in (got[0:1], got[1:2], code) for k in range(chunks)]
-    lines += [note] + [vectors[k : k + 1, :] for k in range(vectors.shape[0])]
+    own = vectors.shape[1]
+    given = jnp.concatenate([vectors[...], jnp.zeros((1, -own % LANES), f32)], 1)
+    lines += [note] + [given[:, k : k + LANES] for k in range(0, given.shape[1], LANES)]
     wide, block = packet.shape[0], up.shape[0]
     hidden = up.shape[1] // (2 * wide)
     first = packet.shape[1] - 2 * block
@@ -374,10 +395,11 @@
         packet[dest] = jnp.concatenate([whole] + pieces, 0).astype(bf16)
 
 
-def cast_kernel(attn_in, attn_out, head, out, head_out):
+def cast_kernel(attn_in, attn_out, head, down, out, down_out):
+    down_out[...] = down[...].astype(bf16)
     out[:, : 3 * D] = attn_in[...].astype(bf16)
     out[:, 3 * D : 4 * D] = attn_out[...].astype(bf16)
-    head_out[...] = head[...].astype(bf16)
+    out[:, 4 * D :] = head[...].astype(bf16)
 
 
 def build_kernel(emb, table):
@@ -421,13 +443,11 @@
     return pl.BlockSpec((1, 1, per * count), lambda i, *s: (i, 0, 0), memory_space=pltpu.SMEM)
 
 
-def lookup_kernel(half_rows, per, unroll, add, where, firsts, numbers, packet, table, *refs):
-    out, buf = refs[-2:]
+def lookup_kernel(half_rows, per, unroll, where, firsts, numbers, packet, table, out, buf):
     feats, count = out.shape[1:]
     group = where[0]
     chunks = count // LANES
     half = table.shape[0]
-    eye = jnp.where(iota((LANES, LANES), 0) == iota((LANES, LANES), 1), 1.0, 0.0).astype(bf16)
     at = pl.program_id(0) * per
     for s in range(per):
         low, high = own_span(firsts[at + s], group, count)
@@ -441,11 +461,10 @@
         lax.fori_loop(low // unroll, (high + unroll - 1) // unroll, step, 0)
     for s in range(per):
         side = side_of(packet, s, chunks, group, half_rows, half)
-        turned = dot(eye, buf[s * count : (s + 1) * count, :].astype(bf16), 1, 1)
+        lines = [buf[s * count + c * LANES : s * count + (c + 1) * LANES, :].astype(bf16).T for c in range(chunks)]
+        turned = jnp.concatenate(lines, 1).astype(f32)
         pick = jnp.where(side > 1.5, turned[SIDE : SIDE + feats], turned[:feats])
         value = jnp.where(side > 0.5, pick, 0.0)
-        if add:
-            value = value + refs[0][s].astype(f32)
         out[s] = value.astype(bf16)
 
 
@@ -453,27 +472,26 @@
     return jnp.concatenate([packet[s, first + c : first + c + 1, :].astype(f32) for c in range(chunks)], 1)
 
 
-def lookup(where, numbers, firsts, packets, table, half_rows, feats, count, add=None, per=4, unroll=32):
+def lookup(where, numbers, firsts, packets, table, half_rows, feats, count, per=4, unroll=64):
     sources = packets.shape[0]
     some = lambda dims: pl.BlockSpec((per,) + dims, lambda i, *s: (i, 0, 0))
-    extra = [] if add is None else [add]
     return pl.pallas_call(
-        partial(lookup_kernel, half_rows, per, unroll, add is not None),
+        partial(lookup_kernel, half_rows, per, unroll),
         out_shape=shape((sources, feats, count), bf16),
         grid_spec=pltpu.PrefetchScalarGridSpec(
             num_scalar_prefetch=2,
             grid=(sources // per,),
-            in_specs=[number_block(per, count), some(packets.shape[1:]), pl.BlockSpec(table.shape, lambda i, *s: (0, 0), pipeline_mode=pl.Buffered(1))] + [some((feats, count)) for _ in extra],
+            in_specs=[number_block(per, count), some(packets.shape[1:]), pl.BlockSpec(table.shape, lambda i, *s: (0, 0), pipeline_mode=pl.Buffered(1))],
             out_specs=some((feats, count)),
             scratch_shapes=[pltpu.VMEM((per * count, LANES), f32)],
         ),
         compiler_params=pltpu.CompilerParams(vmem_limit_bytes=16 * MIB),
         cost_estimate=pl.CostEstimate(flops=10**9, bytes_accessed=10**7, transcendentals=0),
-        name="lookup" if add is None else "lookup_add",
-    )(where, firsts, numbers.reshape(-1, 1, per * count), packets, pinned(table), *extra)
-
-
-def spread_kernel(rows, half_rows, feats, per, unroll, copies, at_early, at_heads, where, firsts, numbers, packet, early_own, early_other, late_own, late_other, p_own, p_other, out, square, *scratch):
+        name="lookup",
+    )(where, firsts, numbers.reshape(-1, 1, per * count), packets, pinned(table))
+
+
+def spread_kernel(rows, half_rows, feats, per, unroll, copies, at_early, where, firsts, numbers, packet, early_own, early_other, late_own, late_other, p_heads, out, square, *scratch):
     parts, buf = scratch[:copies], scratch[copies]
     group = where[0]
     chunks = buf.shape[0] // (per * LANES)
@@ -492,7 +510,6 @@
 
         lax.fori_loop(0, blocks, clear, 0)
 
-    eye = flag(iota((LANES, LANES), 0) == iota((LANES, LANES), 1)).astype(bf16)
     gap = jnp.zeros((SIDE - feats, count), f32)
     block = feats // 2
     lane, slot = iota((LANES, 2 * LANES), 0), iota((LANES, 2 * LANES), 1)
@@ -511,7 +528,7 @@
         slot0 = code >= 8.0
         seq = jnp.where(slot0, code - 8.0, code)
         scores = unpack_heads(pick(late_own, late_other, s, block + ROWS, head_lines(chunks)), chunks)
-        values = unpack_heads(pick(p_own, p_other, s, at_heads, head_lines(chunks)), chunks)
+        values = unpack_heads(p_heads[s, : head_lines(chunks), :], chunks)
         parts_of = [jnp.where(seq == float(r), scores, 0.0) for r in range(rows)] + [empty]
         parts_of += [jnp.where(seq == float(r), values, 0.0) for r in range(rows)] + [empty]
         both = jnp.concatenate([pick(early_own, early_other, s, at_early, block), pick(late_own, late_other, s, 0, block)], 0)
@@ -524,7 +541,7 @@
         tall = jnp.concatenate([jnp.where(side == 1.0, x, 0.0), gap, jnp.where(side == 2.0, x, 0.0), gap], 0).astype(bf16)
         for c in range(chunks):
             start = s * count + c * LANES
-            buf[start : start + LANES, :] = dot(eye, tall[:, c * LANES : (c + 1) * LANES], 1, 1)
+            buf[start : start + LANES, :] = tall[:, c * LANES : (c + 1) * LANES].T.astype(f32)
     for s in range(per):
         low, high = own_span(firsts[step_at * per + s], group, count)
 
@@ -571,35 +588,37 @@
     half = -(-half_rows // (2 * LANES)) * LANES
     some = lambda dims: pl.BlockSpec((per,) + dims, lambda i, *s: (i, 0, 0))
     steps = devices // per
+    ordered = pl.BlockSpec((per, head_lines(count // LANES), LANES), lambda i, where, *s: ((i + where[0] * (steps // 2)) % steps, 0, 0))
     mine = lambda pair: pl.BlockSpec((per,) + pair[0].shape[1:], lambda i, *s: (jnp.minimum(i, steps // 2 - 1), 0, 0))
     theirs = lambda pair: pl.BlockSpec((per,) + pair[0].shape[1:], lambda i, *s: (jnp.maximum(i - steps // 2, 0), 0, 0))
     return pl.pallas_call(
-        partial(spread_kernel, rows, half_rows, feats, per, unroll, copies, at_early, at_early),
+        partial(spread_kernel, rows, half_rows, feats, per, unroll, copies, at_early),
         out_shape=[pltpu.HBM((feats, half_rows), f32), pltpu.HBM((ROWS, LANES), f32)],
         grid_spec=pltpu.PrefetchScalarGridSpec(
             num_scalar_prefetch=2,
             grid=(steps,),
-            in_specs=[number_block(per, count), some(block), mine(early), theirs(early), mine(late), theirs(late), mine(p_heads), theirs(p_heads)],
+            in_specs=[number_block(per, count), some(block), mine(early), theirs(early), mine(late), theirs(late), ordered],
             out_specs=[pl.BlockSpec((feats, half_rows), lambda i, *s: (0, 0), pipeline_mode=pl.Buffered(1)), pl.BlockSpec((ROWS, LANES), lambda i, *s: (0, 0))],
             scratch_shapes=[pltpu.VMEM((half, LANES), f32)] * copies + [pltpu.VMEM((per * count, LANES), f32)],
         ),
         compiler_params=pltpu.CompilerParams(vmem_limit_bytes=52 * MIB),
         cost_estimate=pl.CostEstimate(flops=10**9, bytes_accessed=3 * 10**7, transcendentals=0),
         name="spread_tokens",
-    )(where, firsts, numbers.reshape(-1, 1, per * count), packets, *early, *late, *p_heads)
-
-
-def attend_kernel(rows, mats, xt, vec, moved, sent, heads_out, facts, y_out, probs_out, psum_out, normed_out, inv_out, *scratch):
+    )(where, firsts, numbers.reshape(-1, 1, per * count), packets, *early, *late, p_heads)
+
+
+def attend_kernel(rows, mats, xt, vec, moved, sent, early, known, y_out, probs_out, psum_out, normed_out, inv_out, *scratch):
     w = square_weights(mats, 0, *scratch, (0, 1, 2, 3))
     x1, x00, q, o, probs, psum, normed, inv, qk, y = attend(xt[...], w, vec[...], moved[...], rows)
     tiles = to_tiles(x1)
-    halves = both_halves(qk, rows)
+    halves, heads = both_halves(qk, rows), pack_heads(probs.astype(bf16), rows)
     wide = sent.shape[0]
     block = D // (2 * wide)
     for dest in range(wide):
-        sent[dest] = jnp.concatenate([tiles, table_block(halves, dest, block)], 0).astype(bf16)
-    heads_out[...] = pack_heads(probs.astype(bf16), rows)
-    facts[...] = jnp.concatenate([to_tiles(value.astype(f32)) for value in (x00, q, o)], 0).astype(bf16)
+        sent[dest] = tiles.astype(bf16)
+        early[dest] = table_block(halves, dest, block).astype(bf16)
+    facts = jnp.concatenate([to_tiles(value.astype(f32)) for value in (x00, q, o)], 0).astype(bf16)
+    known[...] = jnp.concatenate([heads, facts], 0)
     y_out[...] = y.astype(bf16)
     probs_out[...], psum_out[...], normed_out[...], inv_out[...] = probs, psum, normed, inv
 
@@ -610,8 +629,11 @@
     block = D // (2 * wide)
     feats = 2 * block
     dx1 = d_res2[pl.ds(pl.multiple_of(place[0] * ROWS, ROWS), ROWS), :]
-    for k in range(wide):
-        dx1 = dx1 + got[k].astype(f32)
+    lines = ROWS * (D // LANES)
+    tiles = got[0, :lines, :].astype(f32)
+    for k in range(1, wide):
+        tiles = tiles + got[k, :lines, :].astype(f32)
+    dx1 = dx1 + jnp.concatenate([tiles[k : k + ROWS] for k in range(0, lines, ROWS)], 1)
     d_a, d_o, d_q, sums, vd, z, extra, ds = attend_back(
         dx1, normed[...], inv[...], probs[...], psum[...], xt[...], w, vec[...], rows
     )
@@ -631,11 +653,11 @@
     last[...] = jnp.concatenate([to_tiles(value) for value in values], 0).astype(bf16)
 
 
-def pack_kernel(rows, facts, last, y, z, d_up, d_up_other, out):
+def pack_kernel(rows, last, y, z, d_up, d_up_other, out):
     wide = out.shape[0]
     block = d_up.shape[0] // wide
     hidden = d_up.shape[1] // 2
-    values = jnp.concatenate([facts[...], last[...]], 0)
+    values = last[...]
     halves_y, halves_z = both_halves(y[...], rows), both_halves(z[...], rows)
     up = d_up[...] + d_up_other[...].astype(f32)
     gap = jnp.zeros((block, LANES - hidden), f32)
@@ -650,31 +672,37 @@
     return jnp.concatenate([from_tiles(own[...], 0), from_tiles(other[...], 0)], 0)
 
 
-def ffn_kernel(x_own, w_up, w_down, bias, u_out, h_out, out):
-    u, h, f = ffn(from_tiles(x_own[...], 0), w_up[...], w_down[...], bias[...])
+def by_core(where, own, other):
+    first = where[0] == 0
+    return jnp.concatenate([jnp.where(first, own[...], other[...]), jnp.where(first, other[...], own[...])], 0)
+
+
+def ffn_kernel(where, x_own, w_up, down_own, down_other, bias, u_out, h_out, out):
+    u, h, f = ffn(from_tiles(x_own[...], 0), w_up[...], by_core(where, down_own, down_other), bias[...])
     u_out[...], h_out[...] = u, h
     out[...] = f.astype(bf16)
 
 
-def total_kernel(got, heads, out):
+def total_kernel(got, out):
     total = got[0].astype(f32)
     for k in range(1, got.shape[0]):
         total = total + got[k].astype(f32)
-    lines = jnp.concatenate([to_tiles(total).astype(bf16), heads[...]], 0)
+    lines = to_tiles(total).astype(bf16)
     for k in range(out.shape[0]):
         out[k] = lines
 
 
-def middle_kernel(mats, x_own, x_other, f_own, f_other, u, w_up, w_down, vec, picks, loss, pooled, d_c, d_res2, d_f, d_u, out, sums, sums_up, *scratch):
-    get = square_weights(mats, 0, *scratch, (0,))
-    w = lambda k: get(0)
+def middle_kernel(where, mats, x_own, x_other, f_own, f_other, u, w_up, down_own, down_other, vec, picks, early, loss, pooled, d_c, d_res2, d_f, d_u, out, sums, sums_up, *scratch):
+    w = square_weights(mats, 4, *scratch, (4,))
     x1 = rows_of(x_own, x_other).astype(f32)
     f = rows_of(f_own, f_other).astype(f32)
-    got = middle(x1, f, u[...], w_up[...], w_down[...], w, vec[...], picks[...])
+    got = middle(x1, f, u[...], w_up[...], by_core(where, down_own, down_other), w, vec[...], picks[...])
     lines = u.shape[0]
     loss[...], pooled[...], d_c[...], d_res2[...] = got[:4]
     d_f[...], d_u[...] = got[4][:lines], got[5]
-    out[...] = got[6].astype(bf16)
+    for dest in range(out.shape[0]):
+        part = to_tiles(got[6][dest * ROWS : (dest + 1) * ROWS]).astype(bf16)
+        out[dest] = jnp.concatenate([part, early[dest]], 0)
     sums[...] = stack_rows(got[7])
     su = jnp.sum(got[5].astype(f32), 0, keepdims=True)
     sums_up[...] = jnp.concatenate([su, jnp.zeros((1, D - su.shape[1]), f32)], 1)
@@ -703,7 +731,7 @@
     d_head[...] = own_rows(pooled[...], d_c[...], own_cols(where[1], block), block)
 
 
-def grads_kernel(rows, where, facts_own, facts_other, d_wh, down_mine, down_other, sums, square, in_out, out_out, up_out, down_out, vec_out, square_out, x00, q_all, o_all, d_q, d_o, d_a, y, z, wide_z):
+def grads_kernel(rows, where, known, facts_own, facts_other, d_wh, down_mine, down_other, sums, square, in_out, out_out, up_out, down_out, vec_out, square_out, x00, q_all, o_all, d_q, d_o, d_a, y, z, wide_z):
     group, device = where[0], where[1]
     wide = facts_own.shape[0]
     devices = 2 * wide
@@ -711,10 +739,13 @@
     hidden = FF // devices
     first = group == 0
     lines = ROWS * (D // LANES)
-    at_up = 6 * lines
+    at_up = 3 * lines
     for base, facts in ((0, facts_own), (1, facts_other)):
         at = slice(base * wide * ROWS, (base + 1) * wide * ROWS)
-        for k, out in enumerate((x00, q_all, o_all, d_q, d_o, d_a)):
+        kept = known[pl.ds(((base + group) % 2) * wide, wide), known.shape[1] - 3 * lines :, :]
+        for k, out in enumerate((x00, q_all, o_all)):
+            out[at, :] = from_tiles(kept, k * lines).astype(f32)
+        for k, out in enumerate((d_q, d_o, d_a)):
             out[at, :] = from_tiles(facts, k * lines).astype(f32)
         for n in range(wide):
             at = slice((base * wide + n) * block, (base * wide + n + 1) * block)
@@ -981,26 +1012,25 @@
     vec_lines = -(-vectors.shape[0] // LANES)
     packet_lines = -(-(3 * chunks + 1 + vec_lines) // ROWS) * ROWS + 2 * block
     at_note = 3 * chunks
-    pieces = [passage_ids.reshape(-1), query_ids.reshape(-1), passage_len, query_len, valid, positive, negatives.reshape(-1)]
+    pieces = [passage_len, query_len, valid, positive]
     size = sum(t.shape[0] for t in pieces)
-    assert size < tokens + LANES
-    base = jnp.concatenate(pieces + [jnp.zeros((-size % (ROWS * LANES),), jnp.int32)]).reshape(-1, LANES)
-    vec_pad = jnp.concatenate([vectors, jnp.zeros((-vectors.shape[0] % LANES,), f32)]).reshape(-1, LANES)
+    assert size + negatives.size < LANES - 1
+    small = jnp.concatenate(pieces + [jnp.zeros((LANES - size,), jnp.int32)])[None]
     packet, moved = call(
-        partial(prepare_kernel, half_rows, tokens, rows),
+        partial(prepare_kernel, half_rows, rows),
         [shape((wide, packet_lines, LANES), bf16), shape((ROWS, tokens))],
-        base, vec_pad, jnp.asarray(seq_np, jnp.int32)[None], jnp.asarray(pos_np, jnp.int32)[None], w_ffn_up,
+        passage_ids, query_ids, negatives, small, vectors[None], jnp.asarray(seq_np, jnp.int32)[None], jnp.asarray(pos_np, jnp.int32)[None], w_ffn_up,
         near_outs=(0,), name="prepare",
     )
     packet_own = exchange(packet)
     (table,) = call(build_kernel, [shape((half, LANES))], embedding, name="build", flops=10**8)
     packet_own, table = tie(packet_own, table)
     packet_other = swap(packet_own)
-    low_mats, low_head = call(cast_kernel, [shape((block, 4 * D), bf16), shape((block, D), bf16)], attn_in, attn_out, head, near_outs=(0, 1), name="cast")
+    low_mats, down_low = call(
+        cast_kernel, [shape((block, 5 * D), bf16), shape((hidden, D), bf16)],
+        attn_in, attn_out, head, w_ffn_down, near_outs=(0,), name="cast",
+    )
     mats = lax.all_gather(low_mats, ALL, axis=0, tiled=True)
-    w_head = lax.all_gather(low_head, ALL, axis=0, tiled=True)
-    down_low = w_ffn_down.astype(bf16)
-    w_down = in_order(down_low, swap(down_low), group)
 
     def numbers_of(packets):
         ids = packets[:, :chunks].astype(f32) * 256.0 + packets[:, chunks : 2 * chunks].astype(f32)
@@ -1012,7 +1042,7 @@
     look = partial(lookup, half_rows=half_rows, feats=feats, count=tokens)
     num_own, num_other = numbers_of(packet_own), numbers_of(packet_other)
     theirs = look(where, *num_other, packet_other, table)
-    xt = exchange(look(where, *num_own, packet_own, table, add=swap(theirs))).reshape(D, tokens)
+    xt = exchange(look(where, *num_own, packet_own, table) + swap(theirs)).reshape(D, tokens)
     numbers = jnp.concatenate([num_own[0], num_other[0]])
     firsts = jnp.concatenate([num_own[1], num_other[1]])
     packets = jnp.concatenate([packet_own, packet_other], 0)
@@ -1032,38 +1062,40 @@
     pick_row = jnp.concatenate([notes[:, 1 : 1 + qry_count, None].astype(jnp.int32), pick_row], 2)
     pick_rows = jnp.pad(pick_row, ((0, 0), (pas_count, ROWS - rows), (0, 0))).reshape(devices * ROWS, -1)
 
-    xt, vec, bias_up, pick_rows, w_up, w_down, packets, numbers, firsts = tie(
-        xt, vec, bias_up, pick_rows, w_up, w_down, packets, numbers, firsts
-    )
+    xt, vec, bias_up, pick_rows, w_up, packets, numbers, firsts = tie(xt, vec, bias_up, pick_rows, w_up, packets, numbers, firsts)
     tile_lines = ROWS * (D // LANES)
     heads_at, units = head_lines(chunks), 2 * hidden
-    sent, p_heads, facts, y, probs, psum, normed1, inv1 = call(
+    sent, early, known, y, probs, psum, normed1, inv1 = call(
         partial(attend_kernel, rows),
         [
-            shape((wide, tile_lines + block, LANES), bf16), shape((heads_at, LANES), bf16), shape((3 * tile_lines, LANES), bf16),
+            shape((wide, tile_lines, LANES), bf16), shape((wide, block, LANES), bf16), shape((heads_at + 3 * tile_lines, LANES), bf16),
             shape((SIDE, D), bf16), shape((SIDE, tokens)), shape((SIDE, 1)), shape((ROWS, D)), shape((ROWS, 1)),
         ],
         xt, vec, moved,
         far=(mats,), near=(0,), near_outs=(0,), scratch=weight_scratch(4), name="attend", flops=10**9,
     )
     x_own, x_other = pair(sent)
+    known_all = lax.all_gather(known, ALL, axis=0, tiled=False)
+    down_other = swap(down_low)
     u, h, f_mine = call(
-        ffn_kernel, [shape((lines, units)), shape((lines, units), bf16), shape((lines, D), bf16)], x_own, w_up, w_down, bias_up,
-        near=(0,), near_outs=(2,), name="ffn", flops=10**8, vmem=16,
+        ffn_kernel, [shape((lines, units)), shape((lines, units), bf16), shape((lines, D), bf16)], x_own, w_up, down_low, down_other, bias_up,
+        scalars=(where,), near=(0, 3), near_outs=(2,), name="ffn", flops=10**8, vmem=16,
     )
     f_parts = exchange(f_mine.reshape(wide, ROWS, D))
-    (f_sum,) = call(total_kernel, [shape((wide, tile_lines + heads_at, LANES), bf16)], f_parts, p_heads, near=(0,), near_outs=(0,), name="total")
+    (f_sum,) = call(total_kernel, [shape((wide, tile_lines, LANES), bf16)], f_parts, near=(0,), near_outs=(0,), name="total")
     f_own, f_other = pair(f_sum)
     loss, pooled, d_c, d_res2, d_f, d_u, d_sum, sums, sums_up = call(
         middle_kernel,
         [
             shape((1, 1)), shape((devices * ROWS, D), bf16), shape((devices * ROWS, D), bf16), shape((devices * ROWS, D)),
-            shape((lines, D), bf16), shape((lines, units), bf16), shape((lines, D), bf16), shape((ROWS, D)), shape((1, D)),
+            shape((lines, D), bf16), shape((lines, units), bf16), shape((wide, tile_lines + block, LANES), bf16),
+            shape((ROWS, D)), shape((1, D)),
         ],
-        x_own, x_other, f_own, f_other, u, w_up, w_down, vec, pick_rows,
-        far=(w_head,), scratch=weight_scratch(1), near=(0, 1, 2, 3), near_outs=(6,), name="middle", flops=10**9, vmem=32,
-    )
-    got = exchange(d_sum.reshape(wide, ROWS, D))
+        x_own, x_other, f_own, f_other, u, w_up, down_low, down_other, vec, pick_rows, early,
+        scalars=(where,), far=(mats,), scratch=weight_scratch(1), near=(0, 1, 2, 3), near_outs=(6,), name="middle", flops=10**9, vmem=32,
+    )
+    got = exchange(d_sum)
+    got_other = swap(got)
     down_mine, down_theirs, d_whead, up_mine, up_theirs = call(
         ffn_grads_kernel,
         [shape((hidden, D)), shape((hidden, D), bf16), shape((block, D)), shape((D // 2, units)), shape((D // 2, units), bf16)],
@@ -1074,17 +1106,16 @@
         partial(attend_back_kernel, rows),
         [shape((wide, block + ROWS + heads_at, LANES), bf16), shape((3 * tile_lines, LANES), bf16), shape((SIDE, D), bf16)],
         got, d_res2, sums_up, normed1, inv1, probs, psum, xt, vec,
-        scalars=(place_at,), far=(mats,), after=(up_mine,), near=(0,), near_outs=(0,), scratch=weight_scratch(4), name="attend_back", flops=10**9,
+        scalars=(place_at,), far=(mats,), after=(pinned(up_mine),), near=(0,), near_outs=(0,), scratch=weight_scratch(4), name="attend_back", flops=10**9,
     )
     late_own, late_other = pair(late)
     (packed,) = call(
-        partial(pack_kernel, rows), [shape((wide, 6 * tile_lines + 4 * block, LANES), bf16)], facts, last, y, z, up_mine, swap(up_theirs),
-        after=(late,), near_outs=(0,), name="pack",
-    )
-    piece = packed[:1, :ROWS] + late_own[:1, :ROWS] * jnp.zeros((), bf16)
-    last_own = exchange(lax.dynamic_update_slice(packed, piece, (0, 0, 0)))
+        partial(pack_kernel, rows), [shape((wide, 3 * tile_lines + 4 * block, LANES), bf16)], last, y, z, up_mine, swap(up_theirs),
+        after=(late,), near=(4,), name="pack",
+    )
+    last_own = exchange(once(packed, late_own))
     d_table, square = spread_tokens(
-        where, numbers, firsts, packets, (x_own, x_other), (late_own, late_other), (f_own, f_other), tile_lines, rows, half_rows, feats, tokens
+        where, numbers, firsts, packets, (got, got_other), (late_own, late_other), known_all, tile_lines, rows, half_rows, feats, tokens
     )
     piece = last_own[:1, :ROWS] + (square[None] * 0.0).astype(bf16)
     last_own = lax.dynamic_update_slice(last_own, piece, (0, 0, 0))
@@ -1092,10 +1123,10 @@
     d_attn_in, d_wo, d_wup, d_down, d_vec, squares = call(
         partial(grads_kernel, rows),
         [shape((block, 3 * D)), shape((block, D)), shape((block, FF)), shape((hidden, D)), shape((16, D)), shape((devices, ROWS, LANES))],
-        last_own, last_other, d_whead, down_mine, swap(down_theirs), sums, square,
+        known_all, last_own, last_other, d_whead, down_mine, swap(down_theirs), sums, square,
         scalars=(where,),
         scratch=[pltpu.VMEM((devices * ROWS, D), f32)] * 6 + [pltpu.VMEM((D, LANES), f32)] * 2 + [pltpu.VMEM((D, D), f32)],
-        near=(0, 1), near_outs=(5,), name="grads", flops=10**9, vmem=32,
+        near=(1, 2, 5), near_outs=(5,), name="grads", flops=10**9, vmem=32,
     )
     squares_got = lax.all_to_all(squares, ALL, split_axis=0, concat_axis=0, tiled=True)
     d_vectors = lax.dynamic_slice(d_vec.reshape(-1), (device * vectors.shape[0],), vectors.shape)

time: 290 us -> 279 us (0.962)
  blocking collectives: 44.7 us -> 11.2 us
  waiting for transfers between devices: 59.4 us -> 87.1 us
  starting transfers between devices: 31.2 us -> 40.5 us
  Pallas kernels: 119 us -> 110 us
  local copies, waits for them, and re-layouts: 10.8 us -> 6.83 us
    all_to_all x3 -> x1, blocking collectives: 44.7 us -> 11.2 us  [exchange(): return lax.all_to_all(x, 'wide', split_axis=0, concat_axis=0, tiled=True)]
    all_to_all x5 -> x7, waiting for transfers between devices: 41.7 us -> 70.2 us  [exchange(): return lax.all_to_all(x, 'wide', split_axis=0, concat_axis=0, tiled=True)]
    all_to_all x5 -> x7, starting transfers between devices: 23.3 us -> 34.1 us  [exchange(): return lax.all_to_all(x, 'wide', split_axis=0, concat_axis=0, tiled=True)]
    pallas_call x1, Pallas kernels: 34.8 us -> 28.3 us  [spread_tokens(): pl.pallas_call(partial(spread_kernel, rows, half_rows, feats, per, unroll...]
    pallas_call x2 -> x3, Pallas kernels: 22.1 us -> 19.4 us  [the longest x2 19.4 us: lookup(): pl.pallas_call(partial(lookup_kernel, half_rows, per, unroll), out_shape=...]
    ppermute x9 -> x10, waiting for transfers between devices: 11.6 us -> 9.71 us  [swap(): return lax.ppermute(x, 'group', [(0, 1), (1, 0)])]
  transfers between devices with their start and end apart: 17 -> 20, of which waited for: 11 -> 14; matrix products, arithmetic and copies ran while one was open for 4% -> 4% of each run, Pallas kernels for 28% -> 28%
where the time goes in v2:
time: 279 us; the launch traced here: 277 us
  Pallas kernels  110 us (39%)
  waiting for transfers between devices  87.1 us (31%)
  starting transfers between devices  40.5 us (15%)
  between operations  15.9 us (6%)
  blocking collectives  11.2 us (4%)
  local copies, waits for them, and re-layouts  6.83 us (2%)
  other arithmetic  5.87 us (2%)
    all_to_all x7, waiting for transfers between devices, exchange(): return lax.all_to_all(x, 'wide', split_axis=0, concat_axis=0, tiled=True)  70.2 us
    pallas_call x12, Pallas kernels, call(): pl.pallas_call(run, grid=(1,), out_shape=shapes, in_specs=in_specs, out_s...  62 us
    all_to_all x7, starting transfers between devices, exchange(): return lax.all_to_all(x, 'wide', split_axis=0, concat_axis=0, tiled=True)  34.1 us
    pallas_call x1, Pallas kernels, spread_tokens(): pl.pallas_call(partial(spread_kernel, rows, half_rows, feats, per, unroll...  28.3 us
    pallas_call x2, Pallas kernels, lookup(): pl.pallas_call(partial(lookup_kernel, half_rows, per, unroll), out_shape=...  19.4 us
    all_to_all x1, blocking collectives, exchange(): return lax.all_to_all(x, 'wide', split_axis=0, concat_axis=0, tiled=True)  11.2 us
    ppermute x10, waiting for transfers between devices, swap(): return lax.ppermute(x, 'group', [(0, 1), (1, 0)])  9.71 us
    all_to_all x1, waiting for transfers between devices, body(): lax.all_to_all(squares, ALL, split_axis=0, concat_axis=0, tiled=True)  6.22 us
  transfers between devices with their start and end apart: 20, of which 14 were waited for; matrix products, arithmetic and copies ran while one was open for 4% of the time, Pallas kernels for 28%

profile of v2, /device:TPU:0, one launch (start us, length us, event | category | flops | bytes accessed | tf_op | source)
XLA Modules:
  0.0 277.2 jit_solution(4643095963821548227)
XLA Ops:
  7.2 1.9 cast.1
  9.8 1.2 broadcast_in_dim.25.refs_4_
  11.0 1.3 concatenate.22
  12.3 2.7 prepare.1
  15.0 8.3 %all-to-all-start = ((bf16[16,72,128]{2,1,0:T(8,128)(2,1)}), bf16[16,72,128]{2,1,0:T(8,128)(2,1)S(1)}, u32[]{:S(2)}, u32[]{:S(2)}) async-start(bf16[16,72,128]{2,1,0:T(8,128)(2,1)} %get-tuple-element.94), calls=%async_computation | async-start | bytes 589824 | tf_op jit(solution)/shard_map/all_to_all | solution.py:871
  23.3 7.0 %build.1.table = f32[12672,128]{1,0:T(8,128)} custom-call(f32[48,25216]{1,0:T(8,128)} %refs_1_.5), custom_call_target="tpu_custom_call" | custom-call | flops 100000000 | bytes 11329536 | tf_op jit(solution)/shard_map/build/pallas_call | solution.py:314
  30.3 6.6 %all-to-all-done.packet = bf16[16,72,128]{2,1,0:T(8,128)(2,1)S(1)} async-done(((bf16[16,72,128]{2,1,0:T(8,128)(2,1)}), bf16[16,72,128]{2,1,0:T(8,128)(2,1)S(1)}, u32[]{:S(2)}, u32[]{:S(2)}) %all-to-all-start) | async-done | bytes 294944 | tf_op jit(solution)/shard_map/all_to_all | solution.py:871
  36.9 0.1 pad_add_fusion.2.where.refs_0_
  37.0 1.5 collective-permute-done.packet
  38.6 0.5 convert_reduce_fusion.firsts
  39.1 9.7 %lookup.3 = bf16[16,48,640]{2,1,0:T(8,128)(2,1)S(1)} custom-call(s32[2]{0:T(128)S(1)} %pad_add_fusion.2.where.refs_0_, s32[16]{0:T(128)S(1)} %convert_reduce_fusion.firsts, s32[4,1,2560]{2,1,0:T(1,128)S(1)} %reshape_reshape.9.numbers, bf16[16,72,128]{2,1,0:T(8,128)(2,1)S(1)} %collective-permute-done.packet, f32[12672,128]{1,0:T(8,128)} %build.1.table), custom_call_target="tpu_custom_call" | custom-call | flops 1000000000 | bytes 10000000 | tf_op jit(solution)/shard_map/lookup/pallas_call | solution.py:478
  49.0 0.5 convert_reduce_fusion.1.firsts
  49.4 9.7 %lookup.2 = bf16[16,48,640]{2,1,0:T(8,128)(2,1)S(1)} custom-call(s32[2]{0:T(128)S(1)} %pad_add_fusion.2.where.refs_0_, s32[16]{0:T(128)S(1)} %convert_reduce_fusion.1.firsts, s32[4,1,2560]{2,1,0:T(1,128)S(1)} %reshape_reshape.8.numbers, bf16[16,72,128]{2,1,0:T(8,128)(2,1)S(1)} %all-to-all-done.packet, f32[12672,128]{1,0:T(8,128)} %build.1.table), custom_call_target="tpu_custom_call" | custom-call | flops 1000000000 | bytes 10000000 | tf_op jit(solution)/shard_map/lookup/pallas_call | solution.py:478
  59.1 2.4 add.67
  61.6 4.0 %all-to-all-start.1 = ((bf16[16,48,640]{2,1,0:T(8,128)(2,1)}), bf16[16,48,640]{2,1,0:T(8,128)(2,1)S(1)}, u32[]{:S(2)}, u32[]{:S(2)}) async-start(bf16[16,48,640]{2,1,0:T(8,128)(2,1)} %add.67), calls=%async_computation.1 | async-start | bytes 1966080 | tf_op jit(solution)/shard_map/all_to_all | solution.py:871
  65.7 0.1 maximum_select_fusion
  65.9 0.1 copy.75
  66.0 0.1 fusion.8
  66.1 0.1 copy.77
  66.2 0.1 copy.76
  66.3 0.1 copy.84
  66.4 0.3 copy.88
  66.7 1.0 reshape.133.refs_2_.refs_7_
  67.7 0.1 reshape.140.refs_2_.refs_10_
  67.9 0.1 reshape.128
  68.0 0.6 reshape.129.refs_5_
  68.6 0.1 pad_add_fusion.3.firsts
  68.7 0.7 pad_bitcast_fusion.refs_11_
  69.4 29.8 %all-to-all-done.1 = bf16[16,48,640]{2,1,0:T(8,128)(2,1)S(1)} async-done(((bf16[16,48,640]{2,1,0:T(8,128)(2,1)}), bf16[16,48,640]{2,1,0:T(8,128)(2,1)S(1)}, u32[]{:S(2)}, u32[]{:S(2)}) %all-to-all-start.1) | async-done | bytes 983072 | tf_op jit(solution)/shard_map/all_to_all | solution.py:871
  99.2 6.4 %attend.1 = (bf16[16,48,128]{2,1,0:T(8,128)(2,1)}, bf16[16,24,128]{2,1,0:T(8,128)(2,1)}, bf16[208,128]{1,0:T(8,128)(2,1)}, bf16[64,768]{1,0:T(8,128)(2,1)}, f32[...) custom-call(bf16[768,3840]{1,0:T(8,128)(2,1)} %all-gather.4.cloned.1.call-done.refs_0_.refs_1_, ...), custom_call_target="tpu_custom_call" | custom-call | flops 1000000000 | bytes 7583008 | tf_op jit(solution)/shard_map/attend/pallas_call | solution.py:314
  105.6 7.2 %all-to-all-start.2 = ((bf16[16,48,128]{2,1,0:T(8,128)(2,1)}), bf16[16,48,128]{2,1,0:T(8,128)(2,1)S(1)}, u32[]{:S(2)}, u32[]{:S(2)}) async-start(bf16[16,48,128]{2,1,0:T(8,128)(2,1)} %get-tuple-element.100), calls=%async_computation.2 | async-start | bytes 393216 | tf_op jit(solution)/shard_map/all_to_all | solution.py:871
  112.9 1.4 collective-permute-done.3.refs_4_.refs_9_
  114.3 7.4 %all-to-all-done.2.refs_1_.refs_2_ = bf16[16,48,128]{2,1,0:T(8,128)(2,1)S(1)} async-done(((bf16[16,48,128]{2,1,0:T(8,128)(2,1)}), bf16[16,48,128]{2,1,0:T(8,128)(2,1)S(1)}, u32[]{:S(2)}, u32[]{:S(2)}) %all-to-all-start.2) | async-done | bytes 196640 | tf_op jit(solution)/shard_map/all_to_all | solution.py:871
  121.6 2.0 ffn.1
  123.6 11.2 %all_to_all.45.refs_0_ = bf16[16,8,768]{2,1,0:T(8,128)(2,1)S(1)} all-to-all(bf16[16,8,768]{2,1,0:T(8,128)(2,1)S(1)} %bitcast.39), channel_id=1, replica_groups=mesh['group'=2,'wide'=16] {'wide'}, dimensions={0} | all-to-all | bytes 393216 | tf_op jit(solution)/shard_map/all_to_all | solution.py:871
  134.9 0.7 total.1
  135.6 3.5 %all-to-all-start.4 = ((bf16[16,48,128]{2,1,0:T(8,128)(2,1)}), bf16[16,48,128]{2,1,0:T(8,128)(2,1)S(1)}, u32[]{:S(2)}, u32[]{:S(2)}) async-start(bf16[16,48,128]{2,1,0:T(8,128)(2,1)} %total.1), calls=%async_computation.4 | async-start | bytes 393216 | tf_op jit(solution)/shard_map/all_to_all | solution.py:871
  139.1 0.2 all-gather.6.cloned.1.call-start
  139.4 7.8 %all-to-all-done.4.refs_4_ = bf16[16,48,128]{2,1,0:T(8,128)(2,1)S(1)} async-done(((bf16[16,48,128]{2,1,0:T(8,128)(2,1)}), bf16[16,48,128]{2,1,0:T(8,128)(2,1)S(1)}, u32[]{:S(2)}, u32[]{:S(2)}) %all-to-all-start.4) | async-done | bytes 196640 | tf_op jit(solution)/shard_map/all_to_all | solution.py:871
  147.2 1.4 collective-permute-done.4.refs_5_
  148.6 7.2 %middle.1 = (f32[1,1]{1,0:T(1,128)}, bf16[256,768]{1,0:T(8,128)(2,1)}, bf16[256,768]{1,0:T(8,128)(2,1)}, f32[256,768]{1,0:T(8,128)}, bf16[128,768]{1,0:T(8,128)(...) custom-call(s32[2]{0:T(128)S(1)} %pad_add_fusion.2.where.refs_0_, ...), custom_call_target="tpu_custom_call" | custom-call | flops 1000000000 | bytes 9667588 | tf_op jit(solution)/shard_map/middle/pallas_call | solution.py:314
  155.8 3.5 %all-to-all-start.5 = ((bf16[16,72,128]{2,1,0:T(8,128)(2,1)}), bf16[16,72,128]{2,1,0:T(8,128)(2,1)S(1)}, u32[]{:S(2)}, u32[]{:S(2)}) async-start(bf16[16,72,128]{2,1,0:T(8,128)(2,1)} %get-tuple-element.112.refs_7_), calls=%async_computation.5 | async-start | bytes 589824 | tf_op jit(solution)/shard_map/all_to_all | solution.py:871
  159.4 2.6 ffn_grads.1
  162.0 8.9 %all-to-all-done.5.refs_2_.early_own = bf16[16,72,128]{2,1,0:T(8,128)(2,1)S(1)} async-done(((bf16[16,72,128]{2,1,0:T(8,128)(2,1)}), bf16[16,72,128]{2,1,0:T(8,128)(2,1)S(1)}, u32[]{:S(2)}, u32[]{:S(2)}) %all-to-all-start.5) | async-done | bytes 294944 | tf_op jit(solution)/shard_map/all_to_all | solution.py:871
  170.9 7.1 %attend_back.1 = (bf16[16,96,128]{2,1,0:T(8,128)(2,1)}, bf16[144,128]{1,0:T(8,128)(2,1)}, bf16[64,768]{1,0:T(8,128)(2,1)}) custom-call(s32[1]{0:T(128)} %bitcast.13.refs_0_, bf16[768,3840]{1,0:T(8,128)(2,1)} %all-gather.4.cloned.1.call-done.refs_0_.refs_1_, bf16[16,72,128]{2,1,0:T(8,128)(2,1)S(1)} %all-to-all-done.5.refs_2_.early_own, ...), custom_call_target="tpu_custom_call" | custom-call | flops 1000000000 | bytes 8728864 | tf_op jit(solution)/shard_map/attend_back/pallas_call | solution.py:314
  178.0 3.6 %all-to-all-start.6 = ((bf16[16,96,128]{2,1,0:T(8,128)(2,1)}), bf16[16,96,128]{2,1,0:T(8,128)(2,1)S(1)}, u32[]{:S(2)}, u32[]{:S(2)}) async-start(bf16[16,96,128]{2,1,0:T(8,128)(2,1)} %get-tuple-element.125.refs_5_), calls=%async_computation.6 | async-start | bytes 786432 | tf_op jit(solution)/shard_map/all_to_all | solution.py:871
  181.6 1.4 collective-permute-done.7.refs_4_
  183.1 2.6 pack.1.refs_0_
  185.6 9.7 %all-to-all-done.6.late_own.refs_1_ = bf16[16,96,128]{2,1,0:T(8,128)(2,1)S(1)} async-done(((bf16[16,96,128]{2,1,0:T(8,128)(2,1)}), bf16[16,96,128]{2,1,0:T(8,128)(2,1)S(1)}, u32[]{:S(2)}, u32[]{:S(2)}) %all-to-all-start.6) | async-done | bytes 393248 | tf_op jit(solution)/shard_map/all_to_all | solution.py:871
  195.3 3.9 %all-to-all-start.7 = ((bf16[16,240,128]{2,1,0:T(8,128)(2,1)}), bf16[16,240,128]{2,1,0:T(8,128)(2,1)S(1)}, u32[]{:S(2)}, u32[]{:S(2)}) async-start(bf16[16,240,128]{2,1,0:T(8,128)(2,1)} %once.1), calls=%async_computation.7 | async-start | bytes 1966080 | tf_op jit(solution)/shard_map/all_to_all | solution.py:871
  199.3 0.5 collective-permute-start.5
  199.8 1.7 collective-permute-done.5.early_other
  201.6 0.9 all-gather.6.cloned.1.call-done
  202.5 28.3 %spread_tokens.1 = (f32[48,25216]{1,0:T(8,128)}, f32[8,128]{1,0:T(8,128)}) custom-call(s32[2]{0:T(128)S(1)} %pad_add_fusion.2.where.refs_0_, s32[32]{0:T(128)S(1)} %pad_add_fusion.3.firsts, s32[4,1,5120]{2,1,0:T(1,128)S(1)} %bitcast.38, bf16[32,72,128]{2,1,0:T(8,128)(2,1)} %copy-done.2, bf16[16,72,128]{2,1,0:T(8,128)(2,1)S(1)} %all-to-all-done.5.refs_2_.early_own, ...), custom_call_target="tpu_custom_call" | custom-call | flops 1000000000 | bytes 30000000 | tf_op jit(solution)/shard_map/spread_tokens/pallas_call | solution.py:594
  230.8 0.7 fusion.18.refs_2_
  231.5 0.5 collective-permute-start.9
  232.0 2.3 collective-permute-done.9.refs_6_
  234.3 6.5 %grads.1 = (f32[24,2304]{1,0:T(8,128)}, f32[24,768]{1,0:T(8,128)}, f32[24,3072]{1,0:T(8,128)}, f32[96,768]{1,0:T(8,128)}, f32[16,768]{1,0:T(8,128)}, /*index=5*/f32[32,8,128]{2,1,0:T(8,128)}) custom-call(s32[2]{0:T(128)S(1)} %pad_add_fusion.2.where.refs_0_, bf16[32,208,128]{2,1,0:T(8,128)(2,1)} %bitcast.41, bf16[16,240,128]{2,1,0:T(8,128)(2,1)S(1)} %fusion.18.refs_2_, ...), custom_call_target="tpu_custom_call" | custom-call | flops 1000000000 | bytes 5279744 | tf_op jit(solution)/shard_map/grads/pallas_call | solution.py:314
  240.8 4.8 %all-to-all-start.8 = ((f32[32,8,128]{2,1,0:T(8,128)}), f32[32,8,128]{2,1,0:T(8,128)S(1)}, u32[]{:S(2)}, u32[]{:S(2)}) async-start(f32[32,8,128]{2,1,0:T(8,128)} %get-tuple-element.137), calls=%async_computation.8 | async-start | bytes 262144 | tf_op jit(solution)/shard_map/all_to_all | solution.py:1131
  246.5 0.1 pad_maximum_fusion.refs_0_
  246.6 0.8 reshape.138
  247.4 6.2 %all-to-all-done.8.refs_5_ = f32[32,8,128]{2,1,0:T(8,128)S(1)} async-done(((f32[32,8,128]{2,1,0:T(8,128)}), f32[32,8,128]{2,1,0:T(8,128)S(1)}, u32[]{:S(2)}, u32[]{:S(2)}) %all-to-all-start.8) | async-done | bytes 131104 | tf_op jit(solution)/shard_map/all_to_all | solution.py:1131
  253.6 15.4 %adam.1 = (f32[1,1]{1,0:T(1,128)}, f32[1,1]{1,0:T(1,128)}, f32[24,2304]{1,0:T(8,128)}, f32[24,2304]{1,0:T(8,128)}, f32[24,2304]{1,0:T(8,128)}, /*index=5*/f32[24...) custom-call(f32[2]{0:T(128)S(1)} %pad_maximum_fusion.refs_0_, ...), custom_call_target="tpu_custom_call" | custom-call | bytes 40730632 | tf_op jit(solution)/shard_map/adam/pallas_call | solution.py:314
  269.0 1.3 multiply_subtract_fusion
  (59 shorter events, 1.0 us)
Async XLA Ops:
  7.2 92.0 %all-gather.4.cloned.1.call-start = ((), (), s32[]{:S(2)}) async-start(), calls=%async_computation.9 | async-start | bytes 6082560 | tf_op jit(solution)/shard_map/all_gather | solution.py:1033
  15.0 22.0 %all-to-all-start = ((bf16[16,72,128]{2,1,0:T(8,128)(2,1)}), bf16[16,72,128]{2,1,0:T(8,128)(2,1)S(1)}, u32[]{:S(2)}, u32[]{:S(2)}) async-start(bf16[16,72,128]{2,1,0:T(8,128)(2,1)} %get-tuple-element.94), calls=%async_computation | async-start | bytes 589824 | tf_op jit(solution)/shard_map/all_to_all | solution.py:871
  36.9 1.6 collective-permute-start
  48.8 10.3 %collective-permute-start.1 = (bf16[16,48,640]{2,1,0:T(8,128)(2,1)S(1)}, bf16[16,48,640]{2,1,0:T(8,128)(2,1)}, u32[]{:S(2)}, u32[]{:S(2)}) collective-permute-start(bf16[16,48,640]{2,1,0:T(8,128)(2,1)S(1)} %lookup.3), channel_id=1, source_target_pairs={{0,16},{16,0},{1,17},{17,1},{2,18},{18,2},{3,19},{19,3},{4,20},{20... | collective-permute-start | bytes 2949128 | tf_op jit(solution)/shard_map/ppermute | solution.py:867
  61.6 37.6 %all-to-all-start.1 = ((bf16[16,48,640]{2,1,0:T(8,128)(2,1)}), bf16[16,48,640]{2,1,0:T(8,128)(2,1)S(1)}, u32[]{:S(2)}, u32[]{:S(2)}) async-start(bf16[16,48,640]{2,1,0:T(8,128)(2,1)} %add.67), calls=%async_computation.1 | async-start | bytes 1966080 | tf_op jit(solution)/shard_map/all_to_all | solution.py:871
  65.7 40.0 %copy-start.2 = (bf16[32,72,128]{2,1,0:T(8,128)(2,1)}, bf16[32,72,128]{2,1,0:T(8,128)(2,1)S(1)}, u32[]{:S(2)}) copy-start(bf16[32,72,128]{2,1,0:T(8,128)(2,1)S(1)} %constant_dynamic-update-slice_fusion.packet) | copy-start | bytes 1769476
  66.3 46.5 %copy-start.4 = (bf16[96,768]{1,0:T(8,128)(2,1)S(1)}, bf16[96,768]{1,0:T(8,128)(2,1)}, u32[]{:S(2)}) copy-start(bf16[96,768]{1,0:T(8,128)(2,1)} %get-tuple-element.102.refs_3_.refs_8_) | copy-start | bytes 442372
  67.8 31.4 %copy-start.3 = (f32[15,768]{1,0:T(8,128)}, f32[15,768]{1,0:T(8,128)S(1)}, u32[]{:S(2)}) copy-start(f32[15,768]{1,0:T(8,128)S(1)} %reshape.140.refs_2_.refs_10_) | copy-start | bytes 138244
  99.2 56.6 %copy-start = (bf16[16,48,640]{2,1,0:T(8,128)(2,1)}, bf16[16,48,640]{2,1,0:T(8,128)(2,1)S(1)}, u32[]{:S(2)}) copy-start(bf16[16,48,640]{2,1,0:T(8,128)(2,1)S(1)} %all-to-all-done.1) | copy-start | bytes 2949124
  105.6 16.0 %all-to-all-start.2 = ((bf16[16,48,128]{2,1,0:T(8,128)(2,1)}), bf16[16,48,128]{2,1,0:T(8,128)(2,1)S(1)}, u32[]{:S(2)}, u32[]{:S(2)}) async-start(bf16[16,48,128]{2,1,0:T(8,128)(2,1)} %get-tuple-element.100), calls=%async_computation.2 | async-start | bytes 393216 | tf_op jit(solution)/shard_map/all_to_all | solution.py:871
  112.8 1.4 collective-permute-start.3
  114.3 34.4 %copy-start.1 = (bf16[96,768]{1,0:T(8,128)(2,1)}, bf16[96,768]{1,0:T(8,128)(2,1)S(1)}, u32[]{:S(2)}) copy-start(bf16[96,768]{1,0:T(8,128)(2,1)S(1)} %collective-permute-done.3.refs_4_.refs_9_) | copy-start | bytes 442372
  135.6 11.6 %all-to-all-start.4 = ((bf16[16,48,128]{2,1,0:T(8,128)(2,1)}), bf16[16,48,128]{2,1,0:T(8,128)(2,1)S(1)}, u32[]{:S(2)}, u32[]{:S(2)}) async-start(bf16[16,48,128]{2,1,0:T(8,128)(2,1)} %total.1), calls=%async_computation.4 | async-start | bytes 393216 | tf_op jit(solution)/shard_map/all_to_all | solution.py:871
  139.1 63.4 %all-gather.6.cloned.1.call-start = ((), (), s32[]{:S(2)}) async-start(), calls=%async_computation.10 | async-start | bytes 1757184 | tf_op jit(solution)/shard_map/all_gather | solution.py:1078
  139.3 7.9 %collective-permute-start.2 = (bf16[16,48,128]{2,1,0:T(8,128)(2,1)S(1)}, bf16[16,48,128]{2,1,0:T(8,128)(2,1)S(1)}, u32[]{:S(2)}, u32[]{:S(2)}) collective-permute-start(bf16[16,48,128]{2,1,0:T(8,128)(2,1)S(1)} %all-to-all-done.2.refs_1_.refs_2_), channel_id=1, source_target_pairs={{0,16},{16,0},{1,17},{17,1},{2,18},{18,2},{3,19},{19,3},{4,20},{20... | collective-permute-start | bytes 589832 | tf_op jit(solution)/shard_map/ppermute | solution.py:867
  147.2 1.4 collective-permute-start.4
  155.8 15.1 %all-to-all-start.5 = ((bf16[16,72,128]{2,1,0:T(8,128)(2,1)}), bf16[16,72,128]{2,1,0:T(8,128)(2,1)S(1)}, u32[]{:S(2)}, u32[]{:S(2)}) async-start(bf16[16,72,128]{2,1,0:T(8,128)(2,1)} %get-tuple-element.112.refs_7_), calls=%async_computation.5 | async-start | bytes 589824 | tf_op jit(solution)/shard_map/all_to_all | solution.py:871
  162.0 19.6 %copy-start.8 = (bf16[384,192]{1,0:T(8,128)(2,1)S(1)}, bf16[384,192]{1,0:T(8,128)(2,1)}, u32[]{:S(2)}) copy-start(bf16[384,192]{1,0:T(8,128)(2,1)} %get-tuple-element.131) | copy-start | bytes 442372
  178.0 17.4 %all-to-all-start.6 = ((bf16[16,96,128]{2,1,0:T(8,128)(2,1)}), bf16[16,96,128]{2,1,0:T(8,128)(2,1)S(1)}, u32[]{:S(2)}, u32[]{:S(2)}) async-start(bf16[16,96,128]{2,1,0:T(8,128)(2,1)} %get-tuple-element.125.refs_5_), calls=%async_computation.6 | async-start | bytes 786432 | tf_op jit(solution)/shard_map/all_to_all | solution.py:871
  181.5 1.5 collective-permute-start.7
  183.1 48.5 %copy-start.9 = (bf16[96,768]{1,0:T(8,128)(2,1)S(1)}, bf16[96,768]{1,0:T(8,128)(2,1)}, u32[]{:S(2)}) copy-start(bf16[96,768]{1,0:T(8,128)(2,1)} %get-tuple-element.135) | copy-start | bytes 442372
  195.3 35.5 %all-to-all-start.7 = ((bf16[16,240,128]{2,1,0:T(8,128)(2,1)}), bf16[16,240,128]{2,1,0:T(8,128)(2,1)S(1)}, u32[]{:S(2)}, u32[]{:S(2)}) async-start(bf16[16,240,128]{2,1,0:T(8,128)(2,1)} %once.1), calls=%async_computation.7 | async-start | bytes 1966080 | tf_op jit(solution)/shard_map/all_to_all | solution.py:871
  199.3 2.3 collective-permute-start.6
  199.3 2.2 collective-permute-start.5
  231.5 2.8 %collective-permute-start.8 = (bf16[16,240,128]{2,1,0:T(8,128)(2,1)S(1)}, bf16[16,240,128]{2,1,0:T(8,128)(2,1)S(1)}, u32[]{:S(2)}, u32[]{:S(2)}) collective-permute-start(bf16[16,240,128]{2,1,0:T(8,128)(2,1)S(1)} %fusion.18.refs_2_), channel_id=1, source_target_pairs={{0,16},{16,0},{1,17},{17,1},{2,18},{18,2},{3,19},{19,3},{4,20},{20... | collective-permute-start | bytes 2949128 | tf_op jit(solution)/shard_map/ppermute | solution.py:867
  231.5 2.8 collective-permute-start.9
  240.8 12.8 %all-to-all-start.8 = ((f32[32,8,128]{2,1,0:T(8,128)}), f32[32,8,128]{2,1,0:T(8,128)S(1)}, u32[]{:S(2)}, u32[]{:S(2)}) async-start(f32[32,8,128]{2,1,0:T(8,128)} %get-tuple-element.137), calls=%async_computation.8 | async-start | bytes 262144 | tf_op jit(solution)/shard_map/all_to_all | solution.py:1131
  253.6 15.4 %copy-start.5 = (f32[360]{0:T(512)S(1)}, f32[360]{0:T(512)}, u32[]{:S(2)}) copy-start(f32[360]{0:T(512)} %param.57) | copy-start | bytes 4324
  253.6 15.4 %copy-start.6 = (f32[360]{0:T(512)S(1)}, f32[360]{0:T(512)}, u32[]{:S(2)}) copy-start(f32[360]{0:T(512)} %param.58) | copy-start | bytes 4324
  253.6 15.4 %copy-start.7 = (f32[360]{0:T(512)S(1)}, f32[360]{0:T(512)}, u32[]{:S(2)}) copy-start(f32[360]{0:T(512)} %param.59) | copy-start | bytes 4324
Sparse Core Ops, SparseCore 0:
  11.5 86.5 all-gather.3
  147.3 55.1 all-gather.5

commit v3 on v2

--- a/solution.py
+++ b/solution.py
@@ -503,12 +503,18 @@
 
     @pl.when(step_at == 0)
     def _():
+        at_once = 3
+
         def clear(i, carry):
             for part in parts:
-                part[pl.ds(pl.multiple_of(i * LANES, LANES), LANES), :] = jnp.zeros((LANES, LANES), f32)
+                for k in range(at_once):
+                    part[pl.ds(pl.multiple_of((i * at_once + k) * LANES, LANES), LANES), :] = jnp.zeros((LANES, LANES), f32)
             return carry
 
-        lax.fori_loop(0, blocks, clear, 0)
+        lax.fori_loop(0, blocks // at_once, clear, 0)
+        for k in range(blocks // at_once * at_once, blocks):
+            for part in parts:
+                part[k * LANES : (k + 1) * LANES, :] = jnp.zeros((LANES, LANES), f32)
 
     gap = jnp.zeros((SIDE - feats, count), f32)
     block = feats // 2
@@ -563,13 +569,13 @@
             for part in parts[1:]:
                 lines = lines + part[pl.ds(start, LANES), :]
             turned = lines.T
-            out[:, pl.ds(start, LANES)] = turned[:feats]
+            out[:, pl.ds(start, LANES)] = turned[:feats].astype(bf16)
             if both:
-                out[:, pl.ds(pl.multiple_of(half + start, LANES), LANES)] = turned[SIDE : SIDE + feats]
+                out[:, pl.ds(pl.multiple_of(half + start, LANES), LANES)] = turned[SIDE : SIDE + feats].astype(bf16)
             return total + lines * lines
 
         second = (vocab - half) // LANES
-        group_of = 7
+        group_of = 14
 
         def several(i, total):
             for k in range(group_of):
@@ -593,7 +599,7 @@
     theirs = lambda pair: pl.BlockSpec((per,) + pair[0].shape[1:], lambda i, *s: (jnp.maximum(i - steps // 2, 0), 0, 0))
     return pl.pallas_call(
         partial(spread_kernel, rows, half_rows, feats, per, unroll, copies, at_early),
-        out_shape=[pltpu.HBM((feats, half_rows), f32), pltpu.HBM((ROWS, LANES), f32)],
+        out_shape=[pltpu.HBM((feats, half_rows), bf16), pltpu.HBM((ROWS, LANES), f32)],
         grid_spec=pltpu.PrefetchScalarGridSpec(
             num_scalar_prefetch=2,
             grid=(steps,),
@@ -816,13 +822,17 @@
     norm_out, factor_out = refs[4 * count : 4 * count + 2]
     outs = refs[4 * count + 2 : 7 * count + 2]
     far = refs[7 * count + 2 : 7 * count + 5]
-    loads, stores, got_in, sent = refs[7 * count + 5 :]
+    loads, grad_loads, stores, got_in, sent = refs[7 * count + 5 :]
     slots, lines = loads.shape[0], loads.shape[2]
     jobs = weight.shape[0] // lines
     sources = (weight, first, second, d_table)
 
     def load(j):
-        return [pltpu.make_async_copy(ref.at[pl.ds(j * lines, lines), :], loads.at[j % slots, k], got_in.at[j % slots, k]) for k, ref in enumerate(sources)]
+        places = [loads.at[j % slots, k] for k in range(3)] + [grad_loads.at[j % slots]]
+        return [
+            pltpu.make_async_copy(ref.at[pl.ds(j * lines, lines), :], place, got_in.at[j % slots, k])
+            for k, (ref, place) in enumerate(zip(sources, places))
+        ]
 
     def store(j):
         return [pltpu.make_async_copy(stores.at[j % slots, k], ref.at[pl.ds(j * lines, lines), :], sent.at[j % slots, k]) for k, ref in enumerate(far)]
@@ -845,7 +855,7 @@
             for copy in store(j - slots):
                 copy.wait()
         old = [loads[j % slots, k] for k in range(3)]
-        new = update(*old, loads[j % slots, 3] * factor, RATES[0], one, two)
+        new = update(*old, grad_loads[j % slots].astype(f32) * factor, RATES[0], one, two)
         for k in range(3):
             stores[j % slots, k] = new[k]
         for copy in store(j):
@@ -1141,7 +1151,8 @@
         squares_got, *grads, *middle_state,
         scalars=(scales,), far=(*state[:3], d_table), far_outs=[shape(embedding.shape)] * 3,
         scratch=[
-            pltpu.VMEM((slots, 4, step_rows, half_rows), f32), pltpu.VMEM((slots, 3, step_rows, half_rows), f32),
+            pltpu.VMEM((slots, 3, step_rows, half_rows), f32), pltpu.VMEM((slots, step_rows, half_rows), bf16),
+            pltpu.VMEM((slots, 3, step_rows, half_rows), f32),
             pltpu.SemaphoreType.DMA((slots, 4)), pltpu.SemaphoreType.DMA((slots, 3)),
         ],
         near=(0,), name="adam", vmem=40,

time: 279 us -> 277 us (level)
  Pallas kernels: 110 us -> 105 us
  starting transfers between devices: 40.5 us -> 44.2 us
    ppermute x10, starting transfers between devices: 1.37 us -> 4.73 us  [swap(): return lax.ppermute(x, 'group', [(0, 1), (1, 0)])]
    pallas_call x1, Pallas kernels: 28.3 us -> 25.4 us  [spread_tokens(): pl.pallas_call(partial(spread_kernel, rows, half_rows, feats, per, unroll...]
  transfers between devices with their start and end apart: 20 -> 20, of which waited for: 14 -> 14; matrix products, arithmetic and copies ran while one was open for 4% -> 4% of each run, Pallas kernels for 28% -> 26%
where the time goes in v3:
time: 277 us; the launch traced here: 276 us
  Pallas kernels  105 us (38%)
  waiting for transfers between devices  87 us (31%)
  starting transfers between devices  44.2 us (16%)
  between operations  15.9 us (6%)
  blocking collectives  11.2 us (4%)
  local copies, waits for them, and re-layouts  6.85 us (2%)
  other arithmetic  5.81 us (2%)
    all_to_all x7, waiting for transfers between devices, exchange(): return lax.all_to_all(x, 'wide', split_axis=0, concat_axis=0, tiled=True)  70.3 us
    pallas_call x12, Pallas kernels, call(): pl.pallas_call(run, grid=(1,), out_shape=shapes, in_specs=in_specs, out_s...  61.4 us
    all_to_all x7, starting transfers between devices, exchange(): return lax.all_to_all(x, 'wide', split_axis=0, concat_axis=0, tiled=True)  34.2 us
    pallas_call x1, Pallas kernels, spread_tokens(): pl.pallas_call(partial(spread_kernel, rows, half_rows, feats, per, unroll...  25.4 us
    pallas_call x2, Pallas kernels, lookup(): pl.pallas_call(partial(lookup_kernel, half_rows, per, unroll), out_shape=...  18.2 us
    all_to_all x1, blocking collectives, exchange(): return lax.all_to_all(x, 'wide', split_axis=0, concat_axis=0, tiled=True)  11.2 us
    ppermute x10, waiting for transfers between devices, swap(): return lax.ppermute(x, 'group', [(0, 1), (1, 0)])  9.78 us
    all_to_all x1, waiting for transfers between devices, body(): lax.all_to_all(squares, ALL, split_axis=0, concat_axis=0, tiled=True)  5.96 us
  transfers between devices with their start and end apart: 20, of which 14 were waited for; matrix products, arithmetic and copies ran while one was open for 4% of the time, Pallas kernels for 26%

profile of v3, /device:TPU:0, one launch (start us, length us, event | category | flops | bytes accessed | tf_op | source)
XLA Modules:
  0.0 276.1 jit_solution(18242323169301827272)
XLA Ops:
  7.2 1.9 cast.1
  9.8 1.2 broadcast_in_dim.25.refs_4_
  11.0 1.3 concatenate.22
  12.3 2.7 prepare.1
  15.0 8.3 %all-to-all-start = ((bf16[16,72,128]{2,1,0:T(8,128)(2,1)}), bf16[16,72,128]{2,1,0:T(8,128)(2,1)S(1)}, u32[]{:S(2)}, u32[]{:S(2)}) async-start(bf16[16,72,128]{2,1,0:T(8,128)(2,1)} %get-tuple-element.94), calls=%async_computation | async-start | bytes 589824 | tf_op jit(solution)/shard_map/all_to_all | solution.py:881
  23.3 7.0 %build.1.table = f32[12672,128]{1,0:T(8,128)} custom-call(f32[48,25216]{1,0:T(8,128)} %refs_1_.5), custom_call_target="tpu_custom_call" | custom-call | flops 100000000 | bytes 11329536 | tf_op jit(solution)/shard_map/build/pallas_call | solution.py:314
  30.3 6.6 %all-to-all-done.packet = bf16[16,72,128]{2,1,0:T(8,128)(2,1)S(1)} async-done(((bf16[16,72,128]{2,1,0:T(8,128)(2,1)}), bf16[16,72,128]{2,1,0:T(8,128)(2,1)S(1)}, u32[]{:S(2)}, u32[]{:S(2)}) %all-to-all-start) | async-done | bytes 294944 | tf_op jit(solution)/shard_map/all_to_all | solution.py:881
  36.9 0.1 pad_add_fusion.2.where.refs_0_
  37.0 1.5 collective-permute-done.packet
  38.6 0.5 convert_reduce_fusion.firsts
  39.1 9.2 %lookup.3 = bf16[16,48,640]{2,1,0:T(8,128)(2,1)S(1)} custom-call(s32[2]{0:T(128)S(1)} %pad_add_fusion.2.where.refs_0_, s32[16]{0:T(128)S(1)} %convert_reduce_fusion.firsts, s32[4,1,2560]{2,1,0:T(1,128)S(1)} %reshape_reshape.9.numbers, bf16[16,72,128]{2,1,0:T(8,128)(2,1)S(1)} %collective-permute-done.packet, f32[12672,128]{1,0:T(8,128)} %build.1.table), custom_call_target="tpu_custom_call" | custom-call | flops 1000000000 | bytes 10000000 | tf_op jit(solution)/shard_map/lookup/pallas_call | solution.py:478
  48.3 1.0 collective-permute-start.1
  49.3 0.5 convert_reduce_fusion.1.firsts
  49.8 9.1 %lookup.2 = bf16[16,48,640]{2,1,0:T(8,128)(2,1)S(1)} custom-call(s32[2]{0:T(128)S(1)} %pad_add_fusion.2.where.refs_0_, s32[16]{0:T(128)S(1)} %convert_reduce_fusion.1.firsts, s32[4,1,2560]{2,1,0:T(1,128)S(1)} %reshape_reshape.8.numbers, bf16[16,72,128]{2,1,0:T(8,128)(2,1)S(1)} %all-to-all-done.packet, f32[12672,128]{1,0:T(8,128)} %build.1.table), custom_call_target="tpu_custom_call" | custom-call | flops 1000000000 | bytes 10000000 | tf_op jit(solution)/shard_map/lookup/pallas_call | solution.py:478
  58.9 2.4 add.67
  61.3 4.1 %all-to-all-start.1 = ((bf16[16,48,640]{2,1,0:T(8,128)(2,1)}), bf16[16,48,640]{2,1,0:T(8,128)(2,1)S(1)}, u32[]{:S(2)}, u32[]{:S(2)}) async-start(bf16[16,48,640]{2,1,0:T(8,128)(2,1)} %add.67), calls=%async_computation.1 | async-start | bytes 1966080 | tf_op jit(solution)/shard_map/all_to_all | solution.py:881
  65.5 0.1 maximum_select_fusion
  65.8 0.1 copy.75
  65.9 0.1 copy.77
  66.0 0.1 copy.76
  66.2 0.1 copy.84
  66.3 0.3 copy.88
  66.6 1.0 reshape.133.refs_2_.refs_7_
  67.6 0.1 reshape.140.refs_2_.refs_10_
  67.8 0.1 reshape.128
  67.9 0.6 reshape.129.refs_5_
  68.5 0.1 pad_add_fusion.3.firsts
  68.6 0.7 pad_bitcast_fusion.refs_11_
  69.3 29.9 %all-to-all-done.1 = bf16[16,48,640]{2,1,0:T(8,128)(2,1)S(1)} async-done(((bf16[16,48,640]{2,1,0:T(8,128)(2,1)}), bf16[16,48,640]{2,1,0:T(8,128)(2,1)S(1)}, u32[]{:S(2)}, u32[]{:S(2)}) %all-to-all-start.1) | async-done | bytes 983072 | tf_op jit(solution)/shard_map/all_to_all | solution.py:881
  99.1 6.4 %attend.1 = (bf16[16,48,128]{2,1,0:T(8,128)(2,1)}, bf16[16,24,128]{2,1,0:T(8,128)(2,1)}, bf16[208,128]{1,0:T(8,128)(2,1)}, bf16[64,768]{1,0:T(8,128)(2,1)}, f32[...) custom-call(bf16[768,3840]{1,0:T(8,128)(2,1)} %all-gather.4.cloned.1.call-done.refs_0_.refs_1_, ...), custom_call_target="tpu_custom_call" | custom-call | flops 1000000000 | bytes 7583008 | tf_op jit(solution)/shard_map/attend/pallas_call | solution.py:314
  105.6 7.2 %all-to-all-start.2 = ((bf16[16,48,128]{2,1,0:T(8,128)(2,1)}), bf16[16,48,128]{2,1,0:T(8,128)(2,1)S(1)}, u32[]{:S(2)}, u32[]{:S(2)}) async-start(bf16[16,48,128]{2,1,0:T(8,128)(2,1)} %get-tuple-element.100), calls=%async_computation.2 | async-start | bytes 393216 | tf_op jit(solution)/shard_map/all_to_all | solution.py:881
  112.9 1.4 collective-permute-done.3.refs_4_.refs_9_
  114.3 7.5 %all-to-all-done.2.refs_1_.refs_2_ = bf16[16,48,128]{2,1,0:T(8,128)(2,1)S(1)} async-done(((bf16[16,48,128]{2,1,0:T(8,128)(2,1)}), bf16[16,48,128]{2,1,0:T(8,128)(2,1)S(1)}, u32[]{:S(2)}, u32[]{:S(2)}) %all-to-all-start.2) | async-done | bytes 196640 | tf_op jit(solution)/shard_map/all_to_all | solution.py:881
  121.7 2.0 ffn.1
  123.8 11.2 %all_to_all.45.refs_0_ = bf16[16,8,768]{2,1,0:T(8,128)(2,1)S(1)} all-to-all(bf16[16,8,768]{2,1,0:T(8,128)(2,1)S(1)} %bitcast.39), channel_id=1, replica_groups=mesh['group'=2,'wide'=16] {'wide'}, dimensions={0} | all-to-all | bytes 393216 | tf_op jit(solution)/shard_map/all_to_all | solution.py:881
  135.0 0.7 total.1
  135.7 3.5 %all-to-all-start.4 = ((bf16[16,48,128]{2,1,0:T(8,128)(2,1)}), bf16[16,48,128]{2,1,0:T(8,128)(2,1)S(1)}, u32[]{:S(2)}, u32[]{:S(2)}) async-start(bf16[16,48,128]{2,1,0:T(8,128)(2,1)} %total.1), calls=%async_computation.4 | async-start | bytes 393216 | tf_op jit(solution)/shard_map/all_to_all | solution.py:881
  139.3 0.2 all-gather.6.cloned.1.call-start
  139.6 7.8 %all-to-all-done.4.refs_4_ = bf16[16,48,128]{2,1,0:T(8,128)(2,1)S(1)} async-done(((bf16[16,48,128]{2,1,0:T(8,128)(2,1)}), bf16[16,48,128]{2,1,0:T(8,128)(2,1)S(1)}, u32[]{:S(2)}, u32[]{:S(2)}) %all-to-all-start.4) | async-done | bytes 196640 | tf_op jit(solution)/shard_map/all_to_all | solution.py:881
  147.4 1.4 collective-permute-done.4.refs_5_
  148.8 7.2 %middle.1 = (f32[1,1]{1,0:T(1,128)}, bf16[256,768]{1,0:T(8,128)(2,1)}, bf16[256,768]{1,0:T(8,128)(2,1)}, f32[256,768]{1,0:T(8,128)}, bf16[128,768]{1,0:T(8,128)(...) custom-call(s32[2]{0:T(128)S(1)} %pad_add_fusion.2.where.refs_0_, ...), custom_call_target="tpu_custom_call" | custom-call | flops 1000000000 | bytes 9667588 | tf_op jit(solution)/shard_map/middle/pallas_call | solution.py:314
  155.9 3.5 %all-to-all-start.5 = ((bf16[16,72,128]{2,1,0:T(8,128)(2,1)}), bf16[16,72,128]{2,1,0:T(8,128)(2,1)S(1)}, u32[]{:S(2)}, u32[]{:S(2)}) async-start(bf16[16,72,128]{2,1,0:T(8,128)(2,1)} %get-tuple-element.112.refs_7_), calls=%async_computation.5 | async-start | bytes 589824 | tf_op jit(solution)/shard_map/all_to_all | solution.py:881
  159.5 2.6 ffn_grads.1
  162.1 8.9 %all-to-all-done.5.refs_2_.early_own = bf16[16,72,128]{2,1,0:T(8,128)(2,1)S(1)} async-done(((bf16[16,72,128]{2,1,0:T(8,128)(2,1)}), bf16[16,72,128]{2,1,0:T(8,128)(2,1)S(1)}, u32[]{:S(2)}, u32[]{:S(2)}) %all-to-all-start.5) | async-done | bytes 294944 | tf_op jit(solution)/shard_map/all_to_all | solution.py:881
  171.0 7.1 %attend_back.1 = (bf16[16,96,128]{2,1,0:T(8,128)(2,1)}, bf16[144,128]{1,0:T(8,128)(2,1)}, bf16[64,768]{1,0:T(8,128)(2,1)}) custom-call(s32[1]{0:T(128)} %bitcast.13.refs_0_, bf16[768,3840]{1,0:T(8,128)(2,1)} %all-gather.4.cloned.1.call-done.refs_0_.refs_1_, bf16[16,72,128]{2,1,0:T(8,128)(2,1)S(1)} %all-to-all-done.5.refs_2_.early_own, ...), custom_call_target="tpu_custom_call" | custom-call | flops 1000000000 | bytes 8728864 | tf_op jit(solution)/shard_map/attend_back/pallas_call | solution.py:314
  178.1 3.6 %all-to-all-start.6 = ((bf16[16,96,128]{2,1,0:T(8,128)(2,1)}), bf16[16,96,128]{2,1,0:T(8,128)(2,1)S(1)}, u32[]{:S(2)}, u32[]{:S(2)}) async-start(bf16[16,96,128]{2,1,0:T(8,128)(2,1)} %get-tuple-element.125.refs_5_), calls=%async_computation.6 | async-start | bytes 786432 | tf_op jit(solution)/shard_map/all_to_all | solution.py:881
  181.8 1.4 collective-permute-done.7.refs_4_
  183.2 2.6 pack.1.refs_0_
  185.8 9.7 %all-to-all-done.6.late_own.refs_1_ = bf16[16,96,128]{2,1,0:T(8,128)(2,1)S(1)} async-done(((bf16[16,96,128]{2,1,0:T(8,128)(2,1)}), bf16[16,96,128]{2,1,0:T(8,128)(2,1)S(1)}, u32[]{:S(2)}, u32[]{:S(2)}) %all-to-all-start.6) | async-done | bytes 393248 | tf_op jit(solution)/shard_map/all_to_all | solution.py:881
  195.5 3.9 %all-to-all-start.7 = ((bf16[16,240,128]{2,1,0:T(8,128)(2,1)}), bf16[16,240,128]{2,1,0:T(8,128)(2,1)S(1)}, u32[]{:S(2)}, u32[]{:S(2)}) async-start(bf16[16,240,128]{2,1,0:T(8,128)(2,1)} %once.1), calls=%async_computation.7 | async-start | bytes 1966080 | tf_op jit(solution)/shard_map/all_to_all | solution.py:881
  199.5 0.5 collective-permute-start.5
  200.0 1.7 collective-permute-done.5.early_other
  201.7 0.9 all-gather.6.cloned.1.call-done
  202.6 25.4 %spread_tokens.1 = (bf16[48,25216]{1,0:T(8,128)(2,1)}, f32[8,128]{1,0:T(8,128)}) custom-call(s32[2]{0:T(128)S(1)} %pad_add_fusion.2.where.refs_0_, s32[32]{0:T(128)S(1)} %pad_add_fusion.3.firsts, s32[4,1,5120]{2,1,0:T(1,128)S(1)} %bitcast.38, bf16[32,72,128]{2,1,0:T(8,128)(2,1)} %copy-done.2, bf16[16,72,128]{2,1,0:T(8,128)(2,1)S(1)} %all-to-all-done.5.refs_2_.early_own, ...), custom_call_target="tpu_custom_call" | custom-call | flops 1000000000 | bytes 30000000 | tf_op jit(solution)/shard_map/spread_tokens/pallas_call | solution.py:600
  228.0 0.7 fusion.18.refs_2_
  228.7 2.9 %collective-permute-start.8 = (bf16[16,240,128]{2,1,0:T(8,128)(2,1)S(1)}, bf16[16,240,128]{2,1,0:T(8,128)(2,1)S(1)}, u32[]{:S(2)}, u32[]{:S(2)}) collective-permute-start(bf16[16,240,128]{2,1,0:T(8,128)(2,1)S(1)} %fusion.18.refs_2_), channel_id=1, source_target_pairs={{0,16},{16,0},{1,17},{17,1},{2,18},{18,2},{3,19},{19,3},{4,20},{20... | collective-permute-start | bytes 2949128 | tf_op jit(solution)/shard_map/ppermute | solution.py:877
  231.6 2.3 collective-permute-done.9.refs_6_
  234.0 6.5 %grads.1 = (f32[24,2304]{1,0:T(8,128)}, f32[24,768]{1,0:T(8,128)}, f32[24,3072]{1,0:T(8,128)}, f32[96,768]{1,0:T(8,128)}, f32[16,768]{1,0:T(8,128)}, /*index=5*/f32[32,8,128]{2,1,0:T(8,128)}) custom-call(s32[2]{0:T(128)S(1)} %pad_add_fusion.2.where.refs_0_, bf16[32,208,128]{2,1,0:T(8,128)(2,1)} %bitcast.41, bf16[16,240,128]{2,1,0:T(8,128)(2,1)S(1)} %fusion.18.refs_2_, ...), custom_call_target="tpu_custom_call" | custom-call | flops 1000000000 | bytes 5279744 | tf_op jit(solution)/shard_map/grads/pallas_call | solution.py:314
  240.5 5.0 %all-to-all-start.8 = ((f32[32,8,128]{2,1,0:T(8,128)}), f32[32,8,128]{2,1,0:T(8,128)S(1)}, u32[]{:S(2)}, u32[]{:S(2)}) async-start(f32[32,8,128]{2,1,0:T(8,128)} %get-tuple-element.137), calls=%async_computation.8 | async-start | bytes 262144 | tf_op jit(solution)/shard_map/all_to_all | solution.py:1141
  246.3 0.1 pad_maximum_fusion.refs_0_
  246.4 0.8 reshape.138
  247.2 6.0 %all-to-all-done.8.refs_5_ = f32[32,8,128]{2,1,0:T(8,128)S(1)} async-done(((f32[32,8,128]{2,1,0:T(8,128)}), f32[32,8,128]{2,1,0:T(8,128)S(1)}, u32[]{:S(2)}, u32[]{:S(2)}) %all-to-all-start.8) | async-done | bytes 131104 | tf_op jit(solution)/shard_map/all_to_all | solution.py:1141
  253.2 14.8 %adam.1 = (f32[1,1]{1,0:T(1,128)}, f32[1,1]{1,0:T(1,128)}, f32[24,2304]{1,0:T(8,128)}, f32[24,2304]{1,0:T(8,128)}, f32[24,2304]{1,0:T(8,128)}, /*index=5*/f32[24...) custom-call(f32[2]{0:T(128)S(1)} %pad_maximum_fusion.refs_0_, ...), custom_call_target="tpu_custom_call" | custom-call | bytes 38309896 | tf_op jit(solution)/shard_map/adam/pallas_call | solution.py:314
  268.0 1.2 multiply_subtract_fusion
  (59 shorter events, 1.0 us)
Async XLA Ops:
  7.2 92.0 %all-gather.4.cloned.1.call-start = ((), (), s32[]{:S(2)}) async-start(), calls=%async_computation.9 | async-start | bytes 6082560 | tf_op jit(solution)/shard_map/all_gather | solution.py:1043
  15.0 22.0 %all-to-all-start = ((bf16[16,72,128]{2,1,0:T(8,128)(2,1)}), bf16[16,72,128]{2,1,0:T(8,128)(2,1)S(1)}, u32[]{:S(2)}, u32[]{:S(2)}) async-start(bf16[16,72,128]{2,1,0:T(8,128)(2,1)} %get-tuple-element.94), calls=%async_computation | async-start | bytes 589824 | tf_op jit(solution)/shard_map/all_to_all | solution.py:881
  36.9 1.6 collective-permute-start
  48.3 10.6 %collective-permute-start.1 = (bf16[16,48,640]{2,1,0:T(8,128)(2,1)S(1)}, bf16[16,48,640]{2,1,0:T(8,128)(2,1)}, u32[]{:S(2)}, u32[]{:S(2)}) collective-permute-start(bf16[16,48,640]{2,1,0:T(8,128)(2,1)S(1)} %lookup.3), channel_id=1, source_target_pairs={{0,16},{16,0},{1,17},{17,1},{2,18},{18,2},{3,19},{19,3},{4,20},{20... | collective-permute-start | bytes 2949128 | tf_op jit(solution)/shard_map/ppermute | solution.py:877
  61.3 37.8 %all-to-all-start.1 = ((bf16[16,48,640]{2,1,0:T(8,128)(2,1)}), bf16[16,48,640]{2,1,0:T(8,128)(2,1)S(1)}, u32[]{:S(2)}, u32[]{:S(2)}) async-start(bf16[16,48,640]{2,1,0:T(8,128)(2,1)} %add.67), calls=%async_computation.1 | async-start | bytes 1966080 | tf_op jit(solution)/shard_map/all_to_all | solution.py:881
  65.5 40.0 %copy-start.2 = (bf16[32,72,128]{2,1,0:T(8,128)(2,1)}, bf16[32,72,128]{2,1,0:T(8,128)(2,1)S(1)}, u32[]{:S(2)}) copy-start(bf16[32,72,128]{2,1,0:T(8,128)(2,1)S(1)} %constant_dynamic-update-slice_fusion.packet) | copy-start | bytes 1769476
  66.2 46.6 %copy-start.4 = (bf16[96,768]{1,0:T(8,128)(2,1)S(1)}, bf16[96,768]{1,0:T(8,128)(2,1)}, u32[]{:S(2)}) copy-start(bf16[96,768]{1,0:T(8,128)(2,1)} %get-tuple-element.102.refs_3_.refs_8_) | copy-start | bytes 442372
  67.7 31.4 %copy-start.3 = (f32[15,768]{1,0:T(8,128)}, f32[15,768]{1,0:T(8,128)S(1)}, u32[]{:S(2)}) copy-start(f32[15,768]{1,0:T(8,128)S(1)} %reshape.140.refs_2_.refs_10_) | copy-start | bytes 138244
  99.1 56.8 %copy-start = (bf16[16,48,640]{2,1,0:T(8,128)(2,1)}, bf16[16,48,640]{2,1,0:T(8,128)(2,1)S(1)}, u32[]{:S(2)}) copy-start(bf16[16,48,640]{2,1,0:T(8,128)(2,1)S(1)} %all-to-all-done.1) | copy-start | bytes 2949124
  105.6 16.2 %all-to-all-start.2 = ((bf16[16,48,128]{2,1,0:T(8,128)(2,1)}), bf16[16,48,128]{2,1,0:T(8,128)(2,1)S(1)}, u32[]{:S(2)}, u32[]{:S(2)}) async-start(bf16[16,48,128]{2,1,0:T(8,128)(2,1)} %get-tuple-element.100), calls=%async_computation.2 | async-start | bytes 393216 | tf_op jit(solution)/shard_map/all_to_all | solution.py:881
  112.8 1.4 collective-permute-start.3
  114.3 34.5 %copy-start.1 = (bf16[96,768]{1,0:T(8,128)(2,1)}, bf16[96,768]{1,0:T(8,128)(2,1)S(1)}, u32[]{:S(2)}) copy-start(bf16[96,768]{1,0:T(8,128)(2,1)S(1)} %collective-permute-done.3.refs_4_.refs_9_) | copy-start | bytes 442372
  135.7 11.6 %all-to-all-start.4 = ((bf16[16,48,128]{2,1,0:T(8,128)(2,1)}), bf16[16,48,128]{2,1,0:T(8,128)(2,1)S(1)}, u32[]{:S(2)}, u32[]{:S(2)}) async-start(bf16[16,48,128]{2,1,0:T(8,128)(2,1)} %total.1), calls=%async_computation.4 | async-start | bytes 393216 | tf_op jit(solution)/shard_map/all_to_all | solution.py:881
  139.3 63.3 %all-gather.6.cloned.1.call-start = ((), (), s32[]{:S(2)}) async-start(), calls=%async_computation.10 | async-start | bytes 1757184 | tf_op jit(solution)/shard_map/all_gather | solution.py:1088
  139.5 7.9 %collective-permute-start.2 = (bf16[16,48,128]{2,1,0:T(8,128)(2,1)S(1)}, bf16[16,48,128]{2,1,0:T(8,128)(2,1)S(1)}, u32[]{:S(2)}, u32[]{:S(2)}) collective-permute-start(bf16[16,48,128]{2,1,0:T(8,128)(2,1)S(1)} %all-to-all-done.2.refs_1_.refs_2_), channel_id=1, source_target_pairs={{0,16},{16,0},{1,17},{17,1},{2,18},{18,2},{3,19},{19,3},{4,20},{20... | collective-permute-start | bytes 589832 | tf_op jit(solution)/shard_map/ppermute | solution.py:877
  147.3 1.4 collective-permute-start.4
  155.9 15.1 %all-to-all-start.5 = ((bf16[16,72,128]{2,1,0:T(8,128)(2,1)}), bf16[16,72,128]{2,1,0:T(8,128)(2,1)S(1)}, u32[]{:S(2)}, u32[]{:S(2)}) async-start(bf16[16,72,128]{2,1,0:T(8,128)(2,1)} %get-tuple-element.112.refs_7_), calls=%async_computation.5 | async-start | bytes 589824 | tf_op jit(solution)/shard_map/all_to_all | solution.py:881
  162.1 19.6 %copy-start.8 = (bf16[384,192]{1,0:T(8,128)(2,1)S(1)}, bf16[384,192]{1,0:T(8,128)(2,1)}, u32[]{:S(2)}) copy-start(bf16[384,192]{1,0:T(8,128)(2,1)} %get-tuple-element.131) | copy-start | bytes 442372
  178.1 17.4 %all-to-all-start.6 = ((bf16[16,96,128]{2,1,0:T(8,128)(2,1)}), bf16[16,96,128]{2,1,0:T(8,128)(2,1)S(1)}, u32[]{:S(2)}, u32[]{:S(2)}) async-start(bf16[16,96,128]{2,1,0:T(8,128)(2,1)} %get-tuple-element.125.refs_5_), calls=%async_computation.6 | async-start | bytes 786432 | tf_op jit(solution)/shard_map/all_to_all | solution.py:881
  181.7 1.5 collective-permute-start.7
  183.2 48.4 %copy-start.9 = (bf16[96,768]{1,0:T(8,128)(2,1)S(1)}, bf16[96,768]{1,0:T(8,128)(2,1)}, u32[]{:S(2)}) copy-start(bf16[96,768]{1,0:T(8,128)(2,1)} %get-tuple-element.135) | copy-start | bytes 442372
  195.5 32.5 %all-to-all-start.7 = ((bf16[16,240,128]{2,1,0:T(8,128)(2,1)}), bf16[16,240,128]{2,1,0:T(8,128)(2,1)S(1)}, u32[]{:S(2)}, u32[]{:S(2)}) async-start(bf16[16,240,128]{2,1,0:T(8,128)(2,1)} %once.1), calls=%async_computation.7 | async-start | bytes 1966080 | tf_op jit(solution)/shard_map/all_to_all | solution.py:881
  199.4 2.3 collective-permute-start.6
  199.5 2.2 collective-permute-start.5
  228.7 5.3 %collective-permute-start.8 = (bf16[16,240,128]{2,1,0:T(8,128)(2,1)S(1)}, bf16[16,240,128]{2,1,0:T(8,128)(2,1)S(1)}, u32[]{:S(2)}, u32[]{:S(2)}) collective-permute-start(bf16[16,240,128]{2,1,0:T(8,128)(2,1)S(1)} %fusion.18.refs_2_), channel_id=1, source_target_pairs={{0,16},{16,0},{1,17},{17,1},{2,18},{18,2},{3,19},{19,3},{4,20},{20... | collective-permute-start | bytes 2949128 | tf_op jit(solution)/shard_map/ppermute | solution.py:877
  231.6 2.4 collective-permute-start.9
  240.5 12.7 %all-to-all-start.8 = ((f32[32,8,128]{2,1,0:T(8,128)}), f32[32,8,128]{2,1,0:T(8,128)S(1)}, u32[]{:S(2)}, u32[]{:S(2)}) async-start(f32[32,8,128]{2,1,0:T(8,128)} %get-tuple-element.137), calls=%async_computation.8 | async-start | bytes 262144 | tf_op jit(solution)/shard_map/all_to_all | solution.py:1141
  253.2 14.8 %copy-start.5 = (f32[360]{0:T(512)S(1)}, f32[360]{0:T(512)}, u32[]{:S(2)}) copy-start(f32[360]{0:T(512)} %param.57) | copy-start | bytes 4324
  253.2 14.8 %copy-start.6 = (f32[360]{0:T(512)S(1)}, f32[360]{0:T(512)}, u32[]{:S(2)}) copy-start(f32[360]{0:T(512)} %param.58) | copy-start | bytes 4324
  253.2 14.8 %copy-start.7 = (f32[360]{0:T(512)S(1)}, f32[360]{0:T(512)}, u32[]{:S(2)}) copy-start(f32[360]{0:T(512)} %param.59) | copy-start | bytes 4324
Sparse Core Ops, SparseCore 0:
  11.5 86.6 all-gather.3
  147.5 55.0 all-gather.5

commit v4 on v3

--- a/solution.py
+++ b/solution.py
@@ -613,20 +613,24 @@
     )(where, firsts, numbers.reshape(-1, 1, per * count), packets, *early, *late, p_heads)
 
 
-def attend_kernel(rows, mats, xt, vec, moved, sent, early, known, y_out, probs_out, psum_out, normed_out, inv_out, *scratch):
+def attend_kernel(rows, mats, xt, vec, moved, sent, qk_out, facts, y_out, probs_out, psum_out, normed_out, inv_out, *scratch):
     w = square_weights(mats, 0, *scratch, (0, 1, 2, 3))
     x1, x00, q, o, probs, psum, normed, inv, qk, y = attend(xt[...], w, vec[...], moved[...], rows)
     tiles = to_tiles(x1)
-    halves, heads = both_halves(qk, rows), pack_heads(probs.astype(bf16), rows)
-    wide = sent.shape[0]
-    block = D // (2 * wide)
-    for dest in range(wide):
+    for dest in range(sent.shape[0]):
         sent[dest] = tiles.astype(bf16)
-        early[dest] = table_block(halves, dest, block).astype(bf16)
-    facts = jnp.concatenate([to_tiles(value.astype(f32)) for value in (x00, q, o)], 0).astype(bf16)
-    known[...] = jnp.concatenate([heads, facts], 0)
+    qk_out[...] = qk.astype(bf16)
+    facts[...] = jnp.concatenate([to_tiles(value.astype(f32)) for value in (x00, q, o)], 0).astype(bf16)
     y_out[...] = y.astype(bf16)
     probs_out[...], psum_out[...], normed_out[...], inv_out[...] = probs, psum, normed, inv
+
+
+def pack_early_kernel(rows, qk, probs, facts, early, known):
+    halves = both_halves(qk[...], rows)
+    wide = early.shape[0]
+    for dest in range(wide):
+        early[dest] = table_block(halves, dest, D // (2 * wide)).astype(bf16)
+    known[...] = jnp.concatenate([pack_heads(probs[...].astype(bf16), rows), facts[...]], 0)
 
 
 def attend_back_kernel(rows, place, mats, got, d_res2, sums_up, normed, inv, probs, psum, xt, vec, late_out, last, z_out, *scratch):
@@ -1075,21 +1079,25 @@
     xt, vec, bias_up, pick_rows, w_up, packets, numbers, firsts = tie(xt, vec, bias_up, pick_rows, w_up, packets, numbers, firsts)
     tile_lines = ROWS * (D // LANES)
     heads_at, units = head_lines(chunks), 2 * hidden
-    sent, early, known, y, probs, psum, normed1, inv1 = call(
+    sent, qk, facts, y, probs, psum, normed1, inv1 = call(
         partial(attend_kernel, rows),
         [
-            shape((wide, tile_lines, LANES), bf16), shape((wide, block, LANES), bf16), shape((heads_at + 3 * tile_lines, LANES), bf16),
+            shape((wide, tile_lines, LANES), bf16), shape((SIDE, D), bf16), shape((3 * tile_lines, LANES), bf16),
             shape((SIDE, D), bf16), shape((SIDE, tokens)), shape((SIDE, 1)), shape((ROWS, D)), shape((ROWS, 1)),
         ],
         xt, vec, moved,
         far=(mats,), near=(0,), near_outs=(0,), scratch=weight_scratch(4), name="attend", flops=10**9,
     )
     x_own, x_other = pair(sent)
+    early, known = call(
+        partial(pack_early_kernel, rows), [shape((wide, block, LANES), bf16), shape((heads_at + 3 * tile_lines, LANES), bf16)],
+        qk, probs, facts, after=(sent,), name="pack_early", flops=10**8,
+    )
     known_all = lax.all_gather(known, ALL, axis=0, tiled=False)
     down_other = swap(down_low)
     u, h, f_mine = call(
         ffn_kernel, [shape((lines, units)), shape((lines, units), bf16), shape((lines, D), bf16)], x_own, w_up, down_low, down_other, bias_up,
-        scalars=(where,), near=(0, 3), near_outs=(2,), name="ffn", flops=10**8, vmem=16,
+        scalars=(where,), after=(pinned(early),), near=(0, 3), near_outs=(2,), name="ffn", flops=10**8, vmem=16,
     )
     f_parts = exchange(f_mine.reshape(wide, ROWS, D))
     (f_sum,) = call(total_kernel, [shape((wide, tile_lines, LANES), bf16)], f_parts, near=(0,), near_outs=(0,), name="total")

time: 277 us -> 277 us (level)
  Pallas kernels: 105 us -> 108 us
    pallas_call x12 -> x13, Pallas kernels: 61.4 us -> 63.4 us  [call(): pl.pallas_call(run, grid=(1,), out_shape=shapes, in_specs=in_specs, out_s...]
  transfers between devices with their start and end apart: 20 -> 20, of which waited for: 14 -> 13; matrix products, arithmetic and copies ran while one was open for 4% -> 4% of each run, Pallas kernels for 26% -> 27%
where the time goes in v4:
time: 277 us; the launch traced here: 275 us
  Pallas kernels  108 us (39%)
  waiting for transfers between devices  84.9 us (31%)
  starting transfers between devices  42.9 us (15%)
  between operations  15.9 us (6%)
  blocking collectives  11.2 us (4%)
  local copies, waits for them, and re-layouts  6.87 us (2%)
  other arithmetic  5.85 us (2%)
    all_to_all x7, waiting for transfers between devices, exchange(): return lax.all_to_all(x, 'wide', split_axis=0, concat_axis=0, tiled=True)  69.6 us
    pallas_call x13, Pallas kernels, call(): pl.pallas_call(run, grid=(1,), out_shape=shapes, in_specs=in_specs, out_s...  63.4 us
    all_to_all x7, starting transfers between devices, exchange(): return lax.all_to_all(x, 'wide', split_axis=0, concat_axis=0, tiled=True)  34.2 us
    pallas_call x1, Pallas kernels, spread_tokens(): pl.pallas_call(partial(spread_kernel, rows, half_rows, feats, per, unroll...  26 us
    pallas_call x2, Pallas kernels, lookup(): pl.pallas_call(partial(lookup_kernel, half_rows, per, unroll), out_shape=...  18.4 us
    all_to_all x1, blocking collectives, exchange(): return lax.all_to_all(x, 'wide', split_axis=0, concat_axis=0, tiled=True)  11.2 us
    ppermute x10, waiting for transfers between devices, swap(): return lax.ppermute(x, 'group', [(0, 1), (1, 0)])  8.42 us
    all_to_all x1, waiting for transfers between devices, body(): lax.all_to_all(squares, ALL, split_axis=0, concat_axis=0, tiled=True)  5.96 us
  transfers between devices with their start and end apart: 20, of which 13 were waited for; matrix products, arithmetic and copies ran while one was open for 4% of the time, Pallas kernels for 27%

profile of v4, /device:TPU:0, one launch (start us, length us, event | category | flops | bytes accessed | tf_op | source)
XLA Modules:
  0.0 275.5 jit_solution(4016533700571504047)
XLA Ops:
  7.2 1.9 cast.1
  9.8 1.2 broadcast_in_dim.25.refs_4_
  11.0 1.3 concatenate.22
  12.3 2.7 prepare.1
  15.0 8.3 %all-to-all-start = ((bf16[16,72,128]{2,1,0:T(8,128)(2,1)}), bf16[16,72,128]{2,1,0:T(8,128)(2,1)S(1)}, u32[]{:S(2)}, u32[]{:S(2)}) async-start(bf16[16,72,128]{2,1,0:T(8,128)(2,1)} %get-tuple-element.96), calls=%async_computation | async-start | bytes 589824 | tf_op jit(solution)/shard_map/all_to_all | solution.py:885
  23.3 7.0 %build.1.table = f32[12672,128]{1,0:T(8,128)} custom-call(f32[48,25216]{1,0:T(8,128)} %refs_1_.5), custom_call_target="tpu_custom_call" | custom-call | flops 100000000 | bytes 11329536 | tf_op jit(solution)/shard_map/build/pallas_call | solution.py:314
  30.3 6.7 %all-to-all-done.packet = bf16[16,72,128]{2,1,0:T(8,128)(2,1)S(1)} async-done(((bf16[16,72,128]{2,1,0:T(8,128)(2,1)}), bf16[16,72,128]{2,1,0:T(8,128)(2,1)S(1)}, u32[]{:S(2)}, u32[]{:S(2)}) %all-to-all-start) | async-done | bytes 294944 | tf_op jit(solution)/shard_map/all_to_all | solution.py:885
  36.9 0.1 pad_add_fusion.2.where.refs_0_
  37.0 1.5 collective-permute-done.packet
  38.6 0.5 convert_reduce_fusion.firsts
  39.1 9.3 %lookup.3 = bf16[16,48,640]{2,1,0:T(8,128)(2,1)S(1)} custom-call(s32[2]{0:T(128)S(1)} %pad_add_fusion.2.where.refs_0_, s32[16]{0:T(128)S(1)} %convert_reduce_fusion.firsts, s32[4,1,2560]{2,1,0:T(1,128)S(1)} %reshape_reshape.9.numbers, bf16[16,72,128]{2,1,0:T(8,128)(2,1)S(1)} %collective-permute-done.packet, f32[12672,128]{1,0:T(8,128)} %build.1.table), custom_call_target="tpu_custom_call" | custom-call | flops 1000000000 | bytes 10000000 | tf_op jit(solution)/shard_map/lookup/pallas_call | solution.py:478
  48.4 0.8 collective-permute-start.1
  49.3 0.5 convert_reduce_fusion.1.firsts
  49.7 9.1 %lookup.2 = bf16[16,48,640]{2,1,0:T(8,128)(2,1)S(1)} custom-call(s32[2]{0:T(128)S(1)} %pad_add_fusion.2.where.refs_0_, s32[16]{0:T(128)S(1)} %convert_reduce_fusion.1.firsts, s32[4,1,2560]{2,1,0:T(1,128)S(1)} %reshape_reshape.8.numbers, bf16[16,72,128]{2,1,0:T(8,128)(2,1)S(1)} %all-to-all-done.packet, f32[12672,128]{1,0:T(8,128)} %build.1.table), custom_call_target="tpu_custom_call" | custom-call | flops 1000000000 | bytes 10000000 | tf_op jit(solution)/shard_map/lookup/pallas_call | solution.py:478
  58.9 2.4 add.67
  61.3 4.1 %all-to-all-start.1 = ((bf16[16,48,640]{2,1,0:T(8,128)(2,1)}), bf16[16,48,640]{2,1,0:T(8,128)(2,1)S(1)}, u32[]{:S(2)}, u32[]{:S(2)}) async-start(bf16[16,48,640]{2,1,0:T(8,128)(2,1)} %add.67), calls=%async_computation.1 | async-start | bytes 1966080 | tf_op jit(solution)/shard_map/all_to_all | solution.py:885
  65.5 0.1 maximum_select_fusion
  65.8 0.1 copy.75
  65.9 0.1 copy.77
  66.0 0.1 copy.76
  66.2 0.1 copy.84
  66.3 0.3 copy.88
  66.6 1.0 reshape.133.refs_2_.refs_7_
  67.6 0.1 reshape.140.refs_2_.refs_10_
  67.7 0.1 reshape.128
  67.8 0.6 reshape.129.refs_5_
  68.5 0.1 pad_add_fusion.3.firsts
  68.6 0.7 pad_bitcast_fusion.refs_11_
  69.3 29.9 %all-to-all-done.1 = bf16[16,48,640]{2,1,0:T(8,128)(2,1)S(1)} async-done(((bf16[16,48,640]{2,1,0:T(8,128)(2,1)}), bf16[16,48,640]{2,1,0:T(8,128)(2,1)S(1)}, u32[]{:S(2)}, u32[]{:S(2)}) %all-to-all-start.1) | async-done | bytes 983072 | tf_op jit(solution)/shard_map/all_to_all | solution.py:885
  99.1 6.3 %attend.1 = (bf16[16,48,128]{2,1,0:T(8,128)(2,1)}, bf16[64,768]{1,0:T(8,128)(2,1)}, bf16[144,128]{1,0:T(8,128)(2,1)}, bf16[64,768]{1,0:T(8,128)(2,1)}, f32[64,64...) custom-call(bf16[768,3840]{1,0:T(8,128)(2,1)} %all-gather.4.cloned.1.call-done.refs_0_.refs_1_, ...), custom_call_target="tpu_custom_call" | custom-call | flops 1000000000 | bytes 7566624 | tf_op jit(solution)/shard_map/attend/pallas_call | solution.py:314
  105.5 7.2 %all-to-all-start.2 = ((bf16[16,48,128]{2,1,0:T(8,128)(2,1)}), bf16[16,48,128]{2,1,0:T(8,128)(2,1)S(1)}, u32[]{:S(2)}, u32[]{:S(2)}) async-start(bf16[16,48,128]{2,1,0:T(8,128)(2,1)} %get-tuple-element.102.refs_3_), calls=%async_computation.2 | async-start | bytes 393216 | tf_op jit(solution)/shard_map/all_to_all | solution.py:885
  112.8 2.0 pack_early.1
  114.9 6.8 %all-to-all-done.2.refs_1_.refs_2_ = bf16[16,48,128]{2,1,0:T(8,128)(2,1)S(1)} async-done(((bf16[16,48,128]{2,1,0:T(8,128)(2,1)}), bf16[16,48,128]{2,1,0:T(8,128)(2,1)S(1)}, u32[]{:S(2)}, u32[]{:S(2)}) %all-to-all-start.2) | async-done | bytes 196640 | tf_op jit(solution)/shard_map/all_to_all | solution.py:885
  121.6 2.0 ffn.1
  123.7 11.2 %all_to_all.45.refs_0_ = bf16[16,8,768]{2,1,0:T(8,128)(2,1)S(1)} all-to-all(bf16[16,8,768]{2,1,0:T(8,128)(2,1)S(1)} %bitcast.39), channel_id=1, replica_groups=mesh['group'=2,'wide'=16] {'wide'}, dimensions={0} | all-to-all | bytes 393216 | tf_op jit(solution)/shard_map/all_to_all | solution.py:885
  134.9 0.7 total.1
  135.6 3.5 %all-to-all-start.4 = ((bf16[16,48,128]{2,1,0:T(8,128)(2,1)}), bf16[16,48,128]{2,1,0:T(8,128)(2,1)S(1)}, u32[]{:S(2)}, u32[]{:S(2)}) async-start(bf16[16,48,128]{2,1,0:T(8,128)(2,1)} %total.1), calls=%async_computation.4 | async-start | bytes 393216 | tf_op jit(solution)/shard_map/all_to_all | solution.py:885
  139.2 0.2 all-gather.6.cloned.1.call-start
  139.5 7.8 %all-to-all-done.4.refs_4_ = bf16[16,48,128]{2,1,0:T(8,128)(2,1)S(1)} async-done(((bf16[16,48,128]{2,1,0:T(8,128)(2,1)}), bf16[16,48,128]{2,1,0:T(8,128)(2,1)S(1)}, u32[]{:S(2)}, u32[]{:S(2)}) %all-to-all-start.4) | async-done | bytes 196640 | tf_op jit(solution)/shard_map/all_to_all | solution.py:885
  147.3 1.4 collective-permute-done.4.refs_5_
  148.7 7.2 %middle.1 = (f32[1,1]{1,0:T(1,128)}, bf16[256,768]{1,0:T(8,128)(2,1)}, bf16[256,768]{1,0:T(8,128)(2,1)}, f32[256,768]{1,0:T(8,128)}, bf16[128,768]{1,0:T(8,128)(...) custom-call(s32[2]{0:T(128)S(1)} %pad_add_fusion.2.where.refs_0_, ...), custom_call_target="tpu_custom_call" | custom-call | flops 1000000000 | bytes 9667588 | tf_op jit(solution)/shard_map/middle/pallas_call | solution.py:314
  155.8 3.5 %all-to-all-start.5 = ((bf16[16,72,128]{2,1,0:T(8,128)(2,1)}), bf16[16,72,128]{2,1,0:T(8,128)(2,1)S(1)}, u32[]{:S(2)}, u32[]{:S(2)}) async-start(bf16[16,72,128]{2,1,0:T(8,128)(2,1)} %get-tuple-element.117.refs_7_), calls=%async_computation.5 | async-start | bytes 589824 | tf_op jit(solution)/shard_map/all_to_all | solution.py:885
  159.4 2.6 ffn_grads.1
  162.0 8.9 %all-to-all-done.5.refs_2_.early_own = bf16[16,72,128]{2,1,0:T(8,128)(2,1)S(1)} async-done(((bf16[16,72,128]{2,1,0:T(8,128)(2,1)}), bf16[16,72,128]{2,1,0:T(8,128)(2,1)S(1)}, u32[]{:S(2)}, u32[]{:S(2)}) %all-to-all-start.5) | async-done | bytes 294944 | tf_op jit(solution)/shard_map/all_to_all | solution.py:885
  170.9 7.1 %attend_back.1 = (bf16[16,96,128]{2,1,0:T(8,128)(2,1)}, bf16[144,128]{1,0:T(8,128)(2,1)}, bf16[64,768]{1,0:T(8,128)(2,1)}) custom-call(s32[1]{0:T(128)} %bitcast.13.refs_0_, bf16[768,3840]{1,0:T(8,128)(2,1)} %all-gather.4.cloned.1.call-done.refs_0_.refs_1_, bf16[16,72,128]{2,1,0:T(8,128)(2,1)S(1)} %all-to-all-done.5.refs_2_.early_own, ...), custom_call_target="tpu_custom_call" | custom-call | flops 1000000000 | bytes 8728864 | tf_op jit(solution)/shard_map/attend_back/pallas_call | solution.py:314
  178.0 3.6 %all-to-all-start.6 = ((bf16[16,96,128]{2,1,0:T(8,128)(2,1)}), bf16[16,96,128]{2,1,0:T(8,128)(2,1)S(1)}, u32[]{:S(2)}, u32[]{:S(2)}) async-start(bf16[16,96,128]{2,1,0:T(8,128)(2,1)} %get-tuple-element.129.refs_5_), calls=%async_computation.6 | async-start | bytes 786432 | tf_op jit(solution)/shard_map/all_to_all | solution.py:885
  181.7 1.4 collective-permute-done.7.refs_4_
  183.1 2.6 pack.1.refs_0_
  185.7 9.7 %all-to-all-done.6.late_own.refs_1_ = bf16[16,96,128]{2,1,0:T(8,128)(2,1)S(1)} async-done(((bf16[16,96,128]{2,1,0:T(8,128)(2,1)}), bf16[16,96,128]{2,1,0:T(8,128)(2,1)S(1)}, u32[]{:S(2)}, u32[]{:S(2)}) %all-to-all-start.6) | async-done | bytes 393248 | tf_op jit(solution)/shard_map/all_to_all | solution.py:885
  195.4 3.9 %all-to-all-start.7 = ((bf16[16,240,128]{2,1,0:T(8,128)(2,1)}), bf16[16,240,128]{2,1,0:T(8,128)(2,1)S(1)}, u32[]{:S(2)}, u32[]{:S(2)}) async-start(bf16[16,240,128]{2,1,0:T(8,128)(2,1)} %once.1), calls=%async_computation.7 | async-start | bytes 1966080 | tf_op jit(solution)/shard_map/all_to_all | solution.py:885
  199.4 0.5 collective-permute-start.5
  199.9 1.7 collective-permute-done.5.early_other
  201.6 0.9 all-gather.6.cloned.1.call-done
  202.5 26.0 %spread_tokens.1 = (bf16[48,25216]{1,0:T(8,128)(2,1)}, f32[8,128]{1,0:T(8,128)}) custom-call(s32[2]{0:T(128)S(1)} %pad_add_fusion.2.where.refs_0_, s32[32]{0:T(128)S(1)} %pad_add_fusion.3.firsts, s32[4,1,5120]{2,1,0:T(1,128)S(1)} %bitcast.38, bf16[32,72,128]{2,1,0:T(8,128)(2,1)} %copy-done.2, bf16[16,72,128]{2,1,0:T(8,128)(2,1)S(1)} %all-to-all-done.5.refs_2_.early_own, ...), custom_call_target="tpu_custom_call" | custom-call | flops 1000000000 | bytes 30000000 | tf_op jit(solution)/shard_map/spread_tokens/pallas_call | solution.py:600
  228.5 0.7 fusion.18.refs_2_
  229.2 1.7 collective-permute-start.8
  230.9 2.3 collective-permute-done.9.refs_6_
  233.3 6.5 %grads.1 = (f32[24,2304]{1,0:T(8,128)}, f32[24,768]{1,0:T(8,128)}, f32[24,3072]{1,0:T(8,128)}, f32[96,768]{1,0:T(8,128)}, f32[16,768]{1,0:T(8,128)}, /*index=5*/f32[32,8,128]{2,1,0:T(8,128)}) custom-call(s32[2]{0:T(128)S(1)} %pad_add_fusion.2.where.refs_0_, bf16[32,208,128]{2,1,0:T(8,128)(2,1)} %bitcast.41, bf16[16,240,128]{2,1,0:T(8,128)(2,1)S(1)} %fusion.18.refs_2_, ...), custom_call_target="tpu_custom_call" | custom-call | flops 1000000000 | bytes 5279744 | tf_op jit(solution)/shard_map/grads/pallas_call | solution.py:314
  239.8 5.0 %all-to-all-start.8 = ((f32[32,8,128]{2,1,0:T(8,128)}), f32[32,8,128]{2,1,0:T(8,128)S(1)}, u32[]{:S(2)}, u32[]{:S(2)}) async-start(f32[32,8,128]{2,1,0:T(8,128)} %get-tuple-element.141), calls=%async_computation.8 | async-start | bytes 262144 | tf_op jit(solution)/shard_map/all_to_all | solution.py:1149
  245.7 0.1 pad_maximum_fusion.refs_0_
  245.7 0.8 reshape.138
  246.5 6.0 %all-to-all-done.8.refs_5_ = f32[32,8,128]{2,1,0:T(8,128)S(1)} async-done(((f32[32,8,128]{2,1,0:T(8,128)}), f32[32,8,128]{2,1,0:T(8,128)S(1)}, u32[]{:S(2)}, u32[]{:S(2)}) %all-to-all-start.8) | async-done | bytes 131104 | tf_op jit(solution)/shard_map/all_to_all | solution.py:1149
  252.5 14.8 %adam.1 = (f32[1,1]{1,0:T(1,128)}, f32[1,1]{1,0:T(1,128)}, f32[24,2304]{1,0:T(8,128)}, f32[24,2304]{1,0:T(8,128)}, f32[24,2304]{1,0:T(8,128)}, /*index=5*/f32[24...) custom-call(f32[2]{0:T(128)S(1)} %pad_maximum_fusion.refs_0_, ...), custom_call_target="tpu_custom_call" | custom-call | bytes 38309896 | tf_op jit(solution)/shard_map/adam/pallas_call | solution.py:314
  267.3 1.3 multiply_subtract_fusion
  (60 shorter events, 1.0 us)
Async XLA Ops:
  7.2 91.9 %all-gather.4.cloned.1.call-start = ((), (), s32[]{:S(2)}) async-start(), calls=%async_computation.9 | async-start | bytes 6082560 | tf_op jit(solution)/shard_map/all_gather | solution.py:1047
  15.0 22.0 %all-to-all-start = ((bf16[16,72,128]{2,1,0:T(8,128)(2,1)}), bf16[16,72,128]{2,1,0:T(8,128)(2,1)S(1)}, u32[]{:S(2)}, u32[]{:S(2)}) async-start(bf16[16,72,128]{2,1,0:T(8,128)(2,1)} %get-tuple-element.96), calls=%async_computation | async-start | bytes 589824 | tf_op jit(solution)/shard_map/all_to_all | solution.py:885
  36.9 1.6 collective-permute-start
  48.4 10.5 %collective-permute-start.1 = (bf16[16,48,640]{2,1,0:T(8,128)(2,1)S(1)}, bf16[16,48,640]{2,1,0:T(8,128)(2,1)}, u32[]{:S(2)}, u32[]{:S(2)}) collective-permute-start(bf16[16,48,640]{2,1,0:T(8,128)(2,1)S(1)} %lookup.3), channel_id=1, source_target_pairs={{0,16},{16,0},{1,17},{17,1},{2,18},{18,2},{3,19},{19,3},{4,20},{20... | collective-permute-start | bytes 2949128 | tf_op jit(solution)/shard_map/ppermute | solution.py:881
  61.3 37.8 %all-to-all-start.1 = ((bf16[16,48,640]{2,1,0:T(8,128)(2,1)}), bf16[16,48,640]{2,1,0:T(8,128)(2,1)S(1)}, u32[]{:S(2)}, u32[]{:S(2)}) async-start(bf16[16,48,640]{2,1,0:T(8,128)(2,1)} %add.67), calls=%async_computation.1 | async-start | bytes 1966080 | tf_op jit(solution)/shard_map/all_to_all | solution.py:885
  65.5 40.0 %copy-start.2 = (bf16[32,72,128]{2,1,0:T(8,128)(2,1)}, bf16[32,72,128]{2,1,0:T(8,128)(2,1)S(1)}, u32[]{:S(2)}) copy-start(bf16[32,72,128]{2,1,0:T(8,128)(2,1)S(1)} %constant_dynamic-update-slice_fusion.packet) | copy-start | bytes 1769476
  66.2 46.6 %copy-start.4 = (bf16[96,768]{1,0:T(8,128)(2,1)S(1)}, bf16[96,768]{1,0:T(8,128)(2,1)}, u32[]{:S(2)}) copy-start(bf16[96,768]{1,0:T(8,128)(2,1)} %get-tuple-element.104.refs_3_.refs_8_) | copy-start | bytes 442372
  67.7 31.4 %copy-start.3 = (f32[15,768]{1,0:T(8,128)}, f32[15,768]{1,0:T(8,128)S(1)}, u32[]{:S(2)}) copy-start(f32[15,768]{1,0:T(8,128)S(1)} %reshape.140.refs_2_.refs_10_) | copy-start | bytes 138244
  99.1 36.5 %copy-start = (bf16[16,48,640]{2,1,0:T(8,128)(2,1)}, bf16[16,48,640]{2,1,0:T(8,128)(2,1)S(1)}, u32[]{:S(2)}) copy-start(bf16[16,48,640]{2,1,0:T(8,128)(2,1)S(1)} %all-to-all-done.1) | copy-start | bytes 2949124
  105.5 16.2 %all-to-all-start.2 = ((bf16[16,48,128]{2,1,0:T(8,128)(2,1)}), bf16[16,48,128]{2,1,0:T(8,128)(2,1)S(1)}, u32[]{:S(2)}, u32[]{:S(2)}) async-start(bf16[16,48,128]{2,1,0:T(8,128)(2,1)} %get-tuple-element.102.refs_3_), calls=%async_computation.2 | async-start | bytes 393216 | tf_op jit(solution)/shard_map/all_to_all | solution.py:885
  112.7 2.1 collective-permute-start.3
  114.9 33.8 %copy-start.1 = (bf16[96,768]{1,0:T(8,128)(2,1)}, bf16[96,768]{1,0:T(8,128)(2,1)S(1)}, u32[]{:S(2)}) copy-start(bf16[96,768]{1,0:T(8,128)(2,1)S(1)} %collective-permute-done.3.refs_4_.refs_9_) | copy-start | bytes 442372
  135.6 11.6 %all-to-all-start.4 = ((bf16[16,48,128]{2,1,0:T(8,128)(2,1)}), bf16[16,48,128]{2,1,0:T(8,128)(2,1)S(1)}, u32[]{:S(2)}, u32[]{:S(2)}) async-start(bf16[16,48,128]{2,1,0:T(8,128)(2,1)} %total.1), calls=%async_computation.4 | async-start | bytes 393216 | tf_op jit(solution)/shard_map/all_to_all | solution.py:885
  139.2 63.3 %all-gather.6.cloned.1.call-start = ((), (), s32[]{:S(2)}) async-start(), calls=%async_computation.10 | async-start | bytes 1757184 | tf_op jit(solution)/shard_map/all_gather | solution.py:1096
  139.4 7.9 %collective-permute-start.2 = (bf16[16,48,128]{2,1,0:T(8,128)(2,1)S(1)}, bf16[16,48,128]{2,1,0:T(8,128)(2,1)S(1)}, u32[]{:S(2)}, u32[]{:S(2)}) collective-permute-start(bf16[16,48,128]{2,1,0:T(8,128)(2,1)S(1)} %all-to-all-done.2.refs_1_.refs_2_), channel_id=1, source_target_pairs={{0,16},{16,0},{1,17},{17,1},{2,18},{18,2},{3,19},{19,3},{4,20},{20... | collective-permute-start | bytes 589832 | tf_op jit(solution)/shard_map/ppermute | solution.py:881
  147.2 1.4 collective-permute-start.4
  155.8 15.1 %all-to-all-start.5 = ((bf16[16,72,128]{2,1,0:T(8,128)(2,1)}), bf16[16,72,128]{2,1,0:T(8,128)(2,1)S(1)}, u32[]{:S(2)}, u32[]{:S(2)}) async-start(bf16[16,72,128]{2,1,0:T(8,128)(2,1)} %get-tuple-element.117.refs_7_), calls=%async_computation.5 | async-start | bytes 589824 | tf_op jit(solution)/shard_map/all_to_all | solution.py:885
  162.0 19.6 %copy-start.8 = (bf16[384,192]{1,0:T(8,128)(2,1)S(1)}, bf16[384,192]{1,0:T(8,128)(2,1)}, u32[]{:S(2)}) copy-start(bf16[384,192]{1,0:T(8,128)(2,1)} %get-tuple-element.135) | copy-start | bytes 442372
  178.0 17.3 %all-to-all-start.6 = ((bf16[16,96,128]{2,1,0:T(8,128)(2,1)}), bf16[16,96,128]{2,1,0:T(8,128)(2,1)S(1)}, u32[]{:S(2)}, u32[]{:S(2)}) async-start(bf16[16,96,128]{2,1,0:T(8,128)(2,1)} %get-tuple-element.129.refs_5_), calls=%async_computation.6 | async-start | bytes 786432 | tf_op jit(solution)/shard_map/all_to_all | solution.py:885
  181.6 1.5 collective-permute-start.7
  183.1 47.7 %copy-start.9 = (bf16[96,768]{1,0:T(8,128)(2,1)S(1)}, bf16[96,768]{1,0:T(8,128)(2,1)}, u32[]{:S(2)}) copy-start(bf16[96,768]{1,0:T(8,128)(2,1)} %get-tuple-element.139) | copy-start | bytes 442372
  195.4 33.1 %all-to-all-start.7 = ((bf16[16,240,128]{2,1,0:T(8,128)(2,1)}), bf16[16,240,128]{2,1,0:T(8,128)(2,1)S(1)}, u32[]{:S(2)}, u32[]{:S(2)}) async-start(bf16[16,240,128]{2,1,0:T(8,128)(2,1)} %once.1), calls=%async_computation.7 | async-start | bytes 1966080 | tf_op jit(solution)/shard_map/all_to_all | solution.py:885
  199.3 2.3 collective-permute-start.6
  199.4 2.2 collective-permute-start.5
  229.2 4.1 %collective-permute-start.8 = (bf16[16,240,128]{2,1,0:T(8,128)(2,1)S(1)}, bf16[16,240,128]{2,1,0:T(8,128)(2,1)S(1)}, u32[]{:S(2)}, u32[]{:S(2)}) collective-permute-start(bf16[16,240,128]{2,1,0:T(8,128)(2,1)S(1)} %fusion.18.refs_2_), channel_id=1, source_target_pairs={{0,16},{16,0},{1,17},{17,1},{2,18},{18,2},{3,19},{19,3},{4,20},{20... | collective-permute-start | bytes 2949128 | tf_op jit(solution)/shard_map/ppermute | solution.py:881
  230.9 2.4 collective-permute-start.9
  239.8 12.7 %all-to-all-start.8 = ((f32[32,8,128]{2,1,0:T(8,128)}), f32[32,8,128]{2,1,0:T(8,128)S(1)}, u32[]{:S(2)}, u32[]{:S(2)}) async-start(f32[32,8,128]{2,1,0:T(8,128)} %get-tuple-element.141), calls=%async_computation.8 | async-start | bytes 262144 | tf_op jit(solution)/shard_map/all_to_all | solution.py:1149
  252.5 14.8 %copy-start.5 = (f32[360]{0:T(512)S(1)}, f32[360]{0:T(512)}, u32[]{:S(2)}) copy-start(f32[360]{0:T(512)} %param.57) | copy-start | bytes 4324
  252.5 14.8 %copy-start.6 = (f32[360]{0:T(512)S(1)}, f32[360]{0:T(512)}, u32[]{:S(2)}) copy-start(f32[360]{0:T(512)} %param.58) | copy-start | bytes 4324
  252.5 14.8 %copy-start.7 = (f32[360]{0:T(512)S(1)}, f32[360]{0:T(512)}, u32[]{:S(2)}) copy-start(f32[360]{0:T(512)} %param.59) | copy-start | bytes 4324
Sparse Core Ops, SparseCore 0:
  11.5 86.6 all-gather.3
  147.4 55.0 all-gather.5
